TPU v7x, 32 devices: a whole 2x2x4 slice. The times are simulated.
32 devices in a mesh: groups: 2 (over y), ctx: 16 (over z, x, core).
Axes of the slice: x: 2, y: 2, z: 4, core: 2. Of those that a mesh axis runs over, the one named last changes fastest.
Arguments:
- outer_gate: bfloat16 [32768, 256], P(('groups', 'ctx')), parts along dimension 0, may hold values from -6 to 6
- inner_gate: bfloat16 [32768, 256], P(('groups', 'ctx')), parts along dimension 0, may hold values from -6 to 6
- values: bfloat16 [32768, 256], P(('groups', 'ctx')), parts along dimension 0, may hold values from -6 to 6
- cotangent: bfloat16 [32768, 256], P(('groups', 'ctx')), parts along dimension 0, may hold values from -6 to 6
- residue: float32 [256, 16], replicated, may hold values from -0.5 to 0.5
- decay_rate: float32 [256, 16], replicated, may hold values from 1.8310547e-05 to 0.1
- skip_gain: float32 [256], replicated, may hold values from -4 to 4
Outputs:
- layer_out: bfloat16 [32768, 256], P(('groups', 'ctx')), parts along dimension 0
- grad_outer: bfloat16 [32768, 256], P(('groups', 'ctx')), parts along dimension 0
- grad_inner: bfloat16 [32768, 256], P(('groups', 'ctx')), parts along dimension 0
- grad_values: bfloat16 [32768, 256], P(('groups', 'ctx')), parts along dimension 0
There are 2 independent parts, one for each index of `groups`. A program takes and returns all parts, laid end to end along the dimension named above; an argument that names none is the same for every part. Nothing has to cross between parts.
All inputs are finite; a program needn't handle non-finite values.
Results may differ from a plain program's by a relative error of at most 0.005.
Values sent between devices are 32-bit elements; how exact they have to be, the bound alone decides.
No kernel may reach another device: no remote copies, remote signals or barrier semaphores. Data moves between devices by JAX's collectives and lax.ppermute only.
A program may use at most 128 MiB of HBM per device.

v0:
```python
import jax
import jax.numpy as jnp
from jax import lax
from jax.sharding import PartitionSpec as P


def product(pattern, first, second):
    return jnp.einsum(pattern, first, second, precision=lax.Precision.HIGH)


def shards(outer_gate, inner_gate, values, cotangent, residue, decay_rate, skip_gain):
    row_count, channels = values.shape
    block_width = min(64, row_count)
    block_count = row_count // block_width
    position = lax.axis_index("ctx")
    rate_table = decay_rate.T
    pole_weight = residue.T
    mixed_input = (inner_gate.astype(jnp.float32) * values.astype(jnp.float32)).astype(jnp.bfloat16)
    mixed_float = lax.optimization_barrier(mixed_input).astype(jnp.float32)
    offsets = jnp.arange(block_width, dtype=jnp.float32)
    enter_table = jnp.exp(-rate_table[None] * (offsets + 1.0)[:, None, None])
    leave_table = jnp.exp(-rate_table[None] * (block_width - 1.0 - offsets)[:, None, None])
    sections = jnp.arange(block_count, dtype=jnp.float32)
    powers = jnp.exp(-rate_table[None] * (block_width * sections)[:, None, None])
    reverse_powers = powers[::-1]
    later_index = jnp.arange(block_count)[:, None]
    earlier_index = jnp.arange(block_count)[None, :]
    spacing = jnp.maximum(later_index - earlier_index - 1, 0).astype(jnp.float32)
    decayed = jnp.exp(-rate_table[None, None] * (block_width * spacing)[:, :, None, None])
    carry_table = jnp.where((earlier_index < later_index)[:, :, None, None], decayed, 0.0)
    tap_values = jnp.sum(
        pole_weight[None] * jnp.exp(-rate_table[None] * offsets[:, None, None]), axis=1
    )
    differ = jnp.arange(block_width)[:, None] - jnp.arange(block_width)[None, :]
    lag_onehot = (differ[:, :, None] == jnp.arange(block_width)[None, None, :]).astype(jnp.float32)
    kernel = jnp.einsum("tsl,lc->tsc", lag_onehot, tap_values, precision=lax.Precision.HIGHEST)
    pieces = mixed_float.reshape(block_count, block_width, channels)
    span_states = product("nsc,skc->nkc", pieces, leave_table)
    own_state = jnp.sum(span_states * reverse_powers, axis=0)
    within = product("nsc,tsc->ntc", pieces, kernel)
    carried = product("mjkc,jkc->mkc", carry_table, span_states)
    across = product("mkc,tkc->mtc", carried * pole_weight[None], enter_table)
    piece = lax.all_gather(own_state[None], "ctx", axis=0, tiled=True)
    anchor = jnp.arange(piece.shape[0])
    distance = position - anchor - 1
    scaled = jnp.exp(
        -rate_table[None]
        * (row_count * jnp.maximum(distance, 0)).astype(jnp.float32)[:, None, None]
    )
    weight_rows = jnp.where((distance >= 0)[:, None, None], scaled, 0.0)
    gathered = jnp.sum(weight_rows * piece, axis=0)
    remote = product("mkc,tkc->mtc", powers * (pole_weight * gathered)[None], enter_table)
    response = skip_gain[None, :] * mixed_float + (within + across + remote).reshape(
        row_count, channels
    )
    layer_out = (outer_gate.astype(jnp.float32) * response).astype(jnp.bfloat16)
    grad_outer = (cotangent.astype(jnp.float32) * response).astype(jnp.bfloat16)
    grad_response = outer_gate.astype(jnp.float32) * cotangent.astype(jnp.float32)
    grad_pieces = grad_response.reshape(block_count, block_width, channels)
    span_adjoint = product("ntc,tkc->nkc", grad_pieces, enter_table)
    own_adjoint = jnp.sum(span_adjoint * powers, axis=0)
    within_back = product("ntc,tsc->nsc", grad_pieces, kernel)
    carried_back = product("mjkc,mkc->jkc", carry_table, span_adjoint)
    across_back = product("jkc,skc->jsc", carried_back * pole_weight[None], leave_table)
    piece = lax.all_gather(own_adjoint[None], "ctx", axis=0, tiled=True)
    anchor = jnp.arange(piece.shape[0])
    distance = anchor - position - 1
    scaled = jnp.exp(
        -rate_table[None]
        * (row_count * jnp.maximum(distance, 0)).astype(jnp.float32)[:, None, None]
    )
    weight_rows = jnp.where((distance >= 0)[:, None, None], scaled, 0.0)
    suffix = jnp.sum(weight_rows * piece, axis=0)
    decoded = product("nkc,skc->nsc", reverse_powers * (pole_weight * suffix)[None], leave_table)
    grad_mixed = skip_gain[None, :] * grad_response + (within_back + across_back + decoded).reshape(
        row_count, channels
    )
    grad_inner = (grad_mixed * values.astype(jnp.float32)).astype(jnp.bfloat16)
    grad_values = (grad_mixed * inner_gate.astype(jnp.float32)).astype(jnp.bfloat16)
    return (layer_out, grad_outer, grad_inner, grad_values)


def solution(mesh):
    return jax.shard_map(
        shards,
        mesh=mesh,
        in_specs=(
            P(("groups", "ctx"), None),
            P(("groups", "ctx"), None),
            P(("groups", "ctx"), None),
            P(("groups", "ctx"), None),
            P(),
            P(),
            P(),
        ),
        out_specs=(
            P(("groups", "ctx"), None),
            P(("groups", "ctx"), None),
            P(("groups", "ctx"), None),
            P(("groups", "ctx"), None),
        ),
        check_vma=False,
    )
```

profile of v0, /device:TPU:0, one launch (start us, length us, event | category | flops | bytes accessed | tf_op | source)
XLA Modules:
  0.0 141.4 jit_solution(13211322422101003060)
XLA Ops:
  3.6 0.7 negate_bitcast_fusion
  5.0 0.8 copy.57
  5.9 2.3 %multiply_reduce_fusion.4 = f32[64,256]{0,1:T(8,128)} fusion(f32[16,256]{0,1:T(8,128)S(1)} %copy.58, f32[16,256]{0,1:T(8,128)S(1)} %bitcast.60), kind=kLoop, calls=%fused_computation.26 | loop fusion | flops 770048 | bytes 98304 | tf_op jit(solution)/shard_map/reduce_sum | solution.py:31
  8.1 1.3 fusion.17
  9.5 1.0 copy.61
  10.5 1.1 convert_multiply_fusion
  11.6 2.5 %copy.68 = f32[16,64,256]{1,0,2:T(8,128)S(1)} copy(f32[16,64,256]{2,1,0:T(8,128)} %bitcast.59) | data formatting | bytes 2097152 | tf_op jit(solution)/shard_map/reshape | solution.py:59
  14.1 4.9 %fusion.14 = f32[64,64,256]{2,1,0:T(8,128)} fusion(s32[64,64]{1,0:T(8,128)S(1)} %iota_subtract_fusion, f32[64,256]{0,1:T(8,128)} %multiply_reduce_fusion.4), kind=kOutput, calls=%fused_computation.28 | convolution fusion | flops 805568512 | bytes 4276224 | tf_op jit(solution)/shard_map/tsl,lc->tsc/dot_general | solution.py:36
  19.0 9.1 %copy.60 = f32[64,64,256]{1,0,2:T(8,128)} copy(f32[64,64,256]{2,1,0:T(8,128)} %fusion.14) | data formatting | bytes 8388608 | tf_op jit(solution)/shard_map/tsl,lc->tsc/dot_general | solution.py:36
  28.2 4.0 %multiply_exponential_fusion = (f32[16,16,256]{1,0,2:T(8,128)}, f32[16,256]{0,1:T(8,128)S(1)}, f32[256,16,16]{1,2,0:T(8,128)}) fusion(f32[16]{0:T(128)S(1)} %iota_multiply_fusion, f32[16,256]{0,1:T(8,128)S(1)} %copy.58, f32[16,64,256]{1,0,2:T(8,128)S(1)} %copy.68, f32[64]{0:T(128)S(1)} %iota_add_fusion), kind=kOutput, calls=%fused_computation.20 | convolution fusion | flops 25620480 | bytes 1605952 | tf_op jit(solution)/shard_map/ntc,tkc->nkc/dot_general | solution.py:8
  32.2 2.4 %rev.3 = f32[16,16,256]{1,0,2:T(8,128)S(1)} reverse(f32[16,16,256]{1,0,2:T(8,128)} %get-tuple-element.12), dimensions={0} | reverse | bytes 524288 | tf_op jit(solution)/shard_map/rev | solution.py:25
  34.7 25.5 %all-gather.1 = f32[256,256]{1,0:T(8,128)} all-gather(f32[16,256]{1,0:T(8,128)S(1)} %copy.70), channel_id=3, replica_groups=mesh['groups'=2,'ctx'=16] {'ctx'}, dimensions={0}, use_global_device_ids=true | all-gather | bytes 278528 | tf_op jit(solution)/shard_map/all_gather | solution.py:65
  60.2 3.2 %copy.92 = f32[16,256,16]{1,0,2:T(8,128)} copy(f32[16,256,16]{0,2,1:T(8,128)} %bitcast.56) | data formatting | bytes 524288
  63.4 2.7 %multiply_reduce_fusion = f32[16,256,16]{1,0,2:T(8,128)} fusion(f32[16,256,16]{1,0,2:T(8,128)} %copy.92, f32[16,16]{1,0:T(8,128)S(1)} %copy-done.11, f32[16,256]{1,0:T(8,128)S(1)} %copy-done.9, pred[16,16]{1,0:T(8,128)(4,1)S(1)} %copy-done.17), kind=kLoop, calls=%fused_computation | loop fusion | flops 4128768 | bytes 541952
  66.1 3.4 %copy.89 = f32[16,256,16]{0,2,1:T(8,128)} copy(f32[16,256,16]{1,0,2:T(8,128)} %multiply_reduce_fusion) | data formatting | bytes 524288 | tf_op jit(solution)/shard_map/mjkc,mkc->jkc/dot_general | solution.py:8
  69.5 4.3 %fusion = f32[256,64,16]{1,2,0:T(8,128)} fusion(f32[16,256,16]{0,2,1:T(8,128)} %copy.89, f32[16,256]{0,1:T(8,128)S(1)} %bitcast.61, f32[64]{0:T(128)S(1)} %copy-done.13, f32[16,256]{0,1:T(8,128)S(1)} %copy.58), kind=kOutput, calls=%fused_computation.3 | convolution fusion | flops 25493504 | bytes 1343744 | tf_op jit(solution)/shard_map/jkc,skc->jsc/dot_general | solution.py:8
  73.7 3.4 %copy.71 = f32[16,16,256]{1,0,2:T(8,128)} copy(f32[16,16,256]{2,1,0:T(8,128)} %bitcast.63) | data formatting | bytes 524288 | tf_op jit(solution)/shard_map/all_gather | solution.py:65
  77.1 3.1 %fusion.5 = (f32[16,256]{0,1:T(8,128)S(1)}, f32[256,16,16]{1,2,0:T(8,128)}) fusion(f32[16,16,256]{1,0,2:T(8,128)S(1)} %rev.3, bf16[16,64,256]{1,0,2:T(8,128)(2,1)S(1)} %copy.61, f32[64]{0:T(128)S(1)} %copy-done.13, f32[16,256]{0,1:T(8,128)S(1)} %copy.58), kind=kOutput, calls=%fused_computation.10 | convolution fusion | flops 25554944 | bytes 1081600 | tf_op jit(solution)/shard_map/nsc,skc->nkc/dot_general | solution.py:8
  80.3 3.2 %copy.91 = f32[16,256,16]{1,0,2:T(8,128)} copy(f32[16,256,16]{0,2,1:T(8,128)} %bitcast.57) | data formatting | bytes 524288
  83.6 2.7 %multiply_reduce_fusion.1 = f32[16,256,16]{1,0,2:T(8,128)} fusion(f32[16,256,16]{1,0,2:T(8,128)} %copy.91, f32[16,16]{1,0:T(8,128)S(1)} %copy-done.12, f32[16,256]{1,0:T(8,128)S(1)} %copy-done.10, pred[16,16]{1,0:T(8,128)(4,1)S(1)} %copy-done.18), kind=kLoop, calls=%fused_computation.1 | loop fusion | flops 4128768 | bytes 541952
  86.3 19.5 %all-gather = f32[256,256]{1,0:T(8,128)} all-gather(f32[16,256]{1,0:T(8,128)S(1)} %copy.64), channel_id=2, replica_groups=mesh['groups'=2,'ctx'=16] {'ctx'}, dimensions={0}, use_global_device_ids=true | all-gather | bytes 278528 | tf_op jit(solution)/shard_map/all_gather | solution.py:43
  105.8 3.4 %copy.65 = f32[16,16,256]{1,0,2:T(8,128)} copy(f32[16,16,256]{2,1,0:T(8,128)} %bitcast.64) | data formatting | bytes 524288 | tf_op jit(solution)/shard_map/all_gather | solution.py:43
  109.2 3.9 %multiply_reduce_fusion.2 = (f32[16,256]{0,1:T(8,128)S(1)}, f32[16,256]{0,1:T(8,128)S(1)}) fusion(f32[16,16,256]{1,0,2:T(8,128)} %copy.71, f32[16]{0:T(128)S(1)} %copy-done.22, f32[16,256]{0,1:T(8,128)S(1)} %copy.58, pred[16]{0:T(512)(128)(4,1)S(1)} %copy-done.25, f32[16,16,256]{1,0,2:T(8,128)} %copy.65, f32[16]{0:T(128)S(1)} %copy-done.23, ...), kind=kLoop, calls=%fused_computation.14 | loop fusion | flops 516096 | bytes 573600 | tf_op jit(solution)/shard_map/reduce_sum | solution.py:73
  113.2 1.4 fusion.6
  115.4 5.8 %add_bitcast_fusion = f32[16,64,256]{1,0,2:T(8,128)S(1)} fusion(f32[256,64,16]{1,2,0:T(8,128)S(1)} %fusion.6, f32[256,64,16]{1,2,0:T(8,128)S(1)} %copy-done.2, f32[64,64,256]{1,0,2:T(8,128)} %copy.60, f32[16,64,256]{1,0,2:T(8,128)S(1)} %copy-done.1), kind=kOutput, calls=%fused_computation.11 | convolution fusion | flops 101187584 | bytes 8388608 | tf_op jit(solution)/shard_map/ntc,tsc->nsc/dot_general | solution.py:8
  121.2 2.1 %copy.72 = f32[16,64,256]{2,1,0:T(8,128)} copy(f32[16,64,256]{1,0,2:T(8,128)S(1)} %add_bitcast_fusion) | data formatting | bytes 2097152 | tf_op jit(solution)/shard_map/add | solution.py:75
  123.3 2.2 %copy.81 = f32[16,256,16]{0,2,1:T(8,128)S(1)} copy(f32[16,256,16]{1,0,2:T(8,128)} %multiply_reduce_fusion.1) | data formatting | bytes 524288 | tf_op jit(solution)/shard_map/mjkc,jkc->mkc/dot_general | solution.py:8
  125.5 1.4 fusion.3
  127.0 1.6 %fusion.9 = f32[256,64,16]{1,2,0:T(8,128)S(1)} fusion(f32[16,256]{0,1:T(8,128)S(1)} %get-tuple-element.15, f32[16]{0:T(128)S(1)} %copy-done.21, f32[16,256]{0,1:T(8,128)S(1)} %copy.58, f32[64]{0:T(128)S(1)} %copy-done.16), kind=kOutput, calls=%fused_computation.17 | convolution fusion | flops 25559040 | bytes 1081664 | tf_op jit(solution)/shard_map/mkc,tkc->mtc/dot_general | solution.py:8
  128.6 6.9 %add_bitcast_fusion.1 = f32[16,64,256]{1,0,2:T(8,128)S(1)} fusion(f32[256,64,16]{1,2,0:T(8,128)S(1)} %fusion.9, f32[256,64,16]{1,2,0:T(8,128)S(1)} %fusion.3, f32[64,64,256]{1,0,2:T(8,128)} %copy.60, bf16[16,64,256]{1,0,2:T(8,128)(2,1)S(1)} %copy.61), kind=kOutput, calls=%fused_computation.16 | convolution fusion | flops 101187584 | bytes 7864320 | tf_op jit(solution)/shard_map/nsc,tsc->ntc/dot_general | solution.py:8
  135.6 2.0 %copy.66 = f32[16,64,256]{2,1,0:T(8,128)} copy(f32[16,64,256]{1,0,2:T(8,128)S(1)} %add_bitcast_fusion.1) | data formatting | bytes 2097152 | tf_op jit(solution)/shard_map/add | solution.py:53
  137.6 3.8 %fusion.19 = (bf16[1024,256]{1,0:T(8,128)(2,1)}, bf16[1024,256]{1,0:T(8,128)(2,1)}, bf16[1024,256]{1,0:T(8,128)(2,1)}, bf16[1024,256]{1,0:T(8,128)(2,1)}) fusion(bf16[1024,256]{1,0:T(8,128)(2,1)} %param.10, f32[16,64,256]{2,1,0:T(8,128)} %copy.66, bf16[1024,256]{1,0:T(8,128)(2,1)S(1)} %copy-done.4, f32[256]{0:T(256)S(1)} %copy-done.19, ...), kind=kLoop, calls=%fused_computation.39 | loop fusion | flops 4718592 | bytes 6816768 | tf_op jit(solution)/shard_map/convert_element_type | solution.py:57
  (64 shorter events, 4.7 us)
Async XLA Ops:
  0.6 9.8 %copy-start.6 = (bf16[1024,256]{1,0:T(8,128)(2,1)S(1)}, bf16[1024,256]{1,0:T(8,128)(2,1)}, u32[]{:S(2)}) copy-start(bf16[1024,256]{1,0:T(8,128)(2,1)} %param.10) | copy-start | bytes 1572868
  0.6 9.8 %copy-start.7 = (bf16[1024,256]{1,0:T(8,128)(2,1)S(1)}, bf16[1024,256]{1,0:T(8,128)(2,1)}, u32[]{:S(2)}) copy-start(bf16[1024,256]{1,0:T(8,128)(2,1)} %param.7) | copy-start | bytes 1572868
  0.7 27.5 %copy-start.15 = (f32[64]{0:T(128)}, f32[64]{0:T(128)S(1)}, u32[]{:S(2)}) copy-start(f32[64]{0:T(128)S(1)} %iota_add_fusion) | copy-start | bytes 772
  1.2 26.9 %copy-start.20 = (f32[16]{0:T(128)}, f32[16]{0:T(128)S(1)}, u32[]{:S(2)}) copy-start(f32[16]{0:T(128)S(1)} %iota_multiply_fusion) | copy-start | bytes 196
  4.3 0.6 copy-start.8
  9.5 2.1 %copy-start.3 = (bf16[1024,256]{1,0:T(8,128)(2,1)}, bf16[1024,256]{1,0:T(8,128)(2,1)S(1)}, u32[]{:S(2)}) copy-start(bf16[1024,256]{1,0:T(8,128)(2,1)S(1)} %fusion.17) | copy-start | bytes 1572868
  14.1 14.1 %copy-start = (f32[16,64,256]{1,0,2:T(8,128)}, f32[16,64,256]{1,0,2:T(8,128)S(1)}, u32[]{:S(2)}) copy-start(f32[16,64,256]{1,0,2:T(8,128)S(1)} %copy.68) | copy-start | bytes 3145732
  34.6 28.7 %copy-start.9 = (f32[16,256]{1,0:T(8,128)S(1)}, f32[16,256]{1,0:T(8,128)}, u32[]{:S(2)}) copy-start(f32[16,256]{1,0:T(8,128)} %copy-done.8) | copy-start | bytes 49156
  34.6 28.7 %copy-start.11 = (f32[16,16]{1,0:T(8,128)S(1)}, f32[16,16]{1,0:T(8,128)}, u32[]{:S(2)}) copy-start(f32[16,16]{1,0:T(8,128)} %convert_multiply_fusion.6) | copy-start | bytes 3076
  34.6 28.7 %copy-start.17 = (pred[16,16]{1,0:T(8,128)(4,1)S(1)}, pred[16,16]{1,0:T(8,128)(4,1)}, u32[]{:S(2)}) copy-start(pred[16,16]{1,0:T(8,128)(4,1)} %iota_compare_fusion.2) | copy-start | bytes 772
  63.4 6.1 %copy-start.13 = (f32[64]{0:T(128)S(1)}, f32[64]{0:T(128)}, u32[]{:S(2)}) copy-start(f32[64]{0:T(128)} %iota_subtract_fusion.1) | copy-start | bytes 772
  80.3 3.2 %copy-start.10 = (f32[16,256]{1,0:T(8,128)S(1)}, f32[16,256]{1,0:T(8,128)}, u32[]{:S(2)}) copy-start(f32[16,256]{1,0:T(8,128)} %copy-done.8) | copy-start | bytes 49156
  80.3 3.2 %copy-start.12 = (f32[16,16]{1,0:T(8,128)S(1)}, f32[16,16]{1,0:T(8,128)}, u32[]{:S(2)}) copy-start(f32[16,16]{1,0:T(8,128)} %convert_multiply_fusion.6) | copy-start | bytes 3076
  80.3 3.2 %copy-start.18 = (pred[16,16]{1,0:T(8,128)(4,1)S(1)}, pred[16,16]{1,0:T(8,128)(4,1)}, u32[]{:S(2)}) copy-start(pred[16,16]{1,0:T(8,128)(4,1)} %iota_compare_fusion.2) | copy-start | bytes 772
  83.5 25.7 %copy-start.22 = (f32[16]{0:T(128)S(1)}, f32[16]{0:T(128)}, u32[]{:S(2)}) copy-start(f32[16]{0:T(128)} %get-tuple-element.19) | copy-start | bytes 196
  83.5 25.7 %copy-start.23 = (f32[16]{0:T(128)S(1)}, f32[16]{0:T(128)}, u32[]{:S(2)}) copy-start(f32[16]{0:T(128)} %get-tuple-element.20) | copy-start | bytes 196
  83.5 25.7 %copy-start.24 = (pred[16]{0:T(512)(128)(4,1)S(1)}, pred[16]{0:T(512)(128)(4,1)}, u32[]{:S(2)}) copy-start(pred[16]{0:T(512)(128)(4,1)} %get-tuple-element.21) | copy-start | bytes 52
  83.6 25.7 %copy-start.25 = (pred[16]{0:T(512)(128)(4,1)S(1)}, pred[16]{0:T(512)(128)(4,1)}, u32[]{:S(2)}) copy-start(pred[16]{0:T(512)(128)(4,1)} %get-tuple-element.22) | copy-start | bytes 52
  109.2 3.9 %copy-start.14 = (f32[64]{0:T(128)S(1)}, f32[64]{0:T(128)}, u32[]{:S(2)}) copy-start(f32[64]{0:T(128)} %iota_subtract_fusion.1) | copy-start | bytes 772
  113.2 1.6 %copy-start.1 = (f32[16,64,256]{1,0,2:T(8,128)S(1)}, f32[16,64,256]{1,0,2:T(8,128)}, u32[]{:S(2)}) copy-start(f32[16,64,256]{1,0,2:T(8,128)} %copy-done) | copy-start | bytes 3145732
  113.2 2.2 %copy-start.2 = (f32[256,64,16]{1,2,0:T(8,128)S(1)}, f32[256,64,16]{1,2,0:T(8,128)}, u32[]{:S(2)}) copy-start(f32[256,64,16]{1,2,0:T(8,128)} %fusion) | copy-start | bytes 3145732
  121.2 4.3 %copy-start.16 = (f32[64]{0:T(128)S(1)}, f32[64]{0:T(128)}, u32[]{:S(2)}) copy-start(f32[64]{0:T(128)} %copy-done.15) | copy-start | bytes 772
  125.5 1.4 copy-start.21
  135.5 2.0 %copy-start.4 = (bf16[1024,256]{1,0:T(8,128)(2,1)S(1)}, bf16[1024,256]{1,0:T(8,128)(2,1)}, u32[]{:S(2)}) copy-start(bf16[1024,256]{1,0:T(8,128)(2,1)} %copy-done.3) | copy-start | bytes 1572868
  135.5 2.0 %copy-start.5 = (bf16[1024,256]{1,0:T(8,128)(2,1)S(1)}, bf16[1024,256]{1,0:T(8,128)(2,1)}, u32[]{:S(2)}) copy-start(bf16[1024,256]{1,0:T(8,128)(2,1)} %param.9) | copy-start | bytes 1572868
  135.5 2.0 %copy-start.19 = (f32[256]{0:T(256)S(1)}, f32[256]{0:T(256)}, u32[]{:S(2)}) copy-start(f32[256]{0:T(256)} %param.13) | copy-start | bytes 3076
where the time goes:
time: 142 us; the launch traced here: 141 us
  blocking collectives  45.1 us (32%)
  local copies, waits for them, and re-layouts  40.4 us (28%)
  matrix products  33.5 us (24%)
  other arithmetic  21.5 us (15%)
    dot_general x8, matrix products, product(): return jnp.einsum(pattern, first, second, precision=lax.Precision.HIGH)  28.6 us
    all_gather x1, blocking collectives, shards(): piece = lax.all_gather(own_adjoint[None], 'ctx', axis=0, tiled=True)  25.5 us
    all_gather x1, blocking collectives, shards(): piece = lax.all_gather(own_state[None], 'ctx', axis=0, tiled=True)  19.5 us
    dot_general x1, local copies, waits for them, and re-layouts, shards(): jnp.einsum('tsl,lc->tsc', lag_onehot, tap_values, precision=lax.Precision...  9.14 us
    unnamed x55, local copies, waits for them, and re-layouts  8.71 us
    dot_general x2, local copies, waits for them, and re-layouts, product(): return jnp.einsum(pattern, first, second, precision=lax.Precision.HIGH)  5.63 us
    unnamed x2, other arithmetic  5.42 us
    dot_general x1, matrix products, shards(): jnp.einsum('tsl,lc->tsc', lag_onehot, tap_values, precision=lax.Precision...  4.9 us

commit v1 on v0

v1 whole, which is shorter than its diff:
```python
import functools
import jax
import jax.numpy as jnp
from jax import lax
from jax.experimental import pallas as pl
from jax.experimental.pallas import tpu as pltpu
from jax.sharding import PartitionSpec as P

SEGS = 8
LANES = 128
PAD = 8
F32 = jnp.float32
BF16 = jnp.bfloat16
VMEM = pl.BlockSpec(memory_space=pltpu.VMEM)
HBM = pl.BlockSpec(memory_space=pltpu.HBM)


def half_slices(channels):
    return [slice(h, h + LANES) for h in range(0, channels, LANES)]


def rows_at(index, pitch):
    return pl.ds(index, SEGS, stride=pitch)


def state_kernel(
    seg_len,
    outer_hbm,
    inner_hbm,
    values_hbm,
    cotangent_hbm,
    rate_ref,
    residue_ref,
    mixed_ref,
    grad_ref,
    ends_ref,
    starts_ref,
    own_ref,
    table_ref,
    outer_ref,
    inner_ref,
    values_ref,
    cotangent_ref,
    copy_sems,
):
    rows, channels = inner_ref.shape
    poles = rate_ref.shape[0]
    pitch = seg_len + PAD
    halves = half_slices(channels)
    pairs = (
        (inner_hbm, inner_ref),
        (values_hbm, values_ref),
        (outer_hbm, outer_ref),
        (cotangent_hbm, cotangent_ref),
    )
    copies = []
    for h, lanes in enumerate(halves):
        line = []
        for j, (source, target) in enumerate(pairs):
            copy = pltpu.make_async_copy(
                source.at[:, lanes], target.at[:, lanes], copy_sems.at[h, j]
            )
            copy.start()
            line.append(copy)
        copies.append(line)
    rate_table = rate_ref[...]
    table_ref[0:poles, :] = rate_table
    table_ref[poles : 2 * poles, :] = residue_ref[...]
    decay = jnp.exp(-rate_table)
    seg_index = lax.broadcasted_iota(jnp.int32, (SEGS, LANES), 0).astype(F32)
    for h, lanes in enumerate(halves):
        for copy in copies[h]:
            copy.wait()
        for q in range(SEGS):
            source = slice(q * seg_len, (q + 1) * seg_len)
            target = slice(q * pitch, q * pitch + seg_len)
            mixed = inner_ref[source, lanes].astype(F32) * values_ref[source, lanes].astype(F32)
            mixed_ref[h, target, :] = mixed.astype(BF16).astype(F32)
            grad_ref[h, target, :] = outer_ref[source, lanes].astype(F32) * cotangent_ref[
                source, lanes
            ].astype(F32)
        steps = [jnp.broadcast_to(decay[k : k + 1, lanes], (SEGS, LANES)) for k in range(poles)]

        def body(i, carry):
            ahead, back = carry
            x = mixed_ref[h, rows_at(i, pitch), :]
            g = grad_ref[h, rows_at(seg_len - 1 - i, pitch), :]
            ahead = tuple(steps[k] * ahead[k] + x for k in range(poles))
            back = tuple(steps[k] * back[k] + g for k in range(poles))
            return ahead, back

        zero = jnp.zeros((SEGS, LANES), F32)
        start = (tuple(zero for _ in range(poles)),) * 2
        ahead, back = lax.fori_loop(0, seg_len, body, start, unroll=8)
        for k in range(poles):
            ends_ref[k, :, lanes] = ahead[k]
            starts_ref[k, :, lanes] = back[k]
            rate = jnp.broadcast_to(rate_table[k : k + 1, lanes], (SEGS, LANES))
            to_end = jnp.exp(-rate * (seg_len * (SEGS - 1.0 - seg_index)))
            to_start = jnp.exp(-rate * (seg_len * seg_index))
            own_ref[k : k + 1, lanes] = jnp.sum(to_end * ahead[k], axis=0, keepdims=True)
            own_ref[poles + k : poles + k + 1, lanes] = jnp.sum(
                to_start * back[k], axis=0, keepdims=True
            )


def local_kernel(seg_len, backward, half, signal_ref, table_ref, skip_ref, out_ref):
    poles = table_ref.shape[0] // 2
    pitch = seg_len + PAD
    lanes = slice(half * LANES, (half + 1) * LANES)
    decay = jnp.exp(-table_ref[0:poles, lanes])
    steps = [jnp.broadcast_to(decay[k : k + 1], (SEGS, LANES)) for k in range(poles)]
    weights = [
        jnp.broadcast_to(table_ref[poles + k : poles + k + 1, lanes], (SEGS, LANES))
        for k in range(poles)
    ]
    skip = jnp.broadcast_to(skip_ref[0:1, lanes], (SEGS, LANES))

    def body(i, states):
        row = seg_len - 1 - i if backward else i
        x = signal_ref[half, rows_at(row, pitch), :]
        states = tuple(steps[k] * states[k] + x for k in range(poles))
        terms = [weights[k] * states[k] for k in range(poles)] + [skip * x]
        while len(terms) > 1:
            terms = [a + b for a, b in zip(terms[::2], terms[1::2])] + (
                [terms[-1]] if len(terms) % 2 else []
            )
        out_ref[rows_at(row, pitch), :] = terms[0]
        return states

    zero = jnp.zeros((SEGS, LANES), F32)
    lax.fori_loop(0, seg_len, body, tuple(zero for _ in range(poles)), unroll=8)


def final_kernel(
    seg_len,
    outer_hbm,
    inner_hbm,
    values_hbm,
    cotangent_hbm,
    ends_ref,
    starts_ref,
    table_ref,
    entry_ref,
    *rest,
):
    channels = table_ref.shape[1]
    halves = half_slices(channels)
    count = len(halves)
    outer_ref, inner_ref, values_ref, cotangent_ref, in_sems = rest[2 * count + 9 :]
    loads = {}
    for h, lanes in enumerate(halves):
        for backward, pairs in (
            (False, ((outer_hbm, outer_ref), (cotangent_hbm, cotangent_ref))),
            (True, ((values_hbm, values_ref), (inner_hbm, inner_ref))),
        ):
            loads[h, backward] = [
                pltpu.make_async_copy(
                    source.at[:, lanes], target.at[:, lanes], in_sems.at[h, 2 * backward + j]
                )
                for j, (source, target) in enumerate(pairs)
            ]
            for copy in loads[h, backward]:
                copy.start()
    ahead_refs, back_refs = rest[:count], rest[count : 2 * count]
    layer_hbm, outer_grad_hbm, inner_grad_hbm, values_grad_hbm = rest[2 * count : 2 * count + 4]
    layer_ref, outer_grad_ref, inner_grad_ref, values_grad_ref = rest[2 * count + 4 : 2 * count + 8]
    sems = rest[2 * count + 8]
    poles = table_ref.shape[0] // 2
    pitch = seg_len + PAD
    step = 16
    inside = lax.broadcasted_iota(jnp.int32, (8, LANES), 0).astype(F32)
    copies = []
    for h, lanes in enumerate(halves):
        rates = [
            jnp.broadcast_to(table_ref[k : k + 1, lanes], (8, LANES)) for k in range(poles)
        ]
        weights = [
            jnp.broadcast_to(table_ref[poles + k : poles + k + 1, lanes], (8, LANES))
            for k in range(poles)
        ]
        strides = [jnp.exp(-8.0 * rates[k]) for k in range(poles)]
        for backward in (False, True):
            if backward:
                local_ref, edge_ref = back_refs[h], starts_ref
                pair = (values_ref, inner_ref)
                targets = ((inner_grad_ref, inner_grad_hbm), (values_grad_ref, values_grad_hbm))
                enter = [weights[k] * jnp.exp(-rates[k] * (8.0 - inside)) for k in range(poles)]
            else:
                local_ref, edge_ref = ahead_refs[h], ends_ref
                pair = (outer_ref, cotangent_ref)
                targets = ((layer_ref, layer_hbm), (outer_grad_ref, outer_grad_hbm))
                enter = [weights[k] * jnp.exp(-rates[k] * (inside + 1.0)) for k in range(poles)]
            base = poles if backward else 0
            carried = tuple(
                enter[k] * jnp.broadcast_to(entry_ref[base + k : base + k + 1, lanes], (8, LANES))
                for k in range(poles)
            )

            for copy in loads[h, backward]:
                copy.wait()

            def total(terms):
                terms = list(terms)
                while len(terms) > 1:
                    terms = [a + b for a, b in zip(terms[::2], terms[1::2])] + (
                        [terms[-1]] if len(terms) % 2 else []
                    )
                return terms[0]

            for n in range(SEGS):
                q = SEGS - 1 - n if backward else n

                def body(i, carried):
                    block = (seg_len // step - 1 - i) if backward else i
                    found = [None, None]
                    for sub in (1, 0) if backward else (0, 1):
                        row = pl.multiple_of(q * pitch + block * step + 8 * sub, 8)
                        found[sub] = total(carried + (local_ref[pl.ds(row, 8), :],))
                        carried = tuple(strides[k] * carried[k] for k in range(poles))
                    whole = jnp.concatenate(found, axis=0)
                    rows = pl.ds(pl.multiple_of(q * seg_len + block * step, step), step)
                    for gate_ref, (target, _) in zip(pair, targets):
                        target[rows, lanes] = (gate_ref[rows, lanes].astype(F32) * whole).astype(
                            BF16
                        )
                    return carried

                carried = lax.fori_loop(0, seg_len // step, body, carried, unroll=4)
                if n < SEGS - 1:
                    carried = tuple(
                        carried[k]
                        + enter[k]
                        * jnp.broadcast_to(edge_ref[k, q : q + 1, lanes], (8, LANES))
                        for k in range(poles)
                    )
            for j, (target, hbm) in enumerate(targets):
                copy = pltpu.make_async_copy(
                    target.at[:, lanes], hbm.at[:, lanes], sems.at[h, 2 * backward + j]
                )
                copy.start()
                copies.append(copy)
    for copy in copies:
        copy.wait()


def shards(outer_gate, inner_gate, values, cotangent, residue, decay_rate, skip_gain):
    rows, channels = values.shape
    poles = residue.shape[1]
    seg_len = rows // SEGS
    padded = SEGS * (seg_len + PAD)
    count = channels // LANES
    blocks = lax.axis_size("ctx")
    position = lax.axis_index("ctx")
    gate = jax.ShapeDtypeStruct((rows, channels), BF16)
    limit = pltpu.CompilerParams(vmem_limit_bytes=4 << 20)
    work = rows * channels * poles
    outer_gate, inner_gate, values, cotangent = (
        pltpu.with_memory_space_constraint(x, pltpu.HBM)
        for x in (outer_gate, inner_gate, values, cotangent)
    )
    mixed, grad, ends, starts, own, table = (
        pl.pallas_call(
            functools.partial(state_kernel, seg_len),
            out_shape=[jax.ShapeDtypeStruct((count, padded, LANES), F32)] * 2
            + [jax.ShapeDtypeStruct((poles, SEGS, channels), F32)] * 2
            + [jax.ShapeDtypeStruct((2 * poles, channels), F32)] * 2,
            in_specs=[HBM] * 4 + [VMEM] * 2,
            out_specs=[VMEM] * 6,
            scratch_shapes=[pltpu.VMEM((rows, channels), BF16)] * 4
            + [pltpu.SemaphoreType.DMA((count, 4))],
            compiler_params=limit,
            name="states",
        )(outer_gate, inner_gate, values, cotangent, decay_rate.T, residue.T)
    )
    skip = skip_gain[None, :]

    def local(signal, backward, half, held):
        signal, _ = lax.optimization_barrier((signal, held))
        return pl.pallas_call(
            functools.partial(local_kernel, seg_len, backward, half),
            out_shape=jax.ShapeDtypeStruct((padded, LANES), F32),
            in_specs=[VMEM] * 3,
            out_specs=VMEM,
            compiler_params=limit,
            cost_estimate=pl.CostEstimate(
                flops=work * 4 // count, bytes_accessed=padded * LANES * 8, transcendentals=0
            ),
            name="local",
        )(signal, table, skip)

    rates = table[:poles]
    jobs = [(mixed, False, h) for h in range(count)] + [(grad, True, h) for h in range(count)]
    found = []
    entry = jnp.zeros_like(own)
    reach = 1
    while reach < blocks:
        other = lax.ppermute(own, "ctx", [(i, i ^ reach) for i in range(blocks)])
        pieces = []
        if reach > 1 and jobs:
            pieces.append(local(*jobs.pop(0), own))
        later = (position // reach) % 2 == 1
        place = position % reach
        ahead_shift = (rows * place).astype(F32)
        back_shift = (rows * (reach - 1 - place)).astype(F32)
        entry = entry + other * jnp.concatenate(
            [
                jnp.where(later, jnp.exp(-rates * ahead_shift), 0.0),
                jnp.where(later, 0.0, jnp.exp(-rates * back_shift)),
            ]
        )
        span = jnp.exp(-rates * float(rows * reach))
        early = jnp.concatenate([span, jnp.ones_like(span)])
        late = jnp.concatenate([jnp.ones_like(span), span])
        own = jnp.where(later, late, early) * own + jnp.where(later, early, late) * other
        reach *= 2
        if reach < blocks:
            own, pieces = lax.optimization_barrier((own, pieces))
        found += pieces
    for job in jobs:
        found.append(local(*job, table))
    return pl.pallas_call(
        functools.partial(final_kernel, seg_len),
        out_shape=[gate] * 4,
        in_specs=[HBM] * 4 + [VMEM] * (4 + 2 * count),
        out_specs=[HBM] * 4,
        scratch_shapes=[pltpu.VMEM((rows, channels), BF16)] * 4
        + [pltpu.SemaphoreType.DMA((count, 4))]
        + [pltpu.VMEM((rows, channels), BF16)] * 4
        + [pltpu.SemaphoreType.DMA((count, 4))],
        compiler_params=pltpu.CompilerParams(vmem_limit_bytes=8 << 20),
        name="final",
    )(outer_gate, inner_gate, values, cotangent, ends, starts, table, entry, *found)


def solution(mesh):
    spread = P(("groups", "ctx"), None)
    return jax.shard_map(
        shards,
        mesh=mesh,
        in_specs=(spread,) * 4 + (P(),) * 3,
        out_specs=(spread,) * 4,
        check_vma=False,
    )
```

time: 142 us -> 28 us (0.20)
  blocking collectives: 45.1 us -> 0 us
  local copies, waits for them, and re-layouts: 40.4 us -> 1.43 us
  matrix products: 33.5 us -> 0 us
  other arithmetic: 21.5 us -> 0.09 us
  Pallas kernels: 0 us -> 14.6 us
  starting transfers between devices: 0 us -> 8.69 us
  waiting for transfers between devices: 0 us -> 2.07 us
    all_gather x2 -> x0, blocking collectives: 45.1 us -> none  [the longest x1 25.5 us: shards(): piece = lax.all_gather(own_adjoint[None], 'ctx', axis=0, tiled=True)]
    dot_general x9 -> x0, matrix products: 33.5 us -> none  [the longest x8 28.6 us: product(): return jnp.einsum(pattern, first, second, precision=lax.Precision.HIGH)]
    dot_general x3 -> x0, local copies, waits for them, and re-layouts: 14.8 us -> none  [the longest x1 9.14 us: shards(): jnp.einsum('tsl,lc->tsc', lag_onehot, tap_values, precision=lax.Precision...]
    pallas_call x0 -> x6, Pallas kernels: none -> 14.6 us  [the longest x1 5.34 us: shards(): pl.pallas_call(functools.partial(final_kernel, seg_len), out_shape=[gate]...]
    ppermute x0 -> x4, starting transfers between devices: none -> 8.69 us  [shards(): other = lax.ppermute(own, 'ctx', [(i, i ^ reach) for i in range(blocks)])]
    unnamed x55 -> x6, local copies, waits for them, and re-layouts: 8.71 us -> 1.43 us
    all_gather x2 -> x0, local copies, waits for them, and re-layouts: 6.76 us -> none  [the longest x1 3.39 us: shards(): piece = lax.all_gather(own_adjoint[None], 'ctx', axis=0, tiled=True)]
    reduce_sum x2 -> x0, other arithmetic: 6.16 us -> none  [the longest x1 3.88 us: shards(): suffix = jnp.sum(weight_rows * piece, axis=0)]
  transfers between devices with their start and end apart: 0 -> 4, of which waited for: 0 -> 3; matrix products, arithmetic and copies ran while one was open for 0% -> 0% of each run, Pallas kernels for 0% -> 18%
where the time goes in v1:
time: 28 us; the launch traced here: 27.6 us
  Pallas kernels  14.6 us (52%)
  starting transfers between devices  8.69 us (31%)
  waiting for transfers between devices  2.07 us (7%)
  local copies, waits for them, and re-layouts  1.43 us (5%)
  between operations  0.72 us (3%)
    ppermute x4, starting transfers between devices, shards(): other = lax.ppermute(own, 'ctx', [(i, i ^ reach) for i in range(blocks)])  8.69 us
    pallas_call x1, Pallas kernels, shards(): pl.pallas_call(functools.partial(final_kernel, seg_len), out_shape=[gate]...  5.34 us
    pallas_call x4, Pallas kernels, local(): pl.pallas_call(functools.partial(local_kernel, seg_len, backward, half),...  5.05 us
    pallas_call x1, Pallas kernels, shards(): pl.pallas_call(functools.partial(state_kernel, seg_len), out_shape=[jax.S...  4.24 us
    ppermute x4, waiting for transfers between devices, shards(): other = lax.ppermute(own, 'ctx', [(i, i ^ reach) for i in range(blocks)])  2.07 us
    unnamed x6, local copies, waits for them, and re-layouts  1.43 us
  transfers between devices with their start and end apart: 4, of which 3 were waited for; matrix products, arithmetic and copies ran while one was open for 0% of the time, Pallas kernels for 18%

profile of v1, /device:TPU:0, one launch (start us, length us, event | category | flops | bytes accessed | tf_op | source)
XLA Modules:
  0.0 27.6 jit_solution(4645377865631451035)
XLA Ops:
  0.6 0.0 copy-start
  0.6 0.7 %copy-done = f32[256,16]{0,1:T(8,128)S(1)} copy-done((f32[256,16]{0,1:T(8,128)S(1)}, f32[256,16]{0,1:T(8,128)}, u32[]{:S(2)}) %copy-start) | copy-done | bytes 16408
  1.4 0.0 copy-start.1
  1.4 0.7 %copy-done.1 = f32[256,16]{0,1:T(8,128)S(1)} copy-done((f32[256,16]{0,1:T(8,128)S(1)}, f32[256,16]{0,1:T(8,128)}, u32[]{:S(2)}) %copy-start.1) | copy-done | bytes 16408
  2.1 0.0 copy-start.2
  2.1 4.2 %states.1 = (f32[2,1088,128]{2,1,0:T(8,128)S(1)}, f32[2,1088,128]{2,1,0:T(8,128)S(1)}, f32[16,8,256]{2,1,0:T(8,128)S(1)}, f32[16,8,256]{2,1,0:T(8,128)S(1)}, f32...) custom-call(bf16[1024,256]{1,0:T(8,128)(2,1)} %outer_hbm.3, bf16[1024,256]{1,0:T(8,128)(2,1)} %inner_hbm.3, ...), custom_call_target="tpu_custom_call" | custom-call | tf_op jit(solution)/shard_map/states/pallas_call | solution.py:263
  6.3 0.5 %collective-permute-start = (f32[32,256]{1,0:T(8,128)S(1)}, f32[32,256]{1,0:T(8,128)S(1)}, u32[]{:S(2)}, u32[]{:S(2)}) collective-permute-start(f32[32,256]{1,0:T(8,128)S(1)} %get-tuple-element.21), channel_id=1, source_target_pairs={{0,1},{1,0},{2,3},{3,2},{4,5},{5,4},{6,7},{7,6},{8,9},{9,8},{10,11... | collective-permute-start | bytes 98312 | tf_op jit(solution)/shard_map/ppermute | solution.py:298
  6.9 0.8 %collective-permute-done = f32[32,256]{1,0:T(8,128)S(1)} collective-permute-done((f32[32,256]{1,0:T(8,128)S(1)}, f32[32,256]{1,0:T(8,128)S(1)}, u32[]{:S(2)}, u32[]{:S(2)}) %collective-permute-start) | collective-permute-done | bytes 32800 | tf_op jit(solution)/shard_map/ppermute | solution.py:298
  7.7 2.9 %collective-permute-start.1 = (f32[32,256]{1,0:T(8,128)S(1)}, f32[32,256]{1,0:T(8,128)S(1)}, u32[]{:S(2)}, u32[]{:S(2)}) collective-permute-start(f32[32,256]{1,0:T(8,128)S(1)} %fusion.1), channel_id=1, source_target_pairs={{0,2},{1,3},{2,0},{3,1},{4,6},{5,7},{6,4},{7,5},{8,10},{9,11},{10,... | collective-permute-start | bytes 98312 | tf_op jit(solution)/shard_map/ppermute | solution.py:298
  10.6 0.0 copy-done.2
  10.6 1.3 %local.4.rest_0_ = f32[1088,128]{1,0:T(8,128)S(1)} custom-call(f32[2,1088,128]{2,1,0:T(8,128)S(1)} %get-tuple-element.25.signal_ref, f32[32,256]{1,0:T(8,128)S(1)} %get-tuple-element.20.table_ref, f32[1,256]{1,0:T(1,128)S(1)} %bitcast.5), custom_call_target="tpu_custom_call" | custom-call | flops 8388608 | bytes 1114112 | tf_op jit(solution)/shard_map/local/pallas_call | solution.py:280
  11.9 0.6 %collective-permute-done.1 = f32[32,256]{1,0:T(8,128)S(1)} collective-permute-done((f32[32,256]{1,0:T(8,128)S(1)}, f32[32,256]{1,0:T(8,128)S(1)}, u32[]{:S(2)}, u32[]{:S(2)}) %collective-permute-start.1) | collective-permute-done | bytes 32800 | tf_op jit(solution)/shard_map/ppermute | solution.py:298
  12.5 2.2 %collective-permute-start.2 = (f32[32,256]{1,0:T(8,128)S(1)}, f32[32,256]{1,0:T(8,128)S(1)}, u32[]{:S(2)}, u32[]{:S(2)}) collective-permute-start(f32[32,256]{1,0:T(8,128)S(1)} %fusion.4), channel_id=1, source_target_pairs={{0,4},{1,5},{2,6},{3,7},{4,0},{5,1},{6,2},{7,3},{8,12},{9,13},{10,... | collective-permute-start | bytes 98312 | tf_op jit(solution)/shard_map/ppermute | solution.py:298
  14.7 1.3 %local.5.rest_1_ = f32[1088,128]{1,0:T(8,128)S(1)} custom-call(f32[2,1088,128]{2,1,0:T(8,128)S(1)} %get-tuple-element.25.signal_ref, f32[32,256]{1,0:T(8,128)S(1)} %get-tuple-element.20.table_ref, f32[1,256]{1,0:T(1,128)S(1)} %bitcast.6), custom_call_target="tpu_custom_call" | custom-call | flops 8388608 | bytes 1114112 | tf_op jit(solution)/shard_map/local/pallas_call | solution.py:280
  16.0 0.6 %collective-permute-done.2 = f32[32,256]{1,0:T(8,128)S(1)} collective-permute-done((f32[32,256]{1,0:T(8,128)S(1)}, f32[32,256]{1,0:T(8,128)S(1)}, u32[]{:S(2)}, u32[]{:S(2)}) %collective-permute-start.2) | collective-permute-done | bytes 32800 | tf_op jit(solution)/shard_map/ppermute | solution.py:298
  16.6 3.1 %collective-permute-start.3 = (f32[32,256]{1,0:T(8,128)S(1)}, f32[32,256]{1,0:T(8,128)S(1)}, u32[]{:S(2)}, u32[]{:S(2)}) collective-permute-start(f32[32,256]{1,0:T(8,128)S(1)} %fusion.7), channel_id=1, source_target_pairs={{0,8},{1,9},{2,10},{3,11},{4,12},{5,13},{6,14},{7,15},{8,0},{9,1},... | collective-permute-start | bytes 98312 | tf_op jit(solution)/shard_map/ppermute | solution.py:298
  19.7 1.3 %local.7.rest_3_ = f32[1088,128]{1,0:T(8,128)S(1)} custom-call(f32[2,1088,128]{2,1,0:T(8,128)S(1)} %get-tuple-element.31.signal_ref, f32[32,256]{1,0:T(8,128)S(1)} %get-tuple-element.20.table_ref, f32[1,256]{1,0:T(1,128)S(1)} %bitcast.7), custom_call_target="tpu_custom_call" | custom-call | flops 8388608 | bytes 1114112 | tf_op jit(solution)/shard_map/local/pallas_call | solution.py:280
  21.0 1.3 %local.6.rest_2_ = f32[1088,128]{1,0:T(8,128)S(1)} custom-call(f32[2,1088,128]{2,1,0:T(8,128)S(1)} %get-tuple-element.31.signal_ref, f32[32,256]{1,0:T(8,128)S(1)} %get-tuple-element.20.table_ref, f32[1,256]{1,0:T(1,128)S(1)} %bitcast.8), custom_call_target="tpu_custom_call" | custom-call | flops 8388608 | bytes 1114112 | tf_op jit(solution)/shard_map/local/pallas_call | solution.py:280
  22.2 0.0 collective-permute-done.3
  22.3 5.3 %final.1 = (bf16[1024,256]{1,0:T(8,128)(2,1)}, bf16[1024,256]{1,0:T(8,128)(2,1)}, bf16[1024,256]{1,0:T(8,128)(2,1)}, bf16[1024,256]{1,0:T(8,128)(2,1)}) custom-call(bf16[1024,256]{1,0:T(8,128)(2,1)} %outer_hbm.3, bf16[1024,256]{1,0:T(8,128)(2,1)} %inner_hbm.3, bf16[1024,256]{1,0:T(8,128)(2,1)} %values_hbm.3, bf16[1024,256]{1,0:T(8,128)(2,1)} %cotangent_hbm.3, ...), custom_call_target="tpu_custom_call" | custom-call | tf_op jit(solution)/shard_map/final/pallas_call | solution.py:322
  (6 shorter events, 0.1 us)
Async XLA Ops:
  0.6 0.7 %copy-start = (f32[256,16]{0,1:T(8,128)S(1)}, f32[256,16]{0,1:T(8,128)}, u32[]{:S(2)}) copy-start(f32[256,16]{0,1:T(8,128)} %param.12) | copy-start | bytes 49156
  1.4 0.7 %copy-start.1 = (f32[256,16]{0,1:T(8,128)S(1)}, f32[256,16]{0,1:T(8,128)}, u32[]{:S(2)}) copy-start(f32[256,16]{0,1:T(8,128)} %param.11) | copy-start | bytes 49156
  2.1 8.5 %copy-start.2 = (f32[256]{0:T(256)S(1)}, f32[256]{0:T(256)}, u32[]{:S(2)}) copy-start(f32[256]{0:T(256)} %param.13) | copy-start | bytes 3076
  6.3 1.4 %collective-permute-start = (f32[32,256]{1,0:T(8,128)S(1)}, f32[32,256]{1,0:T(8,128)S(1)}, u32[]{:S(2)}, u32[]{:S(2)}) collective-permute-start(f32[32,256]{1,0:T(8,128)S(1)} %get-tuple-element.21), channel_id=1, source_target_pairs={{0,1},{1,0},{2,3},{3,2},{4,5},{5,4},{6,7},{7,6},{8,9},{9,8},{10,11... | collective-permute-start | bytes 98312 | tf_op jit(solution)/shard_map/ppermute | solution.py:298
  7.7 4.8 %collective-permute-start.1 = (f32[32,256]{1,0:T(8,128)S(1)}, f32[32,256]{1,0:T(8,128)S(1)}, u32[]{:S(2)}, u32[]{:S(2)}) collective-permute-start(f32[32,256]{1,0:T(8,128)S(1)} %fusion.1), channel_id=1, source_target_pairs={{0,2},{1,3},{2,0},{3,1},{4,6},{5,7},{6,4},{7,5},{8,10},{9,11},{10,... | collective-permute-start | bytes 98312 | tf_op jit(solution)/shard_map/ppermute | solution.py:298
  12.5 4.1 %collective-permute-start.2 = (f32[32,256]{1,0:T(8,128)S(1)}, f32[32,256]{1,0:T(8,128)S(1)}, u32[]{:S(2)}, u32[]{:S(2)}) collective-permute-start(f32[32,256]{1,0:T(8,128)S(1)} %fusion.4), channel_id=1, source_target_pairs={{0,4},{1,5},{2,6},{3,7},{4,0},{5,1},{6,2},{7,3},{8,12},{9,13},{10,... | collective-permute-start | bytes 98312 | tf_op jit(solution)/shard_map/ppermute | solution.py:298
  16.6 5.6 %collective-permute-start.3 = (f32[32,256]{1,0:T(8,128)S(1)}, f32[32,256]{1,0:T(8,128)S(1)}, u32[]{:S(2)}, u32[]{:S(2)}) collective-permute-start(f32[32,256]{1,0:T(8,128)S(1)} %fusion.7), channel_id=1, source_target_pairs={{0,8},{1,9},{2,10},{3,11},{4,12},{5,13},{6,14},{7,15},{8,0},{9,1},... | collective-permute-start | bytes 98312 | tf_op jit(solution)/shard_map/ppermute | solution.py:298

commit v2 on v1

v2 whole, which is shorter than its diff:
```python
import functools
import jax
import jax.numpy as jnp
from jax import lax
from jax.experimental import pallas as pl
from jax.experimental.pallas import tpu as pltpu
from jax.sharding import PartitionSpec as P

SEGS = 8
LANES = 128
PAD = 8
STEP = 16
F32 = jnp.float32
BF16 = jnp.bfloat16
VMEM = pl.BlockSpec(memory_space=pltpu.VMEM)
HBM = pl.BlockSpec(memory_space=pltpu.HBM)


def lane_slice(half):
    return slice(half * LANES, (half + 1) * LANES)


def add_up(terms):
    while len(terms) > 1:
        odd = [terms[-1]] if len(terms) % 2 else []
        terms = [a + b for a, b in zip(terms[::2], terms[1::2])] + odd
    return terms[0]


def spread_rows(table, lanes, count):
    return [jnp.broadcast_to(table[k : k + 1, lanes], (8, LANES)) for k in range(count)]


def state_kernel(
    seg_len,
    outer_hbm,
    inner_hbm,
    values_hbm,
    cotangent_hbm,
    rate_hbm,
    residue_hbm,
    mixed_ref,
    grad_ref,
    ends_ref,
    starts_ref,
    own_ref,
    table_ref,
    outer_ref,
    inner_ref,
    values_ref,
    cotangent_ref,
    copy_sems,
    table_sems,
):
    poles = rate_hbm.shape[0]
    pitch = seg_len + PAD
    count = mixed_ref.shape[0]
    tables = [
        pltpu.make_async_copy(
            source, table_ref.at[pl.ds(j * poles, poles), :], table_sems.at[j]
        )
        for j, source in enumerate((rate_hbm, residue_hbm))
    ]
    for copy in tables:
        copy.start()
    pairs = (
        (inner_hbm, inner_ref),
        (values_hbm, values_ref),
        (outer_hbm, outer_ref),
        (cotangent_hbm, cotangent_ref),
    )
    copies = []
    for h in range(count):
        line = []
        for j, (source, target) in enumerate(pairs):
            copy = pltpu.make_async_copy(
                source.at[:, lane_slice(h)], target.at[:, lane_slice(h)], copy_sems.at[h, j]
            )
            copy.start()
            line.append(copy)
        copies.append(line)
    for copy in tables:
        copy.wait()
    rate_table = table_ref[0:poles, :]
    decay = jnp.exp(-rate_table)
    seg_decay = jnp.exp(-float(seg_len) * rate_table)
    for h in range(count):
        lanes = lane_slice(h)
        for copy in copies[h]:
            copy.wait()

        def convert(q, _):
            source = pl.ds(pl.multiple_of(q * seg_len, 16), seg_len)
            target = pl.ds(pl.multiple_of(q * pitch, 8), seg_len)
            mixed = inner_ref[source, lanes].astype(F32) * values_ref[source, lanes].astype(F32)
            mixed_ref[h, target, :] = mixed.astype(BF16).astype(F32)
            outer, cotangent = outer_ref[source, lanes], cotangent_ref[source, lanes]
            grad_ref[h, target, :] = outer.astype(F32) * cotangent.astype(F32)
            return _

        lax.fori_loop(0, SEGS, convert, 0)
        steps = spread_rows(decay, lanes, poles)

        def body(i, carry):
            ahead, back = carry
            x = mixed_ref[h, pl.ds(i, SEGS, stride=pitch), :]
            g = grad_ref[h, pl.ds(seg_len - 1 - i, SEGS, stride=pitch), :]
            ahead = tuple(steps[k] * ahead[k] + x for k in range(poles))
            back = tuple(steps[k] * back[k] + g for k in range(poles))
            return ahead, back

        zero = jnp.zeros((SEGS, LANES), F32)
        start = (tuple(zero for _ in range(poles)),) * 2
        ahead, back = lax.fori_loop(0, seg_len, body, start, unroll=8)
        for k in range(poles):
            ends_ref[h, 8 * k : 8 * k + 8, :] = ahead[k]
            starts_ref[h, 8 * k : 8 * k + 8, :] = back[k]
        ahead = jnp.zeros((poles, LANES), F32)
        back = jnp.zeros((poles, LANES), F32)
        for q in range(SEGS):
            ahead = seg_decay[:, lanes] * ahead + ends_ref[h, pl.ds(q, poles, stride=8), :]
            back = seg_decay[:, lanes] * back + starts_ref[
                h, pl.ds(SEGS - 1 - q, poles, stride=8), :
            ]
        own_ref[0:poles, lanes] = ahead
        own_ref[poles : 2 * poles, lanes] = back


def local_kernel(seg_len, backward, half, signal_ref, table_ref, skip_ref, out_ref):
    poles = table_ref.shape[0] // 2
    pitch = seg_len + PAD
    lanes = lane_slice(half)
    steps = spread_rows(jnp.exp(-table_ref[0:poles, :]), lanes, poles)
    weights = spread_rows(table_ref[poles : 2 * poles, :], lanes, poles)
    skip = jnp.broadcast_to(skip_ref[0:1, lanes], (SEGS, LANES))

    def body(i, states):
        row = seg_len - 1 - i if backward else i
        x = signal_ref[half, pl.ds(row, SEGS, stride=pitch), :]
        states = tuple(steps[k] * states[k] + x for k in range(poles))
        terms = [weights[k] * states[k] for k in range(poles)] + [skip * x]
        out_ref[pl.ds(row, SEGS, stride=pitch), :] = add_up(terms)
        return states

    zero = jnp.zeros((SEGS, LANES), F32)
    lax.fori_loop(0, seg_len, body, tuple(zero for _ in range(poles)), unroll=8)


def finish_way(seg_len, backward, gates, locals_, edge_ref, table_ref, entry_ref, targets, sems):
    poles = table_ref.shape[0] // 2
    pitch = seg_len + PAD
    inside = lax.broadcasted_iota(jnp.int32, (8, LANES), 0).astype(F32)
    reach = 8.0 - inside if backward else inside + 1.0
    blocks = seg_len // STEP
    copies = []
    for h, local_ref in enumerate(locals_):
        lanes = lane_slice(h)
        rates = spread_rows(table_ref[0:poles, :], lanes, poles)
        weights = spread_rows(table_ref[poles : 2 * poles, :], lanes, poles)
        strides = [jnp.exp(-8.0 * rates[k]) for k in range(poles)]
        enter = [weights[k] * jnp.exp(-rates[k] * reach) for k in range(poles)]
        entry = spread_rows(entry_ref[...], lanes, poles)

        def segment(n, carried, local_ref=local_ref, lanes=lanes, h=h):
            q = SEGS - 1 - n if backward else n

            for i in range(blocks):
                block = blocks - 1 - i if backward else i
                found = [None, None]
                for sub in (1, 0) if backward else (0, 1):
                    row = pl.multiple_of(q * pitch + block * STEP + 8 * sub, 8)
                    found[sub] = add_up([*carried, local_ref[pl.ds(row, 8), :]])
                    carried = tuple(strides[k] * carried[k] for k in range(poles))
                whole = jnp.concatenate(found, axis=0)
                rows = pl.ds(pl.multiple_of(q * seg_len + block * STEP, STEP), STEP)
                for gate_ref, (target, _) in zip(gates, targets):
                    target[rows, lanes] = (gate_ref[rows, lanes].astype(F32) * whole).astype(BF16)
            return tuple(
                carried[k]
                + enter[k]
                * jnp.broadcast_to(edge_ref[h, pl.ds(8 * k + q, 1), :], (8, LANES))
                for k in range(poles)
            )

        lax.fori_loop(0, SEGS, segment, tuple(enter[k] * entry[k] for k in range(poles)))
        for j, (target, hbm) in enumerate(targets):
            copy = pltpu.make_async_copy(target.at[:, lanes], hbm.at[:, lanes], sems.at[h, j])
            copy.start()
            copies.append(copy)
    for copy in copies:
        copy.wait()


def load(pairs, sems):
    copies = [
        pltpu.make_async_copy(source, target, sems.at[j])
        for j, (source, target) in enumerate(pairs)
    ]
    for copy in copies:
        copy.start()
    return copies


def settled_kernel(
    seg_len,
    count,
    blocks,
    outer_hbm,
    inner_hbm,
    values_hbm,
    cotangent_hbm,
    ends_ref,
    starts_ref,
    table_ref,
    entry_ref,
    *rest,
):
    locals_ahead, locals_back = rest[:count], rest[count : 2 * count]
    layer_hbm, outer_grad_hbm, inner_grad_hbm, values_grad_hbm, next_a, next_b = rest[
        2 * count : 2 * count + 6
    ]
    gate_a, gate_b, out_a, out_b, load_sems, next_sems, out_sems = rest[2 * count + 6 :]
    later = lax.axis_index("ctx") >= blocks // 2

    def run(backward):
        pairs = [
            ((outer_hbm, gate_a), (cotangent_hbm, gate_b)),
            ((values_hbm, gate_a), (inner_hbm, gate_b)),
        ]
        others = [
            ((outer_hbm, next_a), (cotangent_hbm, next_b)),
            ((values_hbm, next_a), (inner_hbm, next_b)),
        ]
        now = load(pairs[backward], load_sems)
        following = load(others[1 - backward], next_sems)
        for copy in now:
            copy.wait()
        targets = (
            ((out_a, inner_grad_hbm), (out_b, values_grad_hbm))
            if backward
            else ((out_a, layer_hbm), (out_b, outer_grad_hbm))
        )
        finish_way(
            seg_len,
            backward,
            (gate_a, gate_b),
            locals_back if backward else locals_ahead,
            starts_ref if backward else ends_ref,
            table_ref,
            entry_ref,
            targets,
            out_sems,
        )
        for copy in following:
            copy.wait()

    pl.when(later)(functools.partial(run, True))
    pl.when(jnp.logical_not(later))(functools.partial(run, False))


def last_kernel(
    seg_len,
    count,
    blocks,
    gate_a,
    gate_b,
    ends_ref,
    starts_ref,
    table_ref,
    entry_ref,
    *rest,
):
    locals_ahead, locals_back = rest[:count], rest[count : 2 * count]
    layer_hbm, outer_grad_hbm, inner_grad_hbm, values_grad_hbm = rest[
        2 * count + 4 : 2 * count + 8
    ]
    out_a, out_b, out_sems = rest[2 * count + 8 :]
    later = lax.axis_index("ctx") >= blocks // 2

    def run(backward):
        targets = (
            ((out_a, inner_grad_hbm), (out_b, values_grad_hbm))
            if backward
            else ((out_a, layer_hbm), (out_b, outer_grad_hbm))
        )
        finish_way(
            seg_len,
            backward,
            (gate_a, gate_b),
            locals_back if backward else locals_ahead,
            starts_ref if backward else ends_ref,
            table_ref,
            entry_ref,
            targets,
            out_sems,
        )

    pl.when(later)(functools.partial(run, False))
    pl.when(jnp.logical_not(later))(functools.partial(run, True))


def shards(outer_gate, inner_gate, values, cotangent, residue, decay_rate, skip_gain):
    rows, channels = values.shape
    poles = residue.shape[1]
    seg_len = rows // SEGS
    padded = SEGS * (seg_len + PAD)
    count = channels // LANES
    blocks = lax.axis_size("ctx")
    position = lax.axis_index("ctx")
    gate = jax.ShapeDtypeStruct((rows, channels), BF16)
    limit = pltpu.CompilerParams(vmem_limit_bytes=4 << 20)
    work = rows * channels * poles
    dma = pltpu.SemaphoreType.DMA

    def in_hbm(x):
        return pltpu.with_memory_space_constraint(x, pltpu.HBM)

    arrays = [in_hbm(x) for x in (outer_gate, inner_gate, values, cotangent)]
    mixed, grad, ends, starts, own, table = pl.pallas_call(
        functools.partial(state_kernel, seg_len),
        out_shape=[jax.ShapeDtypeStruct((count, padded, LANES), F32)] * 2
        + [jax.ShapeDtypeStruct((count, 8 * poles, LANES), F32)] * 2
        + [jax.ShapeDtypeStruct((2 * poles, channels), F32)] * 2,
        in_specs=[HBM] * 6,
        out_specs=[VMEM] * 6,
        scratch_shapes=[pltpu.VMEM((rows, channels), BF16)] * 4 + [dma((count, 4)), dma((2,))],
        compiler_params=limit,
        name="states",
    )(*arrays, in_hbm(decay_rate.T), in_hbm(residue.T))
    skip = skip_gain[None, :]

    def local(signal, backward, half, held):
        signal, _ = lax.optimization_barrier((signal, held))
        return pl.pallas_call(
            functools.partial(local_kernel, seg_len, backward, half),
            out_shape=jax.ShapeDtypeStruct((padded, LANES), F32),
            in_specs=[VMEM] * 3,
            out_specs=VMEM,
            compiler_params=limit,
            cost_estimate=pl.CostEstimate(
                flops=work * 4 // count, bytes_accessed=padded * LANES * 8, transcendentals=0
            ),
            name="local",
        )(signal, table, skip)

    rates = table[:poles]
    jobs = [(mixed, False, h) for h in range(count)] + [(grad, True, h) for h in range(count)]
    middle = max(blocks.bit_length() - 3, 1)
    share = -(-len(jobs) // middle)
    found = []
    ahead_entry = jnp.zeros((poles, channels), F32)
    back_entry = ahead_entry
    reach = 1
    while reach < blocks // 2:
        other = lax.ppermute(own, "ctx", [(i, i ^ reach) for i in range(blocks)])
        pieces = []
        if reach > 1:
            now, jobs = jobs[:share], jobs[share:]
            pieces = [local(*job, own) for job in now]
        later = (position // reach) % 2 == 1
        place = position % reach
        ahead_shift = jnp.exp(-rates * (rows * place).astype(F32))
        back_shift = jnp.exp(-rates * (rows * (reach - 1 - place)).astype(F32))
        ahead_entry = ahead_entry + jnp.where(later, ahead_shift, 0.0) * other[:poles]
        back_entry = back_entry + jnp.where(later, 0.0, back_shift) * other[poles:]
        span = jnp.exp(-rates * float(rows * reach))
        early = jnp.concatenate([span, jnp.ones_like(span)])
        late = jnp.concatenate([jnp.ones_like(span), span])
        own = jnp.where(later, late, early) * own + jnp.where(later, early, late) * other
        reach *= 2
        if pieces:
            own, pieces = lax.optimization_barrier((own, pieces))
        found += pieces
    found += [local(*job, own) for job in jobs]
    later = position >= reach
    place = position % reach
    sent = jnp.where(later, own[poles:], own[:poles])
    other = lax.ppermute(sent, "ctx", [(i, i ^ reach) for i in range(blocks)])
    *outs, gate_a, gate_b = pl.pallas_call(
        functools.partial(settled_kernel, seg_len, count, blocks),
        out_shape=[gate] * 6,
        in_specs=[HBM] * 4 + [VMEM] * (4 + 2 * count),
        out_specs=[HBM] * 4 + [VMEM] * 2,
        scratch_shapes=[pltpu.VMEM((rows, channels), BF16)] * 4
        + [dma((2,)), dma((2,)), dma((count, 2))],
        compiler_params=limit,
        cost_estimate=pl.CostEstimate(
            flops=work * 2, bytes_accessed=rows * channels * 12, transcendentals=0
        ),
        name="settled",
    )(*arrays, ends, starts, table, jnp.where(later, back_entry, ahead_entry), *found)
    shift = jnp.exp(-rates * (rows * jnp.where(later, place, reach - 1 - place)).astype(F32))
    entry = jnp.where(later, ahead_entry, back_entry) + shift * other
    first = 6 + 2 * count
    return pl.pallas_call(
        functools.partial(last_kernel, seg_len, count, blocks),
        out_shape=[gate] * 4,
        in_specs=[VMEM] * first + [HBM] * 4,
        out_specs=[HBM] * 4,
        input_output_aliases={first + j: j for j in range(4)},
        scratch_shapes=[pltpu.VMEM((rows, channels), BF16)] * 2 + [dma((count, 2))],
        compiler_params=limit,
        name="last",
    )(gate_a, gate_b, ends, starts, table, entry, *found, *outs)


def solution(mesh):
    spread = P(("groups", "ctx"), None)
    return jax.shard_map(
        shards,
        mesh=mesh,
        in_specs=(spread,) * 4 + (P(),) * 3,
        out_specs=(spread,) * 4,
        check_vma=False,
    )
```

time: 28 us -> 31.4 us (1.12)
  other arithmetic: 0.09 us -> 3.04 us
  Pallas kernels: 14.6 us -> 15.7 us
  starting transfers between devices: 8.69 us -> 7.64 us
    ppermute x4 -> x3, starting transfers between devices: 8.69 us -> 4.98 us  [shards(): other = lax.ppermute(own, 'ctx', [(i, i ^ reach) for i in range(blocks)])]
    ppermute x0 -> x1, starting transfers between devices: none -> 2.65 us  [shards(): other = lax.ppermute(sent, 'ctx', [(i, i ^ reach) for i in range(blocks)])]
    ppermute x0 -> x1, waiting for transfers between devices: none -> 2.05 us  [shards(): other = lax.ppermute(sent, 'ctx', [(i, i ^ reach) for i in range(blocks)])]
    ppermute x4 -> x3, waiting for transfers between devices: 2.07 us -> 0.24 us  [shards(): other = lax.ppermute(own, 'ctx', [(i, i ^ reach) for i in range(blocks)])]
    add x3, other arithmetic: 0.03 us -> 1.57 us  [shards(): jnp.where(later, late, early) * own + jnp.where(later, early, late) * other]
    pallas_call x1 -> x2, Pallas kernels: 5.34 us -> 6.31 us  [the longest x1 3.82 us: shards(): pl.pallas_call(functools.partial(settled_kernel, seg_len, count, blocks),...]
    add x1, other arithmetic: 0.02 us -> 0.84 us  [shards(): entry = jnp.where(later, ahead_entry, back_entry) + shift * other]
    exp x0 -> x1, other arithmetic: none -> 0.62 us  [shards(): span = jnp.exp(-rates * float(rows * reach))]
  transfers between devices with their start and end apart: 4 -> 4, of which waited for: 3 -> 2; matrix products, arithmetic and copies ran while one was open for 0% -> 2% of each run, Pallas kernels for 18% -> 16%
where the time goes in v2:
time: 31.4 us; the launch traced here: 31.1 us
  Pallas kernels  15.7 us (50%)
  starting transfers between devices  7.64 us (24%)
  other arithmetic  3.04 us (10%)
  waiting for transfers between devices  2.29 us (7%)
  local copies, waits for them, and re-layouts  1.57 us (5%)
  between operations  0.78 us (2%)
    pallas_call x4, Pallas kernels, local(): pl.pallas_call(functools.partial(local_kernel, seg_len, backward, half),...  5.05 us
    ppermute x3, starting transfers between devices, shards(): other = lax.ppermute(own, 'ctx', [(i, i ^ reach) for i in range(blocks)])  4.98 us
    pallas_call x1, Pallas kernels, shards(): pl.pallas_call(functools.partial(state_kernel, seg_len), out_shape=[jax.S...  4.37 us
    pallas_call x1, Pallas kernels, shards(): pl.pallas_call(functools.partial(settled_kernel, seg_len, count, blocks),...  3.82 us
    ppermute x1, starting transfers between devices, shards(): other = lax.ppermute(sent, 'ctx', [(i, i ^ reach) for i in range(blocks)])  2.65 us
    pallas_call x1, Pallas kernels, shards(): pl.pallas_call(functools.partial(last_kernel, seg_len, count, blocks), ou...  2.49 us
    ppermute x1, waiting for transfers between devices, shards(): other = lax.ppermute(sent, 'ctx', [(i, i ^ reach) for i in range(blocks)])  2.05 us
    unnamed x14, local copies, waits for them, and re-layouts  1.57 us
  transfers between devices with their start and end apart: 4, of which 2 were waited for; matrix products, arithmetic and copies ran while one was open for 2% of the time, Pallas kernels for 16%

profile of v2, /device:TPU:0, one launch (start us, length us, event | category | flops | bytes accessed | tf_op | source)
XLA Modules:
  0.0 31.1 jit_solution(3290654445857198606)
XLA Ops:
  0.6 0.0 copy-start.2
  0.6 4.4 %states.1 = (f32[2,1088,128]{2,1,0:T(8,128)S(1)}, f32[2,1088,128]{2,1,0:T(8,128)S(1)}, f32[2,128,128]{2,1,0:T(8,128)S(1)}, f32[2,128,128]{2,1,0:T(8,128)S(1)}, f...) custom-call(bf16[1024,256]{1,0:T(8,128)(2,1)} %outer_hbm.3, bf16[1024,256]{1,0:T(8,128)(2,1)} %inner_hbm.3, ...), custom_call_target="tpu_custom_call" | custom-call | tf_op jit(solution)/shard_map/states/pallas_call | solution.py:319
  5.0 0.0 copy-start
  5.0 0.6 %copy-done = f32[2,128,128]{2,1,0:T(8,128)} copy-done((f32[2,128,128]{2,1,0:T(8,128)}, f32[2,128,128]{2,1,0:T(8,128)S(1)}, u32[]{:S(2)}) %copy-start) | copy-done | bytes 131096
  5.7 0.5 %collective-permute-start = (f32[32,256]{1,0:T(8,128)S(1)}, f32[32,256]{1,0:T(8,128)S(1)}, u32[]{:S(2)}, u32[]{:S(2)}) collective-permute-start(f32[32,256]{1,0:T(8,128)S(1)} %get-tuple-element.27), channel_id=1, source_target_pairs={{0,1},{1,0},{2,3},{3,2},{4,5},{5,4},{6,7},{7,6},{8,9},{9,8},{10,11... | collective-permute-start | bytes 98312 | tf_op jit(solution)/shard_map/ppermute | solution.py:355
  6.1 0.6 %multiply_exponential_fusion = (f32[16,256]{1,0:T(8,128)}, f32[16,256]{1,0:T(8,128)S(1)}, f32[16,256]{1,0:T(8,128)}) fusion(f32[32,256]{1,0:T(8,128)S(1)} %get-tuple-element.26.table_ref), kind=kLoop, calls=%fused_computation.27 | loop fusion | flops 16384 | bytes 65536 | tf_op jit(solution)/shard_map/exp | solution.py:366
  6.8 0.2 collective-permute-done
  7.0 0.0 copy-start.3
  7.0 2.9 %collective-permute-start.1 = (f32[32,256]{1,0:T(8,128)S(1)}, f32[32,256]{1,0:T(8,128)}, u32[]{:S(2)}, u32[]{:S(2)}) collective-permute-start(f32[32,256]{1,0:T(8,128)S(1)} %fusion.1), channel_id=1, source_target_pairs={{0,2},{1,3},{2,0},{3,1},{4,6},{5,7},{6,4},{7,5},{8,10},{9,11},{10,... | collective-permute-start | bytes 98312 | tf_op jit(solution)/shard_map/ppermute | solution.py:355
  9.9 0.0 copy-done.4
  9.9 0.0 copy-done.2
  9.9 1.3 %local.5.rest_1_ = f32[1088,128]{1,0:T(8,128)S(1)} custom-call(f32[2,1088,128]{2,1,0:T(8,128)S(1)} %get-tuple-element.29.signal_ref, f32[32,256]{1,0:T(8,128)S(1)} %get-tuple-element.26.table_ref, f32[1,256]{1,0:T(1,128)S(1)} %bitcast.3), custom_call_target="tpu_custom_call" | custom-call | flops 8388608 | bytes 1114112 | tf_op jit(solution)/shard_map/local/pallas_call | solution.py:334
  11.2 0.0 copy-start.6
  11.2 1.3 %local.4.rest_0_ = f32[1088,128]{1,0:T(8,128)S(1)} custom-call(f32[2,1088,128]{2,1,0:T(8,128)S(1)} %get-tuple-element.29.signal_ref, f32[32,256]{1,0:T(8,128)S(1)} %get-tuple-element.26.table_ref, f32[1,256]{1,0:T(1,128)S(1)} %bitcast.4), custom_call_target="tpu_custom_call" | custom-call | flops 8388608 | bytes 1114112 | tf_op jit(solution)/shard_map/local/pallas_call | solution.py:334
  12.5 0.0 copy-done.3
  12.5 0.0 collective-permute-done.1
  12.5 0.0 copy-done.6
  12.5 0.8 %fusion.4 = f32[32,256]{1,0:T(8,128)S(1)} fusion(f32[32,256]{1,0:T(8,128)} %copy-done.3, f32[16,256]{1,0:T(8,128)S(1)} %copy-done.6, f32[32,256]{1,0:T(8,128)} %collective-permute-done.1, pred[]{:T(512)S(6)} %eq.18), kind=kLoop, calls=%fused_computation.10 | loop fusion | flops 40960 | bytes 114689 | tf_op jit(solution)/shard_map/add | solution.py:369
  13.3 1.6 %collective-permute-start.2 = (f32[32,256]{1,0:T(8,128)S(1)}, f32[32,256]{1,0:T(8,128)}, u32[]{:S(2)}, u32[]{:S(2)}) collective-permute-start(f32[32,256]{1,0:T(8,128)S(1)} %fusion.4), channel_id=1, source_target_pairs={{0,4},{1,5},{2,6},{3,7},{4,0},{5,1},{6,2},{7,3},{8,12},{9,13},{10,... | collective-permute-start | bytes 98312 | tf_op jit(solution)/shard_map/ppermute | solution.py:355
  14.9 1.3 %local.7.rest_3_ = f32[1088,128]{1,0:T(8,128)S(1)} custom-call(f32[2,1088,128]{2,1,0:T(8,128)S(1)} %get-tuple-element.34.signal_ref, f32[32,256]{1,0:T(8,128)S(1)} %get-tuple-element.26.table_ref, f32[1,256]{1,0:T(1,128)S(1)} %bitcast.5), custom_call_target="tpu_custom_call" | custom-call | flops 8388608 | bytes 1114112 | tf_op jit(solution)/shard_map/local/pallas_call | solution.py:334
  16.2 0.0 copy-start.5
  16.2 1.3 %local.6.rest_2_ = f32[1088,128]{1,0:T(8,128)S(1)} custom-call(f32[2,1088,128]{2,1,0:T(8,128)S(1)} %get-tuple-element.34.signal_ref, f32[32,256]{1,0:T(8,128)S(1)} %get-tuple-element.26.table_ref, f32[1,256]{1,0:T(1,128)S(1)} %bitcast.6), custom_call_target="tpu_custom_call" | custom-call | flops 8388608 | bytes 1114112 | tf_op jit(solution)/shard_map/local/pallas_call | solution.py:334
  17.5 0.0 collective-permute-done.2
  17.5 0.0 copy-done.5
  17.5 0.8 %fusion.7 = f32[32,256]{1,0:T(8,128)S(1)} fusion(f32[32,256]{1,0:T(8,128)S(1)} %fusion.4, f32[16,256]{1,0:T(8,128)S(1)} %copy-done.5, f32[32,256]{1,0:T(8,128)} %collective-permute-done.2, pred[]{:T(512)S(6)} %eq.19), kind=kLoop, calls=%fused_computation.13 | loop fusion | flops 40960 | bytes 114689 | tf_op jit(solution)/shard_map/add | solution.py:369
  18.3 2.7 %collective-permute-start.3 = (f32[16,256]{1,0:T(8,128)S(1)}, f32[16,256]{1,0:T(8,128)S(1)}, u32[]{:S(2)}, u32[]{:S(2)}) collective-permute-start(f32[16,256]{1,0:T(8,128)S(1)} %slice_select_fusion), channel_id=1, source_target_pairs={{0,8},{1,9},{2,10},{3,11},{4,12},{5,13},{6,14},{7,15},{8,0},{9,1},... | collective-permute-start | bytes 49160 | tf_op jit(solution)/shard_map/ppermute | solution.py:378
  20.9 2.0 %collective-permute-done.3 = f32[16,256]{1,0:T(8,128)S(1)} collective-permute-done((f32[16,256]{1,0:T(8,128)S(1)}, f32[16,256]{1,0:T(8,128)S(1)}, u32[]{:S(2)}, u32[]{:S(2)}) %collective-permute-start.3) | collective-permute-done | bytes 16416 | tf_op jit(solution)/shard_map/ppermute | solution.py:378
  23.0 0.8 %multiply_add_fusion = (f32[16,256]{1,0:T(8,128)S(1)}, f32[16,256]{1,0:T(8,128)S(1)}, f32[16,256]{1,0:T(8,128)S(1)}) fusion(f32[16,256]{1,0:T(8,128)S(1)} %collective-permute-done.3, f32[]{:T(128)S(6)} %convert_element_type.21, pred[]{:T(512)S(6)} %ge.3, f32[32,256]{1,0:T(8,128)S(1)} %get-tuple-element.26.table_ref, f32[32,256]{1,0:T(8,128)} %collective-permute-done.2, ...), kind=kLoop, calls=%fused_computation.25 | loop fusion | flops 106496 | bytes 180248 | tf_op jit(solution)/shard_map/add | solution.py:393
  23.8 0.0 copy-start.1
  23.8 0.9 %copy-done.1 = f32[2,128,128]{2,1,0:T(8,128)S(1)} copy-done((f32[2,128,128]{2,1,0:T(8,128)S(1)}, f32[2,128,128]{2,1,0:T(8,128)}, u32[]{:S(2)}) %copy-start.1) | copy-done | bytes 131096
  24.7 3.8 %settled.1 = (bf16[1024,256]{1,0:T(8,128)(2,1)}, bf16[1024,256]{1,0:T(8,128)(2,1)}, bf16[1024,256]{1,0:T(8,128)(2,1)}, bf16[1024,256]{1,0:T(8,128)(2,1)}, bf16[1...) custom-call(bf16[1024,256]{1,0:T(8,128)(2,1)} %outer_hbm.3, bf16[1024,256]{1,0:T(8,128)(2,1)} %inner_hbm.3, ...), custom_call_target="tpu_custom_call" | custom-call | flops 8388608 | bytes 3145728 | tf_op jit(solution)/shard_map/settled/pallas_call | solution.py:379
  28.6 2.5 %last.1 = (bf16[1024,256]{1,0:T(8,128)(2,1)}, bf16[1024,256]{1,0:T(8,128)(2,1)}, bf16[1024,256]{1,0:T(8,128)(2,1)}, bf16[1024,256]{1,0:T(8,128)(2,1)}) custom-call(bf16[1024,256]{1,0:T(8,128)(2,1)S(1)} %get-tuple-element.37.gate_a, ...), custom_call_target="tpu_custom_call", output_to_operand_aliasing={{0}: (10, {}), {1}: (11, {}), {2}: (12, {}), {3}: (13, {})} | custom-call | tf_op jit(solution)/shard_map/last/pallas_call | solution.py:395
  (4 shorter events, 0.0 us)
Async XLA Ops:
  0.6 9.3 %copy-start.2 = (f32[256]{0:T(256)S(1)}, f32[256]{0:T(256)}, u32[]{:S(2)}) copy-start(f32[256]{0:T(256)} %param.13) | copy-start | bytes 3076
  5.0 0.7 %copy-start = (f32[2,128,128]{2,1,0:T(8,128)}, f32[2,128,128]{2,1,0:T(8,128)S(1)}, u32[]{:S(2)}) copy-start(f32[2,128,128]{2,1,0:T(8,128)S(1)} %get-tuple-element.25.starts_ref) | copy-start | bytes 393220
  5.7 1.3 %collective-permute-start = (f32[32,256]{1,0:T(8,128)S(1)}, f32[32,256]{1,0:T(8,128)S(1)}, u32[]{:S(2)}, u32[]{:S(2)}) collective-permute-start(f32[32,256]{1,0:T(8,128)S(1)} %get-tuple-element.27), channel_id=1, source_target_pairs={{0,1},{1,0},{2,3},{3,2},{4,5},{5,4},{6,7},{7,6},{8,9},{9,8},{10,11... | collective-permute-start | bytes 98312 | tf_op jit(solution)/shard_map/ppermute | solution.py:355
  7.0 2.9 %copy-start.4 = (f32[32,256]{1,0:T(8,128)}, f32[32,256]{1,0:T(8,128)S(1)}, u32[]{:S(2)}) copy-start(f32[32,256]{1,0:T(8,128)S(1)} %collective-permute-done) | copy-start | bytes 98308
  7.0 5.5 %copy-start.3 = (f32[32,256]{1,0:T(8,128)}, f32[32,256]{1,0:T(8,128)S(1)}, u32[]{:S(2)}) copy-start(f32[32,256]{1,0:T(8,128)S(1)} %fusion.1) | copy-start | bytes 98308
  7.0 5.5 %collective-permute-start.1 = (f32[32,256]{1,0:T(8,128)S(1)}, f32[32,256]{1,0:T(8,128)}, u32[]{:S(2)}, u32[]{:S(2)}) collective-permute-start(f32[32,256]{1,0:T(8,128)S(1)} %fusion.1), channel_id=1, source_target_pairs={{0,2},{1,3},{2,0},{3,1},{4,6},{5,7},{6,4},{7,5},{8,10},{9,11},{10,... | collective-permute-start | bytes 98312 | tf_op jit(solution)/shard_map/ppermute | solution.py:355
  11.2 1.3 %copy-start.6 = (f32[16,256]{1,0:T(8,128)S(1)}, f32[16,256]{1,0:T(8,128)}, u32[]{:S(2)}) copy-start(f32[16,256]{1,0:T(8,128)} %get-tuple-element.49) | copy-start | bytes 49156
  13.3 4.2 %collective-permute-start.2 = (f32[32,256]{1,0:T(8,128)S(1)}, f32[32,256]{1,0:T(8,128)}, u32[]{:S(2)}, u32[]{:S(2)}) collective-permute-start(f32[32,256]{1,0:T(8,128)S(1)} %fusion.4), channel_id=1, source_target_pairs={{0,4},{1,5},{2,6},{3,7},{4,0},{5,1},{6,2},{7,3},{8,12},{9,13},{10,... | collective-permute-start | bytes 98312 | tf_op jit(solution)/shard_map/ppermute | solution.py:355
  16.2 1.3 %copy-start.5 = (f32[16,256]{1,0:T(8,128)S(1)}, f32[16,256]{1,0:T(8,128)}, u32[]{:S(2)}) copy-start(f32[16,256]{1,0:T(8,128)} %get-tuple-element.47) | copy-start | bytes 49156
  18.3 4.7 %collective-permute-start.3 = (f32[16,256]{1,0:T(8,128)S(1)}, f32[16,256]{1,0:T(8,128)S(1)}, u32[]{:S(2)}, u32[]{:S(2)}) collective-permute-start(f32[16,256]{1,0:T(8,128)S(1)} %slice_select_fusion), channel_id=1, source_target_pairs={{0,8},{1,9},{2,10},{3,11},{4,12},{5,13},{6,14},{7,15},{8,0},{9,1},... | collective-permute-start | bytes 49160 | tf_op jit(solution)/shard_map/ppermute | solution.py:378
  23.8 0.9 %copy-start.1 = (f32[2,128,128]{2,1,0:T(8,128)S(1)}, f32[2,128,128]{2,1,0:T(8,128)}, u32[]{:S(2)}) copy-start(f32[2,128,128]{2,1,0:T(8,128)} %copy-done) | copy-start | bytes 393220

commit v3 on v2

--- a/solution.py
+++ b/solution.py
@@ -126,34 +126,35 @@
         own_ref[poles : 2 * poles, lanes] = back
 
 
-def local_kernel(seg_len, backward, half, signal_ref, table_ref, skip_ref, out_ref):
+def local_kernel(seg_len, backward, signal_ref, table_ref, skip_ref, out_ref):
     poles = table_ref.shape[0] // 2
     pitch = seg_len + PAD
-    lanes = lane_slice(half)
-    steps = spread_rows(jnp.exp(-table_ref[0:poles, :]), lanes, poles)
-    weights = spread_rows(table_ref[poles : 2 * poles, :], lanes, poles)
-    skip = jnp.broadcast_to(skip_ref[0:1, lanes], (SEGS, LANES))
-
-    def body(i, states):
-        row = seg_len - 1 - i if backward else i
-        x = signal_ref[half, pl.ds(row, SEGS, stride=pitch), :]
-        states = tuple(steps[k] * states[k] + x for k in range(poles))
-        terms = [weights[k] * states[k] for k in range(poles)] + [skip * x]
-        out_ref[pl.ds(row, SEGS, stride=pitch), :] = add_up(terms)
-        return states
-
-    zero = jnp.zeros((SEGS, LANES), F32)
-    lax.fori_loop(0, seg_len, body, tuple(zero for _ in range(poles)), unroll=8)
-
-
-def finish_way(seg_len, backward, gates, locals_, edge_ref, table_ref, entry_ref, targets, sems):
+    for h in range(signal_ref.shape[0]):
+        lanes = lane_slice(h)
+        steps = spread_rows(jnp.exp(-table_ref[0:poles, :]), lanes, poles)
+        weights = spread_rows(table_ref[poles : 2 * poles, :], lanes, poles)
+        skip = jnp.broadcast_to(skip_ref[0:1, lanes], (SEGS, LANES))
+
+        def body(i, states):
+            row = seg_len - 1 - i if backward else i
+            x = signal_ref[h, pl.ds(row, SEGS, stride=pitch), :]
+            states = tuple(steps[k] * states[k] + x for k in range(poles))
+            terms = [weights[k] * states[k] for k in range(poles)] + [skip * x]
+            out_ref[h, pl.ds(row, SEGS, stride=pitch), :] = add_up(terms)
+            return states
+
+        zero = jnp.zeros((SEGS, LANES), F32)
+        lax.fori_loop(0, seg_len, body, tuple(zero for _ in range(poles)), unroll=8)
+
+
+def finish_way(seg_len, backward, gates, local_ref, edge_ref, table_ref, entry_ref, targets, sems):
     poles = table_ref.shape[0] // 2
     pitch = seg_len + PAD
     inside = lax.broadcasted_iota(jnp.int32, (8, LANES), 0).astype(F32)
     reach = 8.0 - inside if backward else inside + 1.0
     blocks = seg_len // STEP
     copies = []
-    for h, local_ref in enumerate(locals_):
+    for h in range(local_ref.shape[0]):
         lanes = lane_slice(h)
         rates = spread_rows(table_ref[0:poles, :], lanes, poles)
         weights = spread_rows(table_ref[poles : 2 * poles, :], lanes, poles)
@@ -161,7 +162,7 @@
         enter = [weights[k] * jnp.exp(-rates[k] * reach) for k in range(poles)]
         entry = spread_rows(entry_ref[...], lanes, poles)
 
-        def segment(n, carried, local_ref=local_ref, lanes=lanes, h=h):
+        def segment(n, carried):
             q = SEGS - 1 - n if backward else n
 
             for i in range(blocks):
@@ -169,7 +170,7 @@
                 found = [None, None]
                 for sub in (1, 0) if backward else (0, 1):
                     row = pl.multiple_of(q * pitch + block * STEP + 8 * sub, 8)
-                    found[sub] = add_up([*carried, local_ref[pl.ds(row, 8), :]])
+                    found[sub] = add_up([*carried, local_ref[h, pl.ds(row, 8), :]])
                     carried = tuple(strides[k] * carried[k] for k in range(poles))
                 whole = jnp.concatenate(found, axis=0)
                 rows = pl.ds(pl.multiple_of(q * seg_len + block * STEP, STEP), STEP)
@@ -203,7 +204,6 @@
 
 def settled_kernel(
     seg_len,
-    count,
     blocks,
     outer_hbm,
     inner_hbm,
@@ -213,13 +213,22 @@
     starts_ref,
     table_ref,
     entry_ref,
-    *rest,
+    ahead_ref,
+    back_ref,
+    layer_hbm,
+    outer_grad_hbm,
+    inner_grad_hbm,
+    values_grad_hbm,
+    next_a,
+    next_b,
+    gate_a,
+    gate_b,
+    out_a,
+    out_b,
+    load_sems,
+    next_sems,
+    out_sems,
 ):
-    locals_ahead, locals_back = rest[:count], rest[count : 2 * count]
-    layer_hbm, outer_grad_hbm, inner_grad_hbm, values_grad_hbm, next_a, next_b = rest[
-        2 * count : 2 * count + 6
-    ]
-    gate_a, gate_b, out_a, out_b, load_sems, next_sems, out_sems = rest[2 * count + 6 :]
     later = lax.axis_index("ctx") >= blocks // 2
 
     def run(backward):
@@ -244,7 +253,7 @@
             seg_len,
             backward,
             (gate_a, gate_b),
-            locals_back if backward else locals_ahead,
+            back_ref if backward else ahead_ref,
             starts_ref if backward else ends_ref,
             table_ref,
             entry_ref,
@@ -260,7 +269,6 @@
 
 def last_kernel(
     seg_len,
-    count,
     blocks,
     gate_a,
     gate_b,
@@ -268,13 +276,20 @@
     starts_ref,
     table_ref,
     entry_ref,
-    *rest,
+    ahead_ref,
+    back_ref,
+    layer_in,
+    outer_grad_in,
+    inner_grad_in,
+    values_grad_in,
+    layer_hbm,
+    outer_grad_hbm,
+    inner_grad_hbm,
+    values_grad_hbm,
+    out_a,
+    out_b,
+    out_sems,
 ):
-    locals_ahead, locals_back = rest[:count], rest[count : 2 * count]
-    layer_hbm, outer_grad_hbm, inner_grad_hbm, values_grad_hbm = rest[
-        2 * count + 4 : 2 * count + 8
-    ]
-    out_a, out_b, out_sems = rest[2 * count + 8 :]
     later = lax.axis_index("ctx") >= blocks // 2
 
     def run(backward):
@@ -287,7 +302,7 @@
             seg_len,
             backward,
             (gate_a, gate_b),
-            locals_back if backward else locals_ahead,
+            back_ref if backward else ahead_ref,
             starts_ref if backward else ends_ref,
             table_ref,
             entry_ref,
@@ -329,34 +344,30 @@
     )(*arrays, in_hbm(decay_rate.T), in_hbm(residue.T))
     skip = skip_gain[None, :]
 
-    def local(signal, backward, half, held):
+    def local(signal, backward, held):
         signal, _ = lax.optimization_barrier((signal, held))
         return pl.pallas_call(
-            functools.partial(local_kernel, seg_len, backward, half),
-            out_shape=jax.ShapeDtypeStruct((padded, LANES), F32),
+            functools.partial(local_kernel, seg_len, backward),
+            out_shape=jax.ShapeDtypeStruct(signal.shape, F32),
             in_specs=[VMEM] * 3,
             out_specs=VMEM,
+            input_output_aliases={0: 0},
             compiler_params=limit,
             cost_estimate=pl.CostEstimate(
-                flops=work * 4 // count, bytes_accessed=padded * LANES * 8, transcendentals=0
+                flops=work * 4, bytes_accessed=signal.size * 8, transcendentals=0
             ),
             name="local",
         )(signal, table, skip)
 
     rates = table[:poles]
-    jobs = [(mixed, False, h) for h in range(count)] + [(grad, True, h) for h in range(count)]
-    middle = max(blocks.bit_length() - 3, 1)
-    share = -(-len(jobs) // middle)
+    jobs = [(mixed, False), (grad, True)]
     found = []
     ahead_entry = jnp.zeros((poles, channels), F32)
     back_entry = ahead_entry
     reach = 1
     while reach < blocks // 2:
         other = lax.ppermute(own, "ctx", [(i, i ^ reach) for i in range(blocks)])
-        pieces = []
-        if reach > 1:
-            now, jobs = jobs[:share], jobs[share:]
-            pieces = [local(*job, own) for job in now]
+        pieces = [local(*jobs.pop(0), own)] if reach > 1 and jobs else []
         later = (position // reach) % 2 == 1
         place = position % reach
         ahead_shift = jnp.exp(-rates * (rows * place).astype(F32))
@@ -368,8 +379,9 @@
         late = jnp.concatenate([jnp.ones_like(span), span])
         own = jnp.where(later, late, early) * own + jnp.where(later, early, late) * other
         reach *= 2
-        if pieces:
-            own, pieces = lax.optimization_barrier((own, pieces))
+        own, ahead_entry, back_entry, pieces = lax.optimization_barrier(
+            (own, ahead_entry, back_entry, pieces)
+        )
         found += pieces
     found += [local(*job, own) for job in jobs]
     later = position >= reach
@@ -377,9 +389,9 @@
     sent = jnp.where(later, own[poles:], own[:poles])
     other = lax.ppermute(sent, "ctx", [(i, i ^ reach) for i in range(blocks)])
     *outs, gate_a, gate_b = pl.pallas_call(
-        functools.partial(settled_kernel, seg_len, count, blocks),
+        functools.partial(settled_kernel, seg_len, blocks),
         out_shape=[gate] * 6,
-        in_specs=[HBM] * 4 + [VMEM] * (4 + 2 * count),
+        in_specs=[HBM] * 4 + [VMEM] * (6),
         out_specs=[HBM] * 4 + [VMEM] * 2,
         scratch_shapes=[pltpu.VMEM((rows, channels), BF16)] * 4
         + [dma((2,)), dma((2,)), dma((count, 2))],
@@ -391,9 +403,9 @@
     )(*arrays, ends, starts, table, jnp.where(later, back_entry, ahead_entry), *found)
     shift = jnp.exp(-rates * (rows * jnp.where(later, place, reach - 1 - place)).astype(F32))
     entry = jnp.where(later, ahead_entry, back_entry) + shift * other
-    first = 6 + 2 * count
+    first = 8
     return pl.pallas_call(
-        functools.partial(last_kernel, seg_len, count, blocks),
+        functools.partial(last_kernel, seg_len, blocks),
         out_shape=[gate] * 4,
         in_specs=[VMEM] * first + [HBM] * 4,
         out_specs=[HBM] * 4,

time: 31.4 us -> 29.1 us (0.927)
  other arithmetic: 3.04 us -> 0.12 us
  Pallas kernels: 15.7 us -> 17.4 us
  local copies, waits for them, and re-layouts: 1.57 us -> 0.01 us
  waiting for transfers between devices: 2.29 us -> 3.04 us
    pallas_call x6 -> x4, Pallas kernels: 11.4 us -> 13 us  [the longest x2 6.67 us: local(): pl.pallas_call(functools.partial(local_kernel, seg_len, backward), out_sh...]
    unnamed x14 -> x2, local copies, waits for them, and re-layouts: 1.57 us -> 0.01 us
    add x3, other arithmetic: 1.57 us -> 0.03 us  [shards(): jnp.where(later, late, early) * own + jnp.where(later, early, late) * other]
    add x1, other arithmetic: 0.84 us -> 0.01 us  [shards(): entry = jnp.where(later, ahead_entry, back_entry) + shift * other]
    ppermute x3, waiting for transfers between devices: 0.24 us -> 0.87 us  [shards(): other = lax.ppermute(own, 'ctx', [(i, i ^ reach) for i in range(blocks)])]
    exp x1 -> x0, other arithmetic: 0.62 us -> none  [shards(): span = jnp.exp(-rates * float(rows * reach))]
  transfers between devices with their start and end apart: 4 -> 4, of which waited for: 2 -> 2; matrix products, arithmetic and copies ran while one was open for 2% -> 0% of each run, Pallas kernels for 16% -> 23%
where the time goes in v3:
time: 29.1 us; the launch traced here: 29 us
  Pallas kernels  17.4 us (60%)
  starting transfers between devices  7.71 us (26%)
  waiting for transfers between devices  3.04 us (10%)
  between operations  0.74 us (3%)
    pallas_call x2, Pallas kernels, local(): pl.pallas_call(functools.partial(local_kernel, seg_len, backward), out_sh...  6.67 us
    ppermute x3, starting transfers between devices, shards(): other = lax.ppermute(own, 'ctx', [(i, i ^ reach) for i in range(blocks)])  5.06 us
    pallas_call x1, Pallas kernels, shards(): pl.pallas_call(functools.partial(state_kernel, seg_len), out_shape=[jax.S...  4.37 us
    pallas_call x1, Pallas kernels, shards(): pl.pallas_call(functools.partial(settled_kernel, seg_len, blocks), out_sh...  3.81 us
    ppermute x1, starting transfers between devices, shards(): other = lax.ppermute(sent, 'ctx', [(i, i ^ reach) for i in range(blocks)])  2.65 us
    pallas_call x1, Pallas kernels, shards(): pl.pallas_call(functools.partial(last_kernel, seg_len, blocks), out_shape...  2.5 us
    ppermute x1, waiting for transfers between devices, shards(): other = lax.ppermute(sent, 'ctx', [(i, i ^ reach) for i in range(blocks)])  2.18 us
    ppermute x3, waiting for transfers between devices, shards(): other = lax.ppermute(own, 'ctx', [(i, i ^ reach) for i in range(blocks)])  0.87 us
  transfers between devices with their start and end apart: 4, of which 2 were waited for; matrix products, arithmetic and copies ran while one was open for 0% of the time, Pallas kernels for 23%

profile of v3, /device:TPU:0, one launch (start us, length us, event | category | flops | bytes accessed | tf_op | source)
XLA Modules:
  0.0 29.0 jit_solution(6149071248211070829)
XLA Ops:
  0.6 0.0 copy-start
  0.6 4.4 %states.1 = (f32[2,1088,128]{2,1,0:T(8,128)S(1)}, f32[2,1088,128]{2,1,0:T(8,128)S(1)}, f32[2,128,128]{2,1,0:T(8,128)S(1)}, f32[2,128,128]{2,1,0:T(8,128)S(1)}, f...) custom-call(bf16[1024,256]{1,0:T(8,128)(2,1)} %outer_hbm.3, bf16[1024,256]{1,0:T(8,128)(2,1)} %inner_hbm.3, ...), custom_call_target="tpu_custom_call" | custom-call | tf_op jit(solution)/shard_map/states/pallas_call | solution.py:334
  5.0 0.5 %collective-permute-start = (f32[32,256]{1,0:T(8,128)S(1)}, f32[32,256]{1,0:T(8,128)S(1)}, u32[]{:S(2)}, u32[]{:S(2)}) collective-permute-start(f32[32,256]{1,0:T(8,128)S(1)} %get-tuple-element.32), channel_id=1, source_target_pairs={{0,1},{1,0},{2,3},{3,2},{4,5},{5,4},{6,7},{7,6},{8,9},{9,8},{10,11... | collective-permute-start | bytes 98312 | tf_op jit(solution)/shard_map/ppermute | solution.py:369
  5.5 0.9 %collective-permute-done = f32[32,256]{1,0:T(8,128)S(1)} collective-permute-done((f32[32,256]{1,0:T(8,128)S(1)}, f32[32,256]{1,0:T(8,128)S(1)}, u32[]{:S(2)}, u32[]{:S(2)}) %collective-permute-start) | collective-permute-done | bytes 32800 | tf_op jit(solution)/shard_map/ppermute | solution.py:369
  6.4 2.9 %collective-permute-start.1 = (f32[32,256]{1,0:T(8,128)S(1)}, f32[32,256]{1,0:T(8,128)S(1)}, u32[]{:S(2)}, u32[]{:S(2)}) collective-permute-start(f32[32,256]{1,0:T(8,128)S(1)} %fusion.7), channel_id=1, source_target_pairs={{0,2},{1,3},{2,0},{3,1},{4,6},{5,7},{6,4},{7,5},{8,10},{9,11},{10,... | collective-permute-start | bytes 98312 | tf_op jit(solution)/shard_map/ppermute | solution.py:369
  9.3 0.0 copy-done
  9.3 3.3 %local.2.ahead_ref = f32[2,1088,128]{2,1,0:T(8,128)S(1)} custom-call(f32[2,1088,128]{2,1,0:T(8,128)S(1)} %get-tuple-element.37.signal_ref, f32[32,256]{1,0:T(8,128)S(1)} %get-tuple-element.31.table_ref, f32[1,256]{1,0:T(1,128)S(1)} %bitcast.3), custom_call_target="tpu_custom_call", output_to_operand_aliasing={{}: (0, {})} | custom-call | flops 16777216 | bytes 2228224 | tf_op jit(solution)/shard_map/local/pallas_call | solution.py:349
  12.6 0.0 collective-permute-done.1
  12.7 1.6 %collective-permute-start.2 = (f32[32,256]{1,0:T(8,128)S(1)}, f32[32,256]{1,0:T(8,128)S(1)}, u32[]{:S(2)}, u32[]{:S(2)}) collective-permute-start(f32[32,256]{1,0:T(8,128)S(1)} %fusion.4), channel_id=1, source_target_pairs={{0,4},{1,5},{2,6},{3,7},{4,0},{5,1},{6,2},{7,3},{8,12},{9,13},{10,... | collective-permute-start | bytes 98312 | tf_op jit(solution)/shard_map/ppermute | solution.py:369
  14.4 3.4 %local.3.back_ref = f32[2,1088,128]{2,1,0:T(8,128)S(1)} custom-call(f32[2,1088,128]{2,1,0:T(8,128)S(1)} %get-tuple-element.42.signal_ref, f32[32,256]{1,0:T(8,128)S(1)} %get-tuple-element.31.table_ref, f32[1,256]{1,0:T(1,128)S(1)} %bitcast.4), custom_call_target="tpu_custom_call", output_to_operand_aliasing={{}: (0, {})} | custom-call | flops 16777216 | bytes 2228224 | tf_op jit(solution)/shard_map/local/pallas_call | solution.py:349
  17.7 0.0 collective-permute-done.2
  17.8 2.7 %collective-permute-start.3 = (f32[16,256]{1,0:T(8,128)S(1)}, f32[16,256]{1,0:T(8,128)S(1)}, u32[]{:S(2)}, u32[]{:S(2)}) collective-permute-start(f32[16,256]{1,0:T(8,128)S(1)} %slice_select_fusion), channel_id=1, source_target_pairs={{0,8},{1,9},{2,10},{3,11},{4,12},{5,13},{6,14},{7,15},{8,0},{9,1},... | collective-permute-start | bytes 49160 | tf_op jit(solution)/shard_map/ppermute | solution.py:390
  20.5 2.2 %collective-permute-done.3 = f32[16,256]{1,0:T(8,128)S(1)} collective-permute-done((f32[16,256]{1,0:T(8,128)S(1)}, f32[16,256]{1,0:T(8,128)S(1)}, u32[]{:S(2)}, u32[]{:S(2)}) %collective-permute-start.3) | collective-permute-done | bytes 16416 | tf_op jit(solution)/shard_map/ppermute | solution.py:390
  22.7 3.8 %settled.1 = (bf16[1024,256]{1,0:T(8,128)(2,1)}, bf16[1024,256]{1,0:T(8,128)(2,1)}, bf16[1024,256]{1,0:T(8,128)(2,1)}, bf16[1024,256]{1,0:T(8,128)(2,1)}, bf16[1...) custom-call(bf16[1024,256]{1,0:T(8,128)(2,1)} %outer_hbm.3, bf16[1024,256]{1,0:T(8,128)(2,1)} %inner_hbm.3, ...), custom_call_target="tpu_custom_call" | custom-call | flops 8388608 | bytes 3145728 | tf_op jit(solution)/shard_map/settled/pallas_call | solution.py:391
  26.5 2.5 %last.1 = (bf16[1024,256]{1,0:T(8,128)(2,1)}, bf16[1024,256]{1,0:T(8,128)(2,1)}, bf16[1024,256]{1,0:T(8,128)(2,1)}, bf16[1024,256]{1,0:T(8,128)(2,1)}) custom-call(bf16[1024,256]{1,0:T(8,128)(2,1)S(1)} %get-tuple-element.47.gate_a, ...), custom_call_target="tpu_custom_call", output_to_operand_aliasing={{0}: (8, {}), {1}: (9, {}), {2}: (10, {}), {3}: (11, {})} | custom-call | tf_op jit(solution)/shard_map/last/pallas_call | solution.py:407
  (8 shorter events, 0.1 us)
Async XLA Ops:
  0.6 8.7 %copy-start = (f32[256]{0:T(256)S(1)}, f32[256]{0:T(256)}, u32[]{:S(2)}) copy-start(f32[256]{0:T(256)} %param.13) | copy-start | bytes 3076
  5.0 1.4 %collective-permute-start = (f32[32,256]{1,0:T(8,128)S(1)}, f32[32,256]{1,0:T(8,128)S(1)}, u32[]{:S(2)}, u32[]{:S(2)}) collective-permute-start(f32[32,256]{1,0:T(8,128)S(1)} %get-tuple-element.32), channel_id=1, source_target_pairs={{0,1},{1,0},{2,3},{3,2},{4,5},{5,4},{6,7},{7,6},{8,9},{9,8},{10,11... | collective-permute-start | bytes 98312 | tf_op jit(solution)/shard_map/ppermute | solution.py:369
  6.4 6.2 %collective-permute-start.1 = (f32[32,256]{1,0:T(8,128)S(1)}, f32[32,256]{1,0:T(8,128)S(1)}, u32[]{:S(2)}, u32[]{:S(2)}) collective-permute-start(f32[32,256]{1,0:T(8,128)S(1)} %fusion.7), channel_id=1, source_target_pairs={{0,2},{1,3},{2,0},{3,1},{4,6},{5,7},{6,4},{7,5},{8,10},{9,11},{10,... | collective-permute-start | bytes 98312 | tf_op jit(solution)/shard_map/ppermute | solution.py:369
  12.7 5.0 %collective-permute-start.2 = (f32[32,256]{1,0:T(8,128)S(1)}, f32[32,256]{1,0:T(8,128)S(1)}, u32[]{:S(2)}, u32[]{:S(2)}) collective-permute-start(f32[32,256]{1,0:T(8,128)S(1)} %fusion.4), channel_id=1, source_target_pairs={{0,4},{1,5},{2,6},{3,7},{4,0},{5,1},{6,2},{7,3},{8,12},{9,13},{10,... | collective-permute-start | bytes 98312 | tf_op jit(solution)/shard_map/ppermute | solution.py:369
  17.8 4.8 %collective-permute-start.3 = (f32[16,256]{1,0:T(8,128)S(1)}, f32[16,256]{1,0:T(8,128)S(1)}, u32[]{:S(2)}, u32[]{:S(2)}) collective-permute-start(f32[16,256]{1,0:T(8,128)S(1)} %slice_select_fusion), channel_id=1, source_target_pairs={{0,8},{1,9},{2,10},{3,11},{4,12},{5,13},{6,14},{7,15},{8,0},{9,1},... | collective-permute-start | bytes 49160 | tf_op jit(solution)/shard_map/ppermute | solution.py:390

commit v4 on v3

--- a/solution.py
+++ b/solution.py
@@ -387,6 +387,12 @@
     later = position >= reach
     place = position % reach
     sent = jnp.where(later, own[poles:], own[:poles])
+    settled_entry = jnp.where(later, back_entry, ahead_entry)
+    open_entry = jnp.where(later, ahead_entry, back_entry)
+    shift = jnp.exp(-rates * (rows * jnp.where(later, place, reach - 1 - place)).astype(F32))
+    sent, settled_entry, open_entry, shift = lax.optimization_barrier(
+        (sent, settled_entry, open_entry, shift)
+    )
     other = lax.ppermute(sent, "ctx", [(i, i ^ reach) for i in range(blocks)])
     *outs, gate_a, gate_b = pl.pallas_call(
         functools.partial(settled_kernel, seg_len, blocks),
@@ -400,9 +406,8 @@
             flops=work * 2, bytes_accessed=rows * channels * 12, transcendentals=0
         ),
         name="settled",
-    )(*arrays, ends, starts, table, jnp.where(later, back_entry, ahead_entry), *found)
-    shift = jnp.exp(-rates * (rows * jnp.where(later, place, reach - 1 - place)).astype(F32))
-    entry = jnp.where(later, ahead_entry, back_entry) + shift * other
+    )(*arrays, ends, starts, table, settled_entry, *found)
+    entry = open_entry + shift * other
     first = 8
     return pl.pallas_call(
         functools.partial(last_kernel, seg_len, blocks),

time: 29.1 us -> 27 us (0.928)
  waiting for transfers between devices: 3.04 us -> 0.87 us
    ppermute x1, waiting for transfers between devices: 2.18 us -> 0.01 us  [shards(): other = lax.ppermute(sent, 'ctx', [(i, i ^ reach) for i in range(blocks)])]
  transfers between devices with their start and end apart: 4 -> 4, of which waited for: 2 -> 1; matrix products, arithmetic and copies ran while one was open for 0% -> 0% of each run, Pallas kernels for 23% -> 39%
where the time goes in v4:
time: 27 us; the launch traced here: 26.8 us
  Pallas kernels  17.4 us (64%)
  starting transfers between devices  7.71 us (29%)
  waiting for transfers between devices  0.87 us (3%)
  between operations  0.75 us (3%)
    pallas_call x2, Pallas kernels, local(): pl.pallas_call(functools.partial(local_kernel, seg_len, backward), out_sh...  6.67 us
    ppermute x3, starting transfers between devices, shards(): other = lax.ppermute(own, 'ctx', [(i, i ^ reach) for i in range(blocks)])  5.06 us
    pallas_call x1, Pallas kernels, shards(): pl.pallas_call(functools.partial(state_kernel, seg_len), out_shape=[jax.S...  4.37 us
    pallas_call x1, Pallas kernels, shards(): pl.pallas_call(functools.partial(settled_kernel, seg_len, blocks), out_sh...  3.79 us
    ppermute x1, starting transfers between devices, shards(): other = lax.ppermute(sent, 'ctx', [(i, i ^ reach) for i in range(blocks)])  2.65 us
    pallas_call x1, Pallas kernels, shards(): pl.pallas_call(functools.partial(last_kernel, seg_len, blocks), out_shape...  2.52 us
    ppermute x3, waiting for transfers between devices, shards(): other = lax.ppermute(own, 'ctx', [(i, i ^ reach) for i in range(blocks)])  0.87 us
  transfers between devices with their start and end apart: 4, of which 1 were waited for; matrix products, arithmetic and copies ran while one was open for 0% of the time, Pallas kernels for 39%

profile of v4, /device:TPU:0, one launch (start us, length us, event | category | flops | bytes accessed | tf_op | source)
XLA Modules:
  0.0 26.8 jit_solution(12218795416667975763)
XLA Ops:
  0.6 0.0 copy-start
  0.6 4.4 %states.1 = (f32[2,1088,128]{2,1,0:T(8,128)S(1)}, f32[2,1088,128]{2,1,0:T(8,128)S(1)}, f32[2,128,128]{2,1,0:T(8,128)S(1)}, f32[2,128,128]{2,1,0:T(8,128)S(1)}, f...) custom-call(bf16[1024,256]{1,0:T(8,128)(2,1)} %outer_hbm.3, bf16[1024,256]{1,0:T(8,128)(2,1)} %inner_hbm.3, ...), custom_call_target="tpu_custom_call" | custom-call | tf_op jit(solution)/shard_map/states/pallas_call | solution.py:334
  5.0 0.5 %collective-permute-start = (f32[32,256]{1,0:T(8,128)S(1)}, f32[32,256]{1,0:T(8,128)S(1)}, u32[]{:S(2)}, u32[]{:S(2)}) collective-permute-start(f32[32,256]{1,0:T(8,128)S(1)} %get-tuple-element.36), channel_id=1, source_target_pairs={{0,1},{1,0},{2,3},{3,2},{4,5},{5,4},{6,7},{7,6},{8,9},{9,8},{10,11... | collective-permute-start | bytes 98312 | tf_op jit(solution)/shard_map/ppermute | solution.py:369
  5.5 0.9 %collective-permute-done = f32[32,256]{1,0:T(8,128)S(1)} collective-permute-done((f32[32,256]{1,0:T(8,128)S(1)}, f32[32,256]{1,0:T(8,128)S(1)}, u32[]{:S(2)}, u32[]{:S(2)}) %collective-permute-start) | collective-permute-done | bytes 32800 | tf_op jit(solution)/shard_map/ppermute | solution.py:369
  6.4 2.9 %collective-permute-start.1 = (f32[32,256]{1,0:T(8,128)S(1)}, f32[32,256]{1,0:T(8,128)S(1)}, u32[]{:S(2)}, u32[]{:S(2)}) collective-permute-start(f32[32,256]{1,0:T(8,128)S(1)} %fusion.7), channel_id=1, source_target_pairs={{0,2},{1,3},{2,0},{3,1},{4,6},{5,7},{6,4},{7,5},{8,10},{9,11},{10,... | collective-permute-start | bytes 98312 | tf_op jit(solution)/shard_map/ppermute | solution.py:369
  9.3 0.0 copy-done
  9.3 3.3 %local.2.ahead_ref = f32[2,1088,128]{2,1,0:T(8,128)S(1)} custom-call(f32[2,1088,128]{2,1,0:T(8,128)S(1)} %get-tuple-element.41.signal_ref, f32[32,256]{1,0:T(8,128)S(1)} %get-tuple-element.35.table_ref, f32[1,256]{1,0:T(1,128)S(1)} %bitcast.3), custom_call_target="tpu_custom_call", output_to_operand_aliasing={{}: (0, {})} | custom-call | flops 16777216 | bytes 2228224 | tf_op jit(solution)/shard_map/local/pallas_call | solution.py:349
  12.7 0.0 collective-permute-done.1
  12.7 1.6 %collective-permute-start.2 = (f32[32,256]{1,0:T(8,128)S(1)}, f32[32,256]{1,0:T(8,128)S(1)}, u32[]{:S(2)}, u32[]{:S(2)}) collective-permute-start(f32[32,256]{1,0:T(8,128)S(1)} %fusion.4), channel_id=1, source_target_pairs={{0,4},{1,5},{2,6},{3,7},{4,0},{5,1},{6,2},{7,3},{8,12},{9,13},{10,... | collective-permute-start | bytes 98312 | tf_op jit(solution)/shard_map/ppermute | solution.py:369
  14.4 3.4 %local.3.back_ref = f32[2,1088,128]{2,1,0:T(8,128)S(1)} custom-call(f32[2,1088,128]{2,1,0:T(8,128)S(1)} %get-tuple-element.46.signal_ref, f32[32,256]{1,0:T(8,128)S(1)} %get-tuple-element.35.table_ref, f32[1,256]{1,0:T(1,128)S(1)} %bitcast.4), custom_call_target="tpu_custom_call", output_to_operand_aliasing={{}: (0, {})} | custom-call | flops 16777216 | bytes 2228224 | tf_op jit(solution)/shard_map/local/pallas_call | solution.py:349
  17.7 0.0 collective-permute-done.2
  17.8 2.7 %collective-permute-start.3 = (f32[16,256]{1,0:T(8,128)S(1)}, f32[16,256]{1,0:T(8,128)S(1)}, u32[]{:S(2)}, u32[]{:S(2)}) collective-permute-start(f32[16,256]{1,0:T(8,128)S(1)} %get-tuple-element.57), channel_id=1, source_target_pairs={{0,8},{1,9},{2,10},{3,11},{4,12},{5,13},{6,14},{7,15},{8,0},{9,1},... | collective-permute-start | bytes 49160 | tf_op jit(solution)/shard_map/ppermute | solution.py:396
  20.5 3.8 %settled.1 = (bf16[1024,256]{1,0:T(8,128)(2,1)}, bf16[1024,256]{1,0:T(8,128)(2,1)}, bf16[1024,256]{1,0:T(8,128)(2,1)}, bf16[1024,256]{1,0:T(8,128)(2,1)}, bf16[1...) custom-call(bf16[1024,256]{1,0:T(8,128)(2,1)} %outer_hbm.3, bf16[1024,256]{1,0:T(8,128)(2,1)} %inner_hbm.3, ...), custom_call_target="tpu_custom_call" | custom-call | flops 8388608 | bytes 3145728 | tf_op jit(solution)/shard_map/settled/pallas_call | solution.py:397
  24.3 0.0 collective-permute-done.3
  24.3 2.5 %last.1 = (bf16[1024,256]{1,0:T(8,128)(2,1)}, bf16[1024,256]{1,0:T(8,128)(2,1)}, bf16[1024,256]{1,0:T(8,128)(2,1)}, bf16[1024,256]{1,0:T(8,128)(2,1)}) custom-call(bf16[1024,256]{1,0:T(8,128)(2,1)S(1)} %get-tuple-element.53.gate_a, ...), custom_call_target="tpu_custom_call", output_to_operand_aliasing={{0}: (8, {}), {1}: (9, {}), {2}: (10, {}), {3}: (11, {})} | custom-call | tf_op jit(solution)/shard_map/last/pallas_call | solution.py:412
  (8 shorter events, 0.1 us)
Async XLA Ops:
  0.6 8.7 %copy-start = (f32[256]{0:T(256)S(1)}, f32[256]{0:T(256)}, u32[]{:S(2)}) copy-start(f32[256]{0:T(256)} %param.13) | copy-start | bytes 3076
  5.0 1.4 %collective-permute-start = (f32[32,256]{1,0:T(8,128)S(1)}, f32[32,256]{1,0:T(8,128)S(1)}, u32[]{:S(2)}, u32[]{:S(2)}) collective-permute-start(f32[32,256]{1,0:T(8,128)S(1)} %get-tuple-element.36), channel_id=1, source_target_pairs={{0,1},{1,0},{2,3},{3,2},{4,5},{5,4},{6,7},{7,6},{8,9},{9,8},{10,11... | collective-permute-start | bytes 98312 | tf_op jit(solution)/shard_map/ppermute | solution.py:369
  6.4 6.2 %collective-permute-start.1 = (f32[32,256]{1,0:T(8,128)S(1)}, f32[32,256]{1,0:T(8,128)S(1)}, u32[]{:S(2)}, u32[]{:S(2)}) collective-permute-start(f32[32,256]{1,0:T(8,128)S(1)} %fusion.7), channel_id=1, source_target_pairs={{0,2},{1,3},{2,0},{3,1},{4,6},{5,7},{6,4},{7,5},{8,10},{9,11},{10,... | collective-permute-start | bytes 98312 | tf_op jit(solution)/shard_map/ppermute | solution.py:369
  12.7 5.0 %collective-permute-start.2 = (f32[32,256]{1,0:T(8,128)S(1)}, f32[32,256]{1,0:T(8,128)S(1)}, u32[]{:S(2)}, u32[]{:S(2)}) collective-permute-start(f32[32,256]{1,0:T(8,128)S(1)} %fusion.4), channel_id=1, source_target_pairs={{0,4},{1,5},{2,6},{3,7},{4,0},{5,1},{6,2},{7,3},{8,12},{9,13},{10,... | collective-permute-start | bytes 98312 | tf_op jit(solution)/shard_map/ppermute | solution.py:369
  17.8 6.5 %collective-permute-start.3 = (f32[16,256]{1,0:T(8,128)S(1)}, f32[16,256]{1,0:T(8,128)S(1)}, u32[]{:S(2)}, u32[]{:S(2)}) collective-permute-start(f32[16,256]{1,0:T(8,128)S(1)} %get-tuple-element.57), channel_id=1, source_target_pairs={{0,8},{1,9},{2,10},{3,11},{4,12},{5,13},{6,14},{7,15},{8,0},{9,1},... | collective-permute-start | bytes 49160 | tf_op jit(solution)/shard_map/ppermute | solution.py:396

commit v5 on v3

v5 whole, which is shorter than its diff:
```python
import functools
import jax
import jax.numpy as jnp
from jax import lax
from jax.experimental import pallas as pl
from jax.experimental.pallas import tpu as pltpu
from jax.sharding import PartitionSpec as P

SEGS = 8
LANES = 128
PAD = 8
STEP = 16
CHUNK = 16
F32 = jnp.float32
BF16 = jnp.bfloat16
VMEM = pl.BlockSpec(memory_space=pltpu.VMEM)
HBM = pl.BlockSpec(memory_space=pltpu.HBM)


def lane_slice(half):
    return slice(half * LANES, (half + 1) * LANES)


def add_up(terms):
    while len(terms) > 1:
        odd = [terms[-1]] if len(terms) % 2 else []
        terms = [a + b for a, b in zip(terms[::2], terms[1::2])] + odd
    return terms[0]


def spread_rows(table, lanes, count):
    return [jnp.broadcast_to(table[k : k + 1, lanes], (8, LANES)) for k in range(count)]


def factor_tables(rates, rows, blocks, factor_ref):
    poles, channels = rates.shape
    me = lax.axis_index("ctx")
    one = jnp.ones((poles, channels), F32)
    zero = jnp.zeros((poles, channels), F32)
    base = 0
    for bit in range(blocks.bit_length() - 1):
        reach = 1 << bit
        later = jnp.bitwise_and(jnp.right_shift(me, bit), 1) == 1
        place = jnp.bitwise_and(me, reach - 1)
        gap = jnp.where(later, place, reach - 1 - place).astype(F32)
        shift = jnp.exp(-rates * (float(rows) * gap))
        if 2 * reach < blocks:
            span = jnp.exp(-float(rows * reach) * rates)
            first, second = jnp.where(later, one, span), jnp.where(later, span, one)
            parts = (first, second, second, first)
            parts += (jnp.where(later, shift, zero), jnp.where(later, zero, shift))
        else:
            parts = (shift, jnp.where(later, one, zero))
        for part in parts:
            factor_ref[base : base + poles, :] = part
            base += poles


def state_kernel(
    seg_len,
    blocks,
    outer_hbm,
    inner_hbm,
    values_hbm,
    cotangent_hbm,
    rate_hbm,
    residue_hbm,
    mixed_ref,
    grad_ref,
    gain_ref,
    loss_ref,
    ends_ref,
    starts_ref,
    own_ref,
    table_ref,
    factor_ref,
    outer_ref,
    inner_ref,
    values_ref,
    cotangent_ref,
    copy_sems,
    table_sems,
):
    poles = rate_hbm.shape[0]
    pitch = seg_len + PAD
    count = mixed_ref.shape[0]
    chunks = seg_len // CHUNK
    tables = [
        pltpu.make_async_copy(
            source, table_ref.at[pl.ds(j * poles, poles), :], table_sems.at[j]
        )
        for j, source in enumerate((rate_hbm, residue_hbm))
    ]
    for copy in tables:
        copy.start()
    pairs = (
        (inner_hbm, inner_ref),
        (values_hbm, values_ref),
        (outer_hbm, outer_ref),
        (cotangent_hbm, cotangent_ref),
    )
    copies = []
    for h in range(count):
        line = []
        for j, (source, target) in enumerate(pairs):
            copy = pltpu.make_async_copy(
                source.at[:, lane_slice(h)], target.at[:, lane_slice(h)], copy_sems.at[h, j]
            )
            copy.start()
            line.append(copy)
        copies.append(line)
    for copy in tables:
        copy.wait()
    rate_table = table_ref[0:poles, :]
    decay = jnp.exp(-rate_table)
    chunk_decay = jnp.exp(-float(CHUNK) * rate_table)
    seg_decay = jnp.exp(-float(seg_len) * rate_table)
    factor_tables(rate_table, seg_len * SEGS, blocks, factor_ref)
    for h in range(count):
        lanes = lane_slice(h)
        for copy in copies[h]:
            copy.wait()

        def convert(q, _):
            source = pl.ds(pl.multiple_of(q * seg_len, 16), seg_len)
            target = pl.ds(pl.multiple_of(q * pitch, 8), seg_len)
            mixed = inner_ref[source, lanes].astype(F32) * values_ref[source, lanes].astype(F32)
            mixed_ref[h, target, :] = mixed.astype(BF16).astype(F32)
            outer, cotangent = outer_ref[source, lanes], cotangent_ref[source, lanes]
            grad_ref[h, target, :] = outer.astype(F32) * cotangent.astype(F32)
            return _

        lax.fori_loop(0, SEGS, convert, 0)
        steps = spread_rows(decay, lanes, poles)

        def body(m, _):
            base = m * CHUNK
            for j in range(CHUNK):
                x = mixed_ref[h, pl.ds(base + j, SEGS, stride=pitch), :]
                g = grad_ref[h, pl.ds(base + CHUNK - 1 - j, SEGS, stride=pitch), :]
                if j:
                    ahead = [steps[k] * ahead[k] + x for k in range(poles)]
                    back = [steps[k] * back[k] + g for k in range(poles)]
                else:
                    ahead, back = [x] * poles, [g] * poles
            for k in range(poles):
                rows = pl.ds(pl.multiple_of((m * poles + k) * SEGS, SEGS), SEGS)
                gain_ref[h, rows, :] = ahead[k]
                loss_ref[h, rows, :] = back[k]
            return _

        lax.fori_loop(0, chunks, body, 0)
        longer = spread_rows(chunk_decay, lanes, poles)
        for k in range(poles):
            ahead = gain_ref[h, SEGS * k : SEGS * (k + 1), :]
            last = ((chunks - 1) * poles + k) * SEGS
            back = loss_ref[h, last : last + SEGS, :]
            for m in range(1, chunks):
                row = (m * poles + k) * SEGS
                ahead = longer[k] * ahead + gain_ref[h, row : row + SEGS, :]
                row = ((chunks - 1 - m) * poles + k) * SEGS
                back = longer[k] * back + loss_ref[h, row : row + SEGS, :]
            ends_ref[h, SEGS * k : SEGS * (k + 1), :] = ahead
            starts_ref[h, SEGS * k : SEGS * (k + 1), :] = back
        ahead = jnp.zeros((poles, LANES), F32)
        back = jnp.zeros((poles, LANES), F32)
        for q in range(SEGS):
            ahead = seg_decay[:, lanes] * ahead + ends_ref[h, pl.ds(q, poles, stride=SEGS), :]
            back = seg_decay[:, lanes] * back + starts_ref[
                h, pl.ds(SEGS - 1 - q, poles, stride=SEGS), :
            ]
        own_ref[0:poles, lanes] = ahead
        own_ref[poles : 2 * poles, lanes] = back


def local_kernel(seg_len, backward, signal_ref, table_ref, skip_ref, out_ref):
    poles = table_ref.shape[0] // 2
    pitch = seg_len + PAD
    chunks = seg_len // CHUNK
    weight = table_ref[poles : 2 * poles, :]
    decay = jnp.exp(-table_ref[0:poles, :])
    rows = []
    for lag in range(CHUNK):
        rows.append(jnp.sum(weight, axis=0, keepdims=True))
        weight = weight * decay
    rows[0] = rows[0] + skip_ref[...]
    for h in range(signal_ref.shape[0]):
        lanes = lane_slice(h)
        taps = [jnp.broadcast_to(row[:, lanes], (SEGS, LANES)) for row in rows]

        def fetch(m):
            return tuple(
                signal_ref[h, pl.ds(m * CHUNK + j, SEGS, stride=pitch), :] for j in range(CHUNK)
            )

        def body(m, held):
            following = fetch(jnp.minimum(m + 1, chunks - 1))
            for j in range(CHUNK):
                lags = range(CHUNK - j) if backward else range(j + 1)
                terms = [taps[lag] * held[j + lag if backward else j - lag] for lag in lags]
                out_ref[h, pl.ds(m * CHUNK + j, SEGS, stride=pitch), :] = add_up(terms)
            return following

        lax.fori_loop(0, chunks, body, fetch(0))


def finish_way(
    seg_len,
    backward,
    gates,
    local_ref,
    chunk_ref,
    edge_ref,
    table_ref,
    entry_ref,
    targets,
    state_ref,
    total_ref,
    sems,
):
    poles = table_ref.shape[0] // 2
    pitch = seg_len + PAD
    chunks = seg_len // CHUNK
    rates = table_ref[0:poles, :]
    decay = jnp.exp(-rates)
    seg_decay = jnp.exp(-float(seg_len) * rates)
    loads = [copy for copy, _ in gates]
    gate_refs = [ref for _, ref in gates]
    copies = []
    for h in range(local_ref.shape[0]):
        lanes = lane_slice(h)
        state = entry_ref[:, lanes]
        for n in range(SEGS):
            q = SEGS - 1 - n if backward else n
            state_ref[pl.ds(q, poles, stride=SEGS), :] = state
            if n < SEGS - 1:
                edge = edge_ref[h, pl.ds(q, poles, stride=SEGS), :]
                state = seg_decay[:, lanes] * state + edge
        steps = spread_rows(decay, lanes, poles)
        weights = spread_rows(table_ref[poles : 2 * poles, :], lanes, poles)
        carried = tuple(
            weights[k] * state_ref[SEGS * k : SEGS * (k + 1), :] for k in range(poles)
        )

        def body(n, carried):
            m = chunks - 1 - n if backward else n
            for i in range(CHUNK):
                row = pl.ds(m * CHUNK + (CHUNK - 1 - i if backward else i), SEGS, stride=pitch)
                carried = [steps[k] * carried[k] for k in range(poles)]
                total_ref[row, :] = add_up([*carried, local_ref[h, row, :]])
            return tuple(
                carried[k]
                + weights[k]
                * chunk_ref[h, pl.ds(pl.multiple_of((m * poles + k) * SEGS, SEGS), SEGS), :]
                for k in range(poles)
            )

        lax.fori_loop(0, chunks, body, carried)
        for copy in loads:
            copy.wait()
        loads = []

        def gate(q, _):
            whole = total_ref[pl.ds(pl.multiple_of(q * pitch, 8), seg_len), :]
            rows = pl.ds(pl.multiple_of(q * seg_len, STEP), seg_len)
            for gate_ref, (target, _hbm) in zip(gate_refs, targets):
                target[rows, lanes] = (gate_ref[rows, lanes].astype(F32) * whole).astype(BF16)
            return _

        lax.fori_loop(0, SEGS, gate, 0)
        for j, (target, hbm) in enumerate(targets):
            copy = pltpu.make_async_copy(target.at[:, lanes], hbm.at[:, lanes], sems.at[h, j])
            copy.start()
            copies.append(copy)
    for copy in copies:
        copy.wait()


def finish_kernel(
    seg_len,
    blocks,
    settled,
    outer_hbm,
    inner_hbm,
    values_hbm,
    cotangent_hbm,
    ahead_ref,
    back_ref,
    gain_ref,
    loss_ref,
    ends_ref,
    starts_ref,
    table_ref,
    entry_ref,
    *rest,
):
    outs, (gate_a, gate_b, out_a, out_b, state_ref, total_ref, load_sems, out_sems) = (
        rest[-12:-8],
        rest[-8:],
    )
    layer_hbm, outer_grad_hbm, inner_grad_hbm, values_grad_hbm = outs
    later = lax.axis_index("ctx") >= blocks // 2

    def run(backward):
        if backward:
            sources = (values_hbm, inner_hbm)
            targets = ((out_a, inner_grad_hbm), (out_b, values_grad_hbm))
            parts = (back_ref, loss_ref, starts_ref)
        else:
            sources = (outer_hbm, cotangent_hbm)
            targets = ((out_a, layer_hbm), (out_b, outer_grad_hbm))
            parts = (ahead_ref, gain_ref, ends_ref)
        gates = []
        for j, (source, target) in enumerate(zip(sources, (gate_a, gate_b))):
            copy = pltpu.make_async_copy(source, target, load_sems.at[j])
            copy.start()
            gates.append((copy, target))
        finish_way(
            seg_len,
            backward,
            gates,
            *parts,
            table_ref,
            entry_ref,
            targets,
            state_ref,
            total_ref,
            out_sems,
        )

    pl.when(later)(functools.partial(run, settled))
    pl.when(jnp.logical_not(later))(functools.partial(run, not settled))


def shards(outer_gate, inner_gate, values, cotangent, residue, decay_rate, skip_gain):
    rows, channels = values.shape
    poles = residue.shape[1]
    seg_len = rows // SEGS
    padded = SEGS * (seg_len + PAD)
    count = channels // LANES
    blocks = lax.axis_size("ctx")
    levels = blocks.bit_length() - 1
    gate = jax.ShapeDtypeStruct((rows, channels), BF16)
    limit = pltpu.CompilerParams(vmem_limit_bytes=4 << 20)
    work = rows * channels * poles
    dma = pltpu.SemaphoreType.DMA

    def in_hbm(x):
        return pltpu.with_memory_space_constraint(x, pltpu.HBM)

    arrays = [in_hbm(x) for x in (outer_gate, inner_gate, values, cotangent)]
    mixed, grad, gain, loss, ends, starts, own, table, factors = pl.pallas_call(
        functools.partial(state_kernel, seg_len, blocks),
        out_shape=[jax.ShapeDtypeStruct((count, padded, LANES), F32)] * 2
        + [jax.ShapeDtypeStruct((count, rows // CHUNK * poles, LANES), F32)] * 2
        + [jax.ShapeDtypeStruct((count, SEGS * poles, LANES), F32)] * 2
        + [jax.ShapeDtypeStruct((2 * poles, channels), F32)] * 2
        + [jax.ShapeDtypeStruct(((6 * levels - 4) * poles, channels), F32)],
        in_specs=[HBM] * 6,
        out_specs=[VMEM] * 9,
        scratch_shapes=[pltpu.VMEM((rows, channels), BF16)] * 4 + [dma((count, 4)), dma((2,))],
        compiler_params=limit,
        name="states",
    )(*arrays, in_hbm(decay_rate.T), in_hbm(residue.T))
    skip = skip_gain[None, :]

    def local(signal, backward, held):
        signal, _ = lax.optimization_barrier((signal, held))
        return pl.pallas_call(
            functools.partial(local_kernel, seg_len, backward),
            out_shape=jax.ShapeDtypeStruct(signal.shape, F32),
            in_specs=[VMEM] * 3,
            out_specs=VMEM,
            input_output_aliases={0: 0},
            compiler_params=limit,
            cost_estimate=pl.CostEstimate(
                flops=rows * channels * 17, bytes_accessed=signal.size * 8, transcendentals=0
            ),
            name="local",
        )(signal, table, skip)

    jobs = [(mixed, False), (grad, True)]
    found = []
    entry = jnp.zeros_like(own)
    for bit in range(levels - 1):
        reach = 1 << bit
        other = lax.ppermute(own, "ctx", [(i, i ^ reach) for i in range(blocks)])
        pieces = [local(*jobs.pop(0), own)] if bit and jobs else []
        keep, take, join = factors[6 * bit * poles : 6 * (bit + 1) * poles].reshape(
            3, 2 * poles, channels
        )
        entry = entry + join * other
        own = keep * own + take * other
        own, entry, pieces = lax.optimization_barrier((own, entry, pieces))
        found += pieces
    found += [local(*job, own) for job in jobs]
    shift, late = factors[6 * (levels - 1) * poles :].reshape(2, poles, channels)

    def choose(when_later, otherwise):
        return late * when_later + (1.0 - late) * otherwise

    ahead, back = own[:poles], own[poles:]
    ahead_entry, back_entry = entry[:poles], entry[poles:]
    sent, settled_entry, open_entry = lax.optimization_barrier(
        (
            choose(back, ahead),
            choose(back_entry, ahead_entry),
            choose(ahead_entry, back_entry),
        )
    )
    other = lax.ppermute(sent, "ctx", [(i, i ^ (blocks // 2)) for i in range(blocks)])

    def finish(settled, entry, before):
        first = 12
        return pl.pallas_call(
            functools.partial(finish_kernel, seg_len, blocks, settled),
            out_shape=[gate] * 4,
            in_specs=[HBM] * 4 + [VMEM] * 8 + [HBM] * len(before),
            out_specs=[HBM] * 4,
            input_output_aliases={first + j: j for j in range(len(before))},
            scratch_shapes=[pltpu.VMEM((rows, channels), BF16)] * 4
            + [pltpu.VMEM((SEGS * poles, LANES), F32), pltpu.VMEM((padded, LANES), F32)]
            + [dma((2,)), dma((count, 2))],
            compiler_params=limit,
            cost_estimate=pl.CostEstimate(
                flops=work * 2, bytes_accessed=rows * channels * 12, transcendentals=0
            ),
            name="settled" if settled else "last",
        )(*arrays, *found, gain, loss, ends, starts, table, entry, *before)

    outs = finish(True, settled_entry, ())
    return finish(False, open_entry + shift * other, outs)


def solution(mesh):
    spread = P(("groups", "ctx"), None)
    return jax.shard_map(
        shards,
        mesh=mesh,
        in_specs=(spread,) * 4 + (P(),) * 3,
        out_specs=(spread,) * 4,
        check_vma=False,
    )
```

time: 29.1 us -> 24.5 us (0.84)
  Pallas kernels: 17.4 us -> 11.9 us
  starting transfers between devices: 7.71 us -> 8.69 us
    pallas_call x2, Pallas kernels: 6.67 us -> 1.67 us  [local(): pl.pallas_call(functools.partial(local_kernel, seg_len, backward), out_sh...]
    ppermute x1, waiting for transfers between devices: 2.18 us -> 0.01 us  [shards(): lax.ppermute(sent, 'ctx', [(i, i ^ blocks // 2) for i in range(blocks)])]
    ppermute x3, waiting for transfers between devices: 0.87 us -> 2.96 us  [shards(): other = lax.ppermute(own, 'ctx', [(i, i ^ reach) for i in range(blocks)])]
    ppermute x3, starting transfers between devices: 5.06 us -> 5.59 us  [shards(): other = lax.ppermute(own, 'ctx', [(i, i ^ reach) for i in range(blocks)])]
    pallas_call x3, Pallas kernels: 10.7 us -> 10.2 us  [the longest x2 5.93 us: finish(): pl.pallas_call(functools.partial(finish_kernel, seg_len, blocks, settled)...]
    ppermute x1, starting transfers between devices: 2.65 us -> 3.1 us  [shards(): lax.ppermute(sent, 'ctx', [(i, i ^ blocks // 2) for i in range(blocks)])]
  transfers between devices with their start and end apart: 4 -> 4, of which waited for: 2 -> 3; matrix products, arithmetic and copies ran while one was open for 0% -> 0% of each run, Pallas kernels for 23% -> 19%
where the time goes in v5:
time: 24.5 us; the launch traced here: 24.3 us
  Pallas kernels  11.9 us (49%)
  starting transfers between devices  8.69 us (35%)
  waiting for transfers between devices  2.97 us (12%)
  between operations  0.7 us (3%)
    pallas_call x2, Pallas kernels, finish(): pl.pallas_call(functools.partial(finish_kernel, seg_len, blocks, settled)...  5.93 us
    ppermute x3, starting transfers between devices, shards(): other = lax.ppermute(own, 'ctx', [(i, i ^ reach) for i in range(blocks)])  5.59 us
    pallas_call x1, Pallas kernels, shards(): pl.pallas_call(functools.partial(state_kernel, seg_len, blocks), out_shap...  4.31 us
    ppermute x1, starting transfers between devices, shards(): lax.ppermute(sent, 'ctx', [(i, i ^ blocks // 2) for i in range(blocks)])  3.1 us
    ppermute x3, waiting for transfers between devices, shards(): other = lax.ppermute(own, 'ctx', [(i, i ^ reach) for i in range(blocks)])  2.96 us
    pallas_call x2, Pallas kernels, local(): pl.pallas_call(functools.partial(local_kernel, seg_len, backward), out_sh...  1.67 us
  transfers between devices with their start and end apart: 4, of which 3 were waited for; matrix products, arithmetic and copies ran while one was open for 0% of the time, Pallas kernels for 19%

profile of v5, /device:TPU:0, one launch (start us, length us, event | category | flops | bytes accessed | tf_op | source)
XLA Modules:
  0.0 24.3 jit_solution(3954325626599496659)
XLA Ops:
  0.6 0.0 copy-start
  0.6 4.3 %states.1 = (f32[2,1088,128]{2,1,0:T(8,128)S(1)}, f32[2,1088,128]{2,1,0:T(8,128)S(1)}, f32[2,1024,128]{2,1,0:T(8,128)S(1)}, f32[2,1024,128]{2,1,0:T(8,128)S(1)},...) custom-call(bf16[1024,256]{1,0:T(8,128)(2,1)} %outer_hbm.5, ...), custom_call_target="tpu_custom_call" | custom-call | tf_op jit(solution)/shard_map/states/pallas_call | solution.py:352
  5.0 0.5 %collective-permute-start = (f32[32,256]{1,0:T(8,128)S(1)}, f32[32,256]{1,0:T(8,128)S(1)}, u32[]{:S(2)}, u32[]{:S(2)}) collective-permute-start(f32[32,256]{1,0:T(8,128)S(1)} %get-tuple-element.31), channel_id=1, source_target_pairs={{0,1},{1,0},{2,3},{3,2},{4,5},{5,4},{6,7},{7,6},{8,9},{9,8},{10,11... | collective-permute-start | bytes 98312 | tf_op jit(solution)/shard_map/ppermute | solution.py:387
  5.5 0.9 %collective-permute-done = f32[32,256]{1,0:T(8,128)S(1)} collective-permute-done((f32[32,256]{1,0:T(8,128)S(1)}, f32[32,256]{1,0:T(8,128)S(1)}, u32[]{:S(2)}, u32[]{:S(2)}) %collective-permute-start) | collective-permute-done | bytes 32800 | tf_op jit(solution)/shard_map/ppermute | solution.py:387
  6.3 2.9 %collective-permute-start.1 = (f32[32,256]{1,0:T(8,128)S(1)}, f32[32,256]{1,0:T(8,128)S(1)}, u32[]{:S(2)}, u32[]{:S(2)}) collective-permute-start(f32[32,256]{1,0:T(8,128)S(1)} %get-tuple-element.32), channel_id=1, source_target_pairs={{0,2},{1,3},{2,0},{3,1},{4,6},{5,7},{6,4},{7,5},{8,10},{9,11},{10,... | collective-permute-start | bytes 98312 | tf_op jit(solution)/shard_map/ppermute | solution.py:387
  9.2 0.0 copy-done
  9.2 0.9 %local.2.ahead_ref = f32[2,1088,128]{2,1,0:T(8,128)S(1)} custom-call(f32[2,1088,128]{2,1,0:T(8,128)S(1)} %get-tuple-element.35.signal_ref, f32[32,256]{1,0:T(8,128)S(1)} %get-tuple-element.36.table_ref, f32[1,256]{1,0:T(1,128)S(1)} %bitcast.3), custom_call_target="tpu_custom_call", output_to_operand_aliasing={{}: (0, {})} | custom-call | flops 4456448 | bytes 2228224 | tf_op jit(solution)/shard_map/local/pallas_call | solution.py:369
  10.1 1.0 %collective-permute-done.1 = f32[32,256]{1,0:T(8,128)S(1)} collective-permute-done((f32[32,256]{1,0:T(8,128)S(1)}, f32[32,256]{1,0:T(8,128)S(1)}, u32[]{:S(2)}, u32[]{:S(2)}) %collective-permute-start.1) | collective-permute-done | bytes 32800 | tf_op jit(solution)/shard_map/ppermute | solution.py:387
  11.2 2.2 %collective-permute-start.2 = (f32[32,256]{1,0:T(8,128)S(1)}, f32[32,256]{1,0:T(8,128)S(1)}, u32[]{:S(2)}, u32[]{:S(2)}) collective-permute-start(f32[32,256]{1,0:T(8,128)S(1)} %get-tuple-element.38), channel_id=1, source_target_pairs={{0,4},{1,5},{2,6},{3,7},{4,0},{5,1},{6,2},{7,3},{8,12},{9,13},{10,... | collective-permute-start | bytes 98312 | tf_op jit(solution)/shard_map/ppermute | solution.py:387
  13.3 0.8 %local.3.back_ref = f32[2,1088,128]{2,1,0:T(8,128)S(1)} custom-call(f32[2,1088,128]{2,1,0:T(8,128)S(1)} %get-tuple-element.41.signal_ref, f32[32,256]{1,0:T(8,128)S(1)} %get-tuple-element.36.table_ref, f32[1,256]{1,0:T(1,128)S(1)} %bitcast.4), custom_call_target="tpu_custom_call", output_to_operand_aliasing={{}: (0, {})} | custom-call | flops 4456448 | bytes 2228224 | tf_op jit(solution)/shard_map/local/pallas_call | solution.py:369
  14.2 1.1 %collective-permute-done.2 = f32[32,256]{1,0:T(8,128)S(1)} collective-permute-done((f32[32,256]{1,0:T(8,128)S(1)}, f32[32,256]{1,0:T(8,128)S(1)}, u32[]{:S(2)}, u32[]{:S(2)}) %collective-permute-start.2) | collective-permute-done | bytes 32800 | tf_op jit(solution)/shard_map/ppermute | solution.py:387
  15.3 3.1 %collective-permute-start.3 = (f32[16,256]{1,0:T(8,128)S(1)}, f32[16,256]{1,0:T(8,128)S(1)}, u32[]{:S(2)}, u32[]{:S(2)}) collective-permute-start(f32[16,256]{1,0:T(8,128)S(1)} %get-tuple-element.50), channel_id=1, source_target_pairs={{0,8},{1,9},{2,10},{3,11},{4,12},{5,13},{6,14},{7,15},{8,0},{9,1},... | collective-permute-start | bytes 49160 | tf_op jit(solution)/shard_map/ppermute | solution.py:411
  18.4 2.9 %settled.1 = (bf16[1024,256]{1,0:T(8,128)(2,1)}, bf16[1024,256]{1,0:T(8,128)(2,1)}, bf16[1024,256]{1,0:T(8,128)(2,1)}, bf16[1024,256]{1,0:T(8,128)(2,1)}) custom-call(bf16[1024,256]{1,0:T(8,128)(2,1)} %outer_hbm.5, bf16[1024,256]{1,0:T(8,128)(2,1)} %inner_hbm.5, bf16[1024,256]{1,0:T(8,128)(2,1)} %values_hbm.5, bf16[1024,256]{1,0:T(8,128)(2,1)} %cotangent_hbm.5, ...), custom_call_target="tpu_custom_call" | custom-call | flops 8388608 | bytes 3145728 | tf_op jit(solution)/shard_map/settled/pallas_call | solution.py:415
  21.3 0.0 collective-permute-done.3
  21.3 3.0 %last.1 = (bf16[1024,256]{1,0:T(8,128)(2,1)}, bf16[1024,256]{1,0:T(8,128)(2,1)}, bf16[1024,256]{1,0:T(8,128)(2,1)}, bf16[1024,256]{1,0:T(8,128)(2,1)}) custom-call(bf16[1024,256]{1,0:T(8,128)(2,1)} %outer_hbm.5, bf16[1024,256]{1,0:T(8,128)(2,1)} %inner_hbm.5, ...), custom_call_target="tpu_custom_call", output_to_operand_aliasing={{0}: (12, {}), {1}: (13, {}), {2}: (14, {}), {3}: (15, {})} | custom-call | flops 8388608 | bytes 3145728 | tf_op jit(solution)/shard_map/last/pallas_call | solution.py:415
  (5 shorter events, 0.1 us)
Async XLA Ops:
  0.6 8.6 %copy-start = (f32[256]{0:T(256)S(1)}, f32[256]{0:T(256)}, u32[]{:S(2)}) copy-start(f32[256]{0:T(256)} %param.13) | copy-start | bytes 3076
  5.0 1.4 %collective-permute-start = (f32[32,256]{1,0:T(8,128)S(1)}, f32[32,256]{1,0:T(8,128)S(1)}, u32[]{:S(2)}, u32[]{:S(2)}) collective-permute-start(f32[32,256]{1,0:T(8,128)S(1)} %get-tuple-element.31), channel_id=1, source_target_pairs={{0,1},{1,0},{2,3},{3,2},{4,5},{5,4},{6,7},{7,6},{8,9},{9,8},{10,11... | collective-permute-start | bytes 98312 | tf_op jit(solution)/shard_map/ppermute | solution.py:387
  6.3 4.8 %collective-permute-start.1 = (f32[32,256]{1,0:T(8,128)S(1)}, f32[32,256]{1,0:T(8,128)S(1)}, u32[]{:S(2)}, u32[]{:S(2)}) collective-permute-start(f32[32,256]{1,0:T(8,128)S(1)} %get-tuple-element.32), channel_id=1, source_target_pairs={{0,2},{1,3},{2,0},{3,1},{4,6},{5,7},{6,4},{7,5},{8,10},{9,11},{10,... | collective-permute-start | bytes 98312 | tf_op jit(solution)/shard_map/ppermute | solution.py:387
  11.2 4.1 %collective-permute-start.2 = (f32[32,256]{1,0:T(8,128)S(1)}, f32[32,256]{1,0:T(8,128)S(1)}, u32[]{:S(2)}, u32[]{:S(2)}) collective-permute-start(f32[32,256]{1,0:T(8,128)S(1)} %get-tuple-element.38), channel_id=1, source_target_pairs={{0,4},{1,5},{2,6},{3,7},{4,0},{5,1},{6,2},{7,3},{8,12},{9,13},{10,... | collective-permute-start | bytes 98312 | tf_op jit(solution)/shard_map/ppermute | solution.py:387
  15.3 6.1 %collective-permute-start.3 = (f32[16,256]{1,0:T(8,128)S(1)}, f32[16,256]{1,0:T(8,128)S(1)}, u32[]{:S(2)}, u32[]{:S(2)}) collective-permute-start(f32[16,256]{1,0:T(8,128)S(1)} %get-tuple-element.50), channel_id=1, source_target_pairs={{0,8},{1,9},{2,10},{3,11},{4,12},{5,13},{6,14},{7,15},{8,0},{9,1},... | collective-permute-start | bytes 49160 | tf_op jit(solution)/shard_map/ppermute | solution.py:411

commit v6 on v5

--- a/solution.py
+++ b/solution.py
@@ -11,6 +11,7 @@
 PAD = 8
 STEP = 16
 CHUNK = 16
+PIECES = 2
 F32 = jnp.float32
 BF16 = jnp.bfloat16
 VMEM = pl.BlockSpec(memory_space=pltpu.VMEM)
@@ -118,38 +119,43 @@
     factor_tables(rate_table, seg_len * SEGS, blocks, factor_ref)
     for h in range(count):
         lanes = lane_slice(h)
-        for copy in copies[h]:
+        steps = spread_rows(decay, lanes, poles)
+
+        def convert(first_ref, second_ref, target_ref, rounded):
+            def segment(q, _):
+                source = pl.ds(pl.multiple_of(q * seg_len, STEP), seg_len)
+                target = pl.ds(pl.multiple_of(q * pitch, 8), seg_len)
+                product = first_ref[source, lanes].astype(F32) * second_ref[
+                    source, lanes
+                ].astype(F32)
+                if rounded:
+                    product = product.astype(BF16).astype(F32)
+                target_ref[h, target, :] = product
+                return _
+
+            lax.fori_loop(0, SEGS, segment, 0)
+
+        def sums(signal_ref, chunk_ref, backward):
+            def chunk(m, _):
+                for j in range(CHUNK):
+                    row = m * CHUNK + (CHUNK - 1 - j if backward else j)
+                    x = signal_ref[h, pl.ds(row, SEGS, stride=pitch), :]
+                    state = [steps[k] * state[k] + x for k in range(poles)] if j else [x] * poles
+                for k in range(poles):
+                    rows = pl.ds(pl.multiple_of((m * poles + k) * SEGS, SEGS), SEGS)
+                    chunk_ref[h, rows, :] = state[k]
+                return _
+
+            lax.fori_loop(0, chunks, chunk, 0, unroll=2)
+
+        for copy in copies[h][:2]:
             copy.wait()
-
-        def convert(q, _):
-            source = pl.ds(pl.multiple_of(q * seg_len, 16), seg_len)
-            target = pl.ds(pl.multiple_of(q * pitch, 8), seg_len)
-            mixed = inner_ref[source, lanes].astype(F32) * values_ref[source, lanes].astype(F32)
-            mixed_ref[h, target, :] = mixed.astype(BF16).astype(F32)
-            outer, cotangent = outer_ref[source, lanes], cotangent_ref[source, lanes]
-            grad_ref[h, target, :] = outer.astype(F32) * cotangent.astype(F32)
-            return _
-
-        lax.fori_loop(0, SEGS, convert, 0)
-        steps = spread_rows(decay, lanes, poles)
-
-        def body(m, _):
-            base = m * CHUNK
-            for j in range(CHUNK):
-                x = mixed_ref[h, pl.ds(base + j, SEGS, stride=pitch), :]
-                g = grad_ref[h, pl.ds(base + CHUNK - 1 - j, SEGS, stride=pitch), :]
-                if j:
-                    ahead = [steps[k] * ahead[k] + x for k in range(poles)]
-                    back = [steps[k] * back[k] + g for k in range(poles)]
-                else:
-                    ahead, back = [x] * poles, [g] * poles
-            for k in range(poles):
-                rows = pl.ds(pl.multiple_of((m * poles + k) * SEGS, SEGS), SEGS)
-                gain_ref[h, rows, :] = ahead[k]
-                loss_ref[h, rows, :] = back[k]
-            return _
-
-        lax.fori_loop(0, chunks, body, 0)
+        convert(inner_ref, values_ref, mixed_ref, True)
+        sums(mixed_ref, gain_ref, False)
+        for copy in copies[h][2:]:
+            copy.wait()
+        convert(outer_ref, cotangent_ref, grad_ref, False)
+        sums(grad_ref, loss_ref, True)
         longer = spread_rows(chunk_decay, lanes, poles)
         for k in range(poles):
             ahead = gain_ref[h, SEGS * k : SEGS * (k + 1), :]
@@ -216,7 +222,7 @@
     targets,
     state_ref,
     total_ref,
-    sems,
+    send,
 ):
     poles = table_ref.shape[0] // 2
     pitch = seg_len + PAD
@@ -224,9 +230,6 @@
     rates = table_ref[0:poles, :]
     decay = jnp.exp(-rates)
     seg_decay = jnp.exp(-float(seg_len) * rates)
-    loads = [copy for copy, _ in gates]
-    gate_refs = [ref for _, ref in gates]
-    copies = []
     for h in range(local_ref.shape[0]):
         lanes = lane_slice(h)
         state = entry_ref[:, lanes]
@@ -256,34 +259,28 @@
             )
 
         lax.fori_loop(0, chunks, body, carried)
-        for copy in loads:
-            copy.wait()
-        loads = []
 
         def gate(q, _):
             whole = total_ref[pl.ds(pl.multiple_of(q * pitch, 8), seg_len), :]
             rows = pl.ds(pl.multiple_of(q * seg_len, STEP), seg_len)
-            for gate_ref, (target, _hbm) in zip(gate_refs, targets):
+            for gate_ref, target in zip(gates, targets):
                 target[rows, lanes] = (gate_ref[rows, lanes].astype(F32) * whole).astype(BF16)
             return _
 
-        lax.fori_loop(0, SEGS, gate, 0)
-        for j, (target, hbm) in enumerate(targets):
-            copy = pltpu.make_async_copy(target.at[:, lanes], hbm.at[:, lanes], sems.at[h, j])
-            copy.start()
-            copies.append(copy)
-    for copy in copies:
-        copy.wait()
+        for part in range(PIECES):
+            first, last = part * SEGS // PIECES, (part + 1) * SEGS // PIECES
+            lax.fori_loop(first, last, gate, 0)
+            send(h, part, pl.ds(first * seg_len, (last - first) * seg_len), lanes)
 
 
 def finish_kernel(
     seg_len,
     blocks,
     settled,
-    outer_hbm,
-    inner_hbm,
-    values_hbm,
-    cotangent_hbm,
+    outer_ref,
+    inner_ref,
+    values_ref,
+    cotangent_ref,
     ahead_ref,
     back_ref,
     gain_ref,
@@ -294,27 +291,38 @@
     entry_ref,
     *rest,
 ):
-    outs, (gate_a, gate_b, out_a, out_b, state_ref, total_ref, load_sems, out_sems) = (
-        rest[-12:-8],
-        rest[-8:],
-    )
-    layer_hbm, outer_grad_hbm, inner_grad_hbm, values_grad_hbm = outs
+    if settled:
+        out_a, out_b, state_ref, total_ref = rest
+    else:
+        done_a, done_b, *outs, out_a, out_b, state_ref, total_ref, done_sems, out_sems = rest
     later = lax.axis_index("ctx") >= blocks // 2
 
     def run(backward):
+        copies = []
+        if not settled:
+            here = (2, 3) if backward else (0, 1)
+            there = (0, 1) if backward else (2, 3)
+            for j, ready in enumerate((done_a, done_b)):
+                copy = pltpu.make_async_copy(ready, outs[there[j]], done_sems.at[j])
+                copy.start()
+                copies.append(copy)
+
+        def send(h, part, rows, lanes):
+            if settled:
+                return
+            for j, ready in enumerate((out_a, out_b)):
+                copy = pltpu.make_async_copy(
+                    ready.at[rows, lanes], outs[here[j]].at[rows, lanes], out_sems.at[h, part, j]
+                )
+                copy.start()
+                copies.append(copy)
+
         if backward:
-            sources = (values_hbm, inner_hbm)
-            targets = ((out_a, inner_grad_hbm), (out_b, values_grad_hbm))
+            gates = (values_ref, inner_ref)
             parts = (back_ref, loss_ref, starts_ref)
         else:
-            sources = (outer_hbm, cotangent_hbm)
-            targets = ((out_a, layer_hbm), (out_b, outer_grad_hbm))
+            gates = (outer_ref, cotangent_ref)
             parts = (ahead_ref, gain_ref, ends_ref)
-        gates = []
-        for j, (source, target) in enumerate(zip(sources, (gate_a, gate_b))):
-            copy = pltpu.make_async_copy(source, target, load_sems.at[j])
-            copy.start()
-            gates.append((copy, target))
         finish_way(
             seg_len,
             backward,
@@ -322,11 +330,13 @@
             *parts,
             table_ref,
             entry_ref,
-            targets,
+            (out_a, out_b),
             state_ref,
             total_ref,
-            out_sems,
+            send,
         )
+        for copy in copies:
+            copy.wait()
 
     pl.when(later)(functools.partial(run, settled))
     pl.when(jnp.logical_not(later))(functools.partial(run, not settled))
@@ -349,16 +359,17 @@
         return pltpu.with_memory_space_constraint(x, pltpu.HBM)
 
     arrays = [in_hbm(x) for x in (outer_gate, inner_gate, values, cotangent)]
-    mixed, grad, gain, loss, ends, starts, own, table, factors = pl.pallas_call(
+    mixed, grad, gain, loss, ends, starts, own, table, factors, *gates = pl.pallas_call(
         functools.partial(state_kernel, seg_len, blocks),
         out_shape=[jax.ShapeDtypeStruct((count, padded, LANES), F32)] * 2
         + [jax.ShapeDtypeStruct((count, rows // CHUNK * poles, LANES), F32)] * 2
         + [jax.ShapeDtypeStruct((count, SEGS * poles, LANES), F32)] * 2
         + [jax.ShapeDtypeStruct((2 * poles, channels), F32)] * 2
-        + [jax.ShapeDtypeStruct(((6 * levels - 4) * poles, channels), F32)],
+        + [jax.ShapeDtypeStruct(((6 * levels - 4) * poles, channels), F32)]
+        + [gate] * 4,
         in_specs=[HBM] * 6,
-        out_specs=[VMEM] * 9,
-        scratch_shapes=[pltpu.VMEM((rows, channels), BF16)] * 4 + [dma((count, 4)), dma((2,))],
+        out_specs=[VMEM] * 13,
+        scratch_shapes=[dma((count, 4)), dma((2,))],
         compiler_params=limit,
         name="states",
     )(*arrays, in_hbm(decay_rate.T), in_hbm(residue.T))
@@ -379,12 +390,14 @@
             name="local",
         )(signal, table, skip)
 
+    def partners(bit):
+        return [(i, i ^ (1 << bit) ^ (1 if bit else 0)) for i in range(blocks)]
+
     jobs = [(mixed, False), (grad, True)]
     found = []
     entry = jnp.zeros_like(own)
     for bit in range(levels - 1):
-        reach = 1 << bit
-        other = lax.ppermute(own, "ctx", [(i, i ^ reach) for i in range(blocks)])
+        other = lax.ppermute(own, "ctx", partners(bit))
         pieces = [local(*jobs.pop(0), own)] if bit and jobs else []
         keep, take, join = factors[6 * bit * poles : 6 * (bit + 1) * poles].reshape(
             3, 2 * poles, channels
@@ -408,28 +421,29 @@
             choose(ahead_entry, back_entry),
         )
     )
-    other = lax.ppermute(sent, "ctx", [(i, i ^ (blocks // 2)) for i in range(blocks)])
+    other = lax.ppermute(sent, "ctx", partners(levels - 1))
 
     def finish(settled, entry, before):
-        first = 12
+        work_space = [pltpu.VMEM((SEGS * poles, LANES), F32), pltpu.VMEM((padded, LANES), F32)]
+        if not settled:
+            work_space = [pltpu.VMEM((rows, channels), BF16)] * 2 + work_space
+            work_space += [dma((2,)), dma((count, PIECES, 2))]
         return pl.pallas_call(
             functools.partial(finish_kernel, seg_len, blocks, settled),
-            out_shape=[gate] * 4,
-            in_specs=[HBM] * 4 + [VMEM] * 8 + [HBM] * len(before),
-            out_specs=[HBM] * 4,
-            input_output_aliases={first + j: j for j in range(len(before))},
-            scratch_shapes=[pltpu.VMEM((rows, channels), BF16)] * 4
-            + [pltpu.VMEM((SEGS * poles, LANES), F32), pltpu.VMEM((padded, LANES), F32)]
-            + [dma((2,)), dma((count, 2))],
+            out_shape=[gate] * (2 if settled else 4),
+            in_specs=[VMEM] * (12 + len(before)),
+            out_specs=[VMEM] * 2 if settled else [HBM] * 4,
+            scratch_shapes=work_space,
             compiler_params=limit,
             cost_estimate=pl.CostEstimate(
                 flops=work * 2, bytes_accessed=rows * channels * 12, transcendentals=0
             ),
             name="settled" if settled else "last",
-        )(*arrays, *found, gain, loss, ends, starts, table, entry, *before)
-
-    outs = finish(True, settled_entry, ())
-    return finish(False, open_entry + shift * other, outs)
+        )(*gates, *found, gain, loss, ends, starts, table, entry, *before)
+
+    ready = finish(True, settled_entry, ())
+    other, ready = lax.optimization_barrier((other, ready))
+    return finish(False, open_entry + shift * other, ready)
 
 
 def solution(mesh):

time: 24.5 us -> 21.2 us (0.87)
  Pallas kernels: 11.9 us -> 10 us
  starting transfers between devices: 8.69 us -> 7.91 us
  waiting for transfers between devices: 2.97 us -> 2.38 us
    pallas_call x2, Pallas kernels: 5.93 us -> 3.98 us  [finish(): pl.pallas_call(functools.partial(finish_kernel, seg_len, blocks, settled)...]
    ppermute x4, starting transfers between devices: 8.69 us -> 7.91 us  [the longest x3 5.08 us: shards(): other = lax.ppermute(own, 'ctx', partners(bit))]
    ppermute x4, waiting for transfers between devices: 2.97 us -> 2.38 us  [the longest x3 2.37 us: shards(): other = lax.ppermute(own, 'ctx', partners(bit))]
  transfers between devices with their start and end apart: 4 -> 4, of which waited for: 3 -> 3; matrix products, arithmetic and copies ran while one was open for 0% -> 0% of each run, Pallas kernels for 19% -> 15%
where the time goes in v6:
time: 21.2 us; the launch traced here: 21.1 us
  Pallas kernels  10 us (47%)
  starting transfers between devices  7.91 us (37%)
  waiting for transfers between devices  2.38 us (11%)
  between operations  0.7 us (3%)
    ppermute x3, starting transfers between devices, shards(): other = lax.ppermute(own, 'ctx', partners(bit))  5.08 us
    pallas_call x1, Pallas kernels, shards(): pl.pallas_call(functools.partial(state_kernel, seg_len, blocks), out_shap...  4.36 us
    pallas_call x2, Pallas kernels, finish(): pl.pallas_call(functools.partial(finish_kernel, seg_len, blocks, settled)...  3.98 us
    ppermute x1, starting transfers between devices, shards(): other = lax.ppermute(sent, 'ctx', partners(levels - 1))  2.82 us
    ppermute x3, waiting for transfers between devices, shards(): other = lax.ppermute(own, 'ctx', partners(bit))  2.37 us
    pallas_call x2, Pallas kernels, local(): pl.pallas_call(functools.partial(local_kernel, seg_len, backward), out_sh...  1.67 us
  transfers between devices with their start and end apart: 4, of which 3 were waited for; matrix products, arithmetic and copies ran while one was open for 0% of the time, Pallas kernels for 15%

profile of v6, /device:TPU:0, one launch (start us, length us, event | category | flops | bytes accessed | tf_op | source)
XLA Modules:
  0.0 21.1 jit_solution(15120227437989496160)
XLA Ops:
  0.6 0.0 copy-start
  0.6 4.4 %states.1 = (f32[2,1088,128]{2,1,0:T(8,128)S(1)}, f32[2,1088,128]{2,1,0:T(8,128)S(1)}, f32[2,1024,128]{2,1,0:T(8,128)S(1)}, f32[2,1024,128]{2,1,0:T(8,128)S(1)},...) custom-call(bf16[1024,256]{1,0:T(8,128)(2,1)} %outer_hbm.1, ...), custom_call_target="tpu_custom_call" | custom-call | tf_op jit(solution)/shard_map/states/pallas_call | solution.py:362
  5.0 0.5 %collective-permute-start = (f32[32,256]{1,0:T(8,128)S(1)}, f32[32,256]{1,0:T(8,128)S(1)}, u32[]{:S(2)}, u32[]{:S(2)}) collective-permute-start(f32[32,256]{1,0:T(8,128)S(1)} %get-tuple-element.40), channel_id=1, source_target_pairs={{0,1},{1,0},{2,3},{3,2},{4,5},{5,4},{6,7},{7,6},{8,9},{9,8},{10,11... | collective-permute-start | bytes 98312 | tf_op jit(solution)/shard_map/ppermute | solution.py:400
  5.5 0.9 %collective-permute-done = f32[32,256]{1,0:T(8,128)S(1)} collective-permute-done((f32[32,256]{1,0:T(8,128)S(1)}, f32[32,256]{1,0:T(8,128)S(1)}, u32[]{:S(2)}, u32[]{:S(2)}) %collective-permute-start) | collective-permute-done | bytes 32800 | tf_op jit(solution)/shard_map/ppermute | solution.py:400
  6.4 2.7 %collective-permute-start.1 = (f32[32,256]{1,0:T(8,128)S(1)}, f32[32,256]{1,0:T(8,128)S(1)}, u32[]{:S(2)}, u32[]{:S(2)}) collective-permute-start(f32[32,256]{1,0:T(8,128)S(1)} %get-tuple-element.41), channel_id=1, source_target_pairs={{0,3},{1,2},{2,1},{3,0},{4,7},{5,6},{6,5},{7,4},{8,11},{9,10},{10,... | collective-permute-start | bytes 98312 | tf_op jit(solution)/shard_map/ppermute | solution.py:400
  9.1 0.0 copy-done
  9.1 0.9 %local.2.ahead_ref = f32[2,1088,128]{2,1,0:T(8,128)S(1)} custom-call(f32[2,1088,128]{2,1,0:T(8,128)S(1)} %get-tuple-element.44.signal_ref, f32[32,256]{1,0:T(8,128)S(1)} %get-tuple-element.45.table_ref, f32[1,256]{1,0:T(1,128)S(1)} %bitcast.3), custom_call_target="tpu_custom_call", output_to_operand_aliasing={{}: (0, {})} | custom-call | flops 4456448 | bytes 2228224 | tf_op jit(solution)/shard_map/local/pallas_call | solution.py:380
  9.9 0.7 %collective-permute-done.1 = f32[32,256]{1,0:T(8,128)S(1)} collective-permute-done((f32[32,256]{1,0:T(8,128)S(1)}, f32[32,256]{1,0:T(8,128)S(1)}, u32[]{:S(2)}, u32[]{:S(2)}) %collective-permute-start.1) | collective-permute-done | bytes 32800 | tf_op jit(solution)/shard_map/ppermute | solution.py:400
  10.7 1.9 %collective-permute-start.2 = (f32[32,256]{1,0:T(8,128)S(1)}, f32[32,256]{1,0:T(8,128)S(1)}, u32[]{:S(2)}, u32[]{:S(2)}) collective-permute-start(f32[32,256]{1,0:T(8,128)S(1)} %get-tuple-element.47), channel_id=1, source_target_pairs={{0,5},{1,4},{2,7},{3,6},{4,1},{5,0},{6,3},{7,2},{8,13},{9,12},{10,... | collective-permute-start | bytes 98312 | tf_op jit(solution)/shard_map/ppermute | solution.py:400
  12.6 0.8 %local.3.back_ref = f32[2,1088,128]{2,1,0:T(8,128)S(1)} custom-call(f32[2,1088,128]{2,1,0:T(8,128)S(1)} %get-tuple-element.50.signal_ref, f32[32,256]{1,0:T(8,128)S(1)} %get-tuple-element.45.table_ref, f32[1,256]{1,0:T(1,128)S(1)} %bitcast.4), custom_call_target="tpu_custom_call", output_to_operand_aliasing={{}: (0, {})} | custom-call | flops 4456448 | bytes 2228224 | tf_op jit(solution)/shard_map/local/pallas_call | solution.py:380
  13.4 0.8 %collective-permute-done.2 = f32[32,256]{1,0:T(8,128)S(1)} collective-permute-done((f32[32,256]{1,0:T(8,128)S(1)}, f32[32,256]{1,0:T(8,128)S(1)}, u32[]{:S(2)}, u32[]{:S(2)}) %collective-permute-start.2) | collective-permute-done | bytes 32800 | tf_op jit(solution)/shard_map/ppermute | solution.py:400
  14.2 2.8 %collective-permute-start.3 = (f32[16,256]{1,0:T(8,128)S(1)}, f32[16,256]{1,0:T(8,128)S(1)}, u32[]{:S(2)}, u32[]{:S(2)}) collective-permute-start(f32[16,256]{1,0:T(8,128)S(1)} %get-tuple-element.59), channel_id=1, source_target_pairs={{0,9},{1,8},{2,11},{3,10},{4,13},{5,12},{6,15},{7,14},{8,1},{9,0},... | collective-permute-start | bytes 49160 | tf_op jit(solution)/shard_map/ppermute | solution.py:424
  17.0 1.6 %settled.1 = (bf16[1024,256]{1,0:T(8,128)(2,1)S(1)}, bf16[1024,256]{1,0:T(8,128)(2,1)S(1)}) custom-call(bf16[1024,256]{1,0:T(8,128)(2,1)S(1)} %get-tuple-element.35.outer_ref, bf16[1024,256]{1,0:T(8,128)(2,1)S(1)} %get-tuple-element.36.inner_ref, bf16[1024,256]{1,0:T(8,128)(2,1)S(1)} %get-tuple-element.37.values_ref, ...), custom_call_target="tpu_custom_call" | custom-call | flops 8388608 | bytes 3145728 | tf_op jit(solution)/shard_map/settled/pallas_call | solution.py:431
  18.6 0.0 collective-permute-done.3
  18.6 2.4 %last.1 = (bf16[1024,256]{1,0:T(8,128)(2,1)}, bf16[1024,256]{1,0:T(8,128)(2,1)}, bf16[1024,256]{1,0:T(8,128)(2,1)}, bf16[1024,256]{1,0:T(8,128)(2,1)}) custom-call(bf16[1024,256]{1,0:T(8,128)(2,1)S(1)} %get-tuple-element.35.outer_ref, bf16[1024,256]{1,0:T(8,128)(2,1)S(1)} %get-tuple-element.36.inner_ref, bf16[1024,256]{1,0:T(8,128)(2,1)S(1)} %get-tuple-element.37.values_ref, ...), custom_call_target="tpu_custom_call" | custom-call | flops 8388608 | bytes 3145728 | tf_op jit(solution)/shard_map/last/pallas_call | solution.py:431
  (5 shorter events, 0.1 us)
Async XLA Ops:
  0.6 8.4 %copy-start = (f32[256]{0:T(256)S(1)}, f32[256]{0:T(256)}, u32[]{:S(2)}) copy-start(f32[256]{0:T(256)} %param.13) | copy-start | bytes 3076
  5.0 1.4 %collective-permute-start = (f32[32,256]{1,0:T(8,128)S(1)}, f32[32,256]{1,0:T(8,128)S(1)}, u32[]{:S(2)}, u32[]{:S(2)}) collective-permute-start(f32[32,256]{1,0:T(8,128)S(1)} %get-tuple-element.40), channel_id=1, source_target_pairs={{0,1},{1,0},{2,3},{3,2},{4,5},{5,4},{6,7},{7,6},{8,9},{9,8},{10,11... | collective-permute-start | bytes 98312 | tf_op jit(solution)/shard_map/ppermute | solution.py:400
  6.4 4.3 %collective-permute-start.1 = (f32[32,256]{1,0:T(8,128)S(1)}, f32[32,256]{1,0:T(8,128)S(1)}, u32[]{:S(2)}, u32[]{:S(2)}) collective-permute-start(f32[32,256]{1,0:T(8,128)S(1)} %get-tuple-element.41), channel_id=1, source_target_pairs={{0,3},{1,2},{2,1},{3,0},{4,7},{5,6},{6,5},{7,4},{8,11},{9,10},{10,... | collective-permute-start | bytes 98312 | tf_op jit(solution)/shard_map/ppermute | solution.py:400
  10.7 3.5 %collective-permute-start.2 = (f32[32,256]{1,0:T(8,128)S(1)}, f32[32,256]{1,0:T(8,128)S(1)}, u32[]{:S(2)}, u32[]{:S(2)}) collective-permute-start(f32[32,256]{1,0:T(8,128)S(1)} %get-tuple-element.47), channel_id=1, source_target_pairs={{0,5},{1,4},{2,7},{3,6},{4,1},{5,0},{6,3},{7,2},{8,13},{9,12},{10,... | collective-permute-start | bytes 98312 | tf_op jit(solution)/shard_map/ppermute | solution.py:400
  14.2 4.4 %collective-permute-start.3 = (f32[16,256]{1,0:T(8,128)S(1)}, f32[16,256]{1,0:T(8,128)S(1)}, u32[]{:S(2)}, u32[]{:S(2)}) collective-permute-start(f32[16,256]{1,0:T(8,128)S(1)} %get-tuple-element.59), channel_id=1, source_target_pairs={{0,9},{1,8},{2,11},{3,10},{4,13},{5,12},{6,15},{7,14},{8,1},{9,0},... | collective-permute-start | bytes 49160 | tf_op jit(solution)/shard_map/ppermute | solution.py:424

commit v7 on v6

--- a/solution.py
+++ b/solution.py
@@ -33,13 +33,13 @@
     return [jnp.broadcast_to(table[k : k + 1, lanes], (8, LANES)) for k in range(count)]
 
 
-def factor_tables(rates, rows, blocks, factor_ref):
+def factor_tables(rates, rows, blocks, bits, factor_ref):
     poles, channels = rates.shape
     me = lax.axis_index("ctx")
     one = jnp.ones((poles, channels), F32)
     zero = jnp.zeros((poles, channels), F32)
     base = 0
-    for bit in range(blocks.bit_length() - 1):
+    for bit in bits:
         reach = 1 << bit
         later = jnp.bitwise_and(jnp.right_shift(me, bit), 1) == 1
         place = jnp.bitwise_and(me, reach - 1)
@@ -86,56 +86,50 @@
     pitch = seg_len + PAD
     count = mixed_ref.shape[0]
     chunks = seg_len // CHUNK
+    pairs = (
+        (inner_hbm, inner_ref),
+        (values_hbm, values_ref),
+        (outer_hbm, outer_ref),
+        (cotangent_hbm, cotangent_ref),
+    )
+    copies = [
+        [
+            pltpu.make_async_copy(
+                source.at[:, lane_slice(h)], target.at[:, lane_slice(h)], copy_sems.at[h, j]
+            )
+            for j, (source, target) in enumerate(pairs)
+        ]
+        for h in range(count)
+    ]
     tables = [
         pltpu.make_async_copy(
             source, table_ref.at[pl.ds(j * poles, poles), :], table_sems.at[j]
         )
         for j, source in enumerate((rate_hbm, residue_hbm))
     ]
-    for copy in tables:
+    first = copies[0][:2]
+    for copy in first + tables + copies[0][2:]:
         copy.start()
-    pairs = (
-        (inner_hbm, inner_ref),
-        (values_hbm, values_ref),
-        (outer_hbm, outer_ref),
-        (cotangent_hbm, cotangent_ref),
-    )
-    copies = []
-    for h in range(count):
-        line = []
-        for j, (source, target) in enumerate(pairs):
-            copy = pltpu.make_async_copy(
-                source.at[:, lane_slice(h)], target.at[:, lane_slice(h)], copy_sems.at[h, j]
-            )
-            copy.start()
-            line.append(copy)
-        copies.append(line)
-    for copy in tables:
-        copy.wait()
-    rate_table = table_ref[0:poles, :]
-    decay = jnp.exp(-rate_table)
-    chunk_decay = jnp.exp(-float(CHUNK) * rate_table)
-    seg_decay = jnp.exp(-float(seg_len) * rate_table)
-    factor_tables(rate_table, seg_len * SEGS, blocks, factor_ref)
     for h in range(count):
         lanes = lane_slice(h)
-        steps = spread_rows(decay, lanes, poles)
 
         def convert(first_ref, second_ref, target_ref, rounded):
             def segment(q, _):
                 source = pl.ds(pl.multiple_of(q * seg_len, STEP), seg_len)
                 target = pl.ds(pl.multiple_of(q * pitch, 8), seg_len)
-                product = first_ref[source, lanes].astype(F32) * second_ref[
-                    source, lanes
-                ].astype(F32)
+                first, second = first_ref[source, lanes], second_ref[source, lanes]
                 if rounded:
-                    product = product.astype(BF16).astype(F32)
+                    product = (first * second).astype(F32)
+                else:
+                    product = first.astype(F32) * second.astype(F32)
                 target_ref[h, target, :] = product
                 return _
 
-            lax.fori_loop(0, SEGS, segment, 0)
+            lax.fori_loop(0, SEGS, segment, 0, unroll=4)
 
         def sums(signal_ref, chunk_ref, backward):
+            steps = spread_rows(decay, lanes, poles)
+
             def chunk(m, _):
                 for j in range(CHUNK):
                     row = m * CHUNK + (CHUNK - 1 - j if backward else j)
@@ -146,11 +140,23 @@
                     chunk_ref[h, rows, :] = state[k]
                 return _
 
-            lax.fori_loop(0, chunks, chunk, 0, unroll=2)
+            lax.fori_loop(0, chunks, chunk, 0, unroll=8)
 
         for copy in copies[h][:2]:
             copy.wait()
+        if h == 0:
+            for line in copies[1:]:
+                for copy in line:
+                    copy.start()
         convert(inner_ref, values_ref, mixed_ref, True)
+        if h == 0:
+            for copy in tables:
+                copy.wait()
+            rate_table = table_ref[0:poles, :]
+            decay = jnp.exp(-rate_table)
+            chunk_decay = jnp.exp(-float(CHUNK) * rate_table)
+            seg_decay = jnp.exp(-float(seg_len) * rate_table)
+            factor_tables(rate_table, seg_len * SEGS, blocks, range(1), factor_ref)
         sums(mixed_ref, gain_ref, False)
         for copy in copies[h][2:]:
             copy.wait()
@@ -179,10 +185,13 @@
         own_ref[poles : 2 * poles, lanes] = back
 
 
-def local_kernel(seg_len, backward, signal_ref, table_ref, skip_ref, out_ref):
+def local_kernel(seg_len, blocks, backward, signal_ref, table_ref, skip_ref, out_ref, *factor_refs):
     poles = table_ref.shape[0] // 2
     pitch = seg_len + PAD
     chunks = seg_len // CHUNK
+    for factor_ref in factor_refs:
+        bits = range(1, blocks.bit_length() - 1)
+        factor_tables(table_ref[0:poles, :], seg_len * SEGS, blocks, bits, factor_ref)
     weight = table_ref[poles : 2 * poles, :]
     decay = jnp.exp(-table_ref[0:poles, :])
     rows = []
@@ -269,7 +278,7 @@
 
         for part in range(PIECES):
             first, last = part * SEGS // PIECES, (part + 1) * SEGS // PIECES
-            lax.fori_loop(first, last, gate, 0)
+            lax.fori_loop(first, last, gate, 0, unroll=4)
             send(h, part, pl.ds(first * seg_len, (last - first) * seg_len), lanes)
 
 
@@ -365,7 +374,7 @@
         + [jax.ShapeDtypeStruct((count, rows // CHUNK * poles, LANES), F32)] * 2
         + [jax.ShapeDtypeStruct((count, SEGS * poles, LANES), F32)] * 2
         + [jax.ShapeDtypeStruct((2 * poles, channels), F32)] * 2
-        + [jax.ShapeDtypeStruct(((6 * levels - 4) * poles, channels), F32)]
+        + [jax.ShapeDtypeStruct((6 * poles, channels), F32)]
         + [gate] * 4,
         in_specs=[HBM] * 6,
         out_specs=[VMEM] * 13,
@@ -377,11 +386,14 @@
 
     def local(signal, backward, held):
         signal, _ = lax.optimization_barrier((signal, held))
+        shapes = [jax.ShapeDtypeStruct(signal.shape, F32)]
+        if not backward:
+            shapes.append(jax.ShapeDtypeStruct((6 * (levels - 2) * poles + 2 * poles, channels), F32))
         return pl.pallas_call(
-            functools.partial(local_kernel, seg_len, backward),
-            out_shape=jax.ShapeDtypeStruct(signal.shape, F32),
+            functools.partial(local_kernel, seg_len, blocks, backward),
+            out_shape=shapes,
             in_specs=[VMEM] * 3,
-            out_specs=VMEM,
+            out_specs=[VMEM] * len(shapes),
             input_output_aliases={0: 0},
             compiler_params=limit,
             cost_estimate=pl.CostEstimate(
@@ -398,16 +410,22 @@
     entry = jnp.zeros_like(own)
     for bit in range(levels - 1):
         other = lax.ppermute(own, "ctx", partners(bit))
-        pieces = [local(*jobs.pop(0), own)] if bit and jobs else []
-        keep, take, join = factors[6 * bit * poles : 6 * (bit + 1) * poles].reshape(
-            3, 2 * poles, channels
-        )
+        pieces = []
+        if bit and jobs:
+            piece, *more = local(*jobs.pop(0), own)
+            pieces = [piece]
+            factors = more[0] if more else factors
+        base = 6 * max(bit - 1, 0) * poles
+        keep, take, join = factors[base : base + 6 * poles].reshape(3, 2 * poles, channels)
         entry = entry + join * other
         own = keep * own + take * other
         own, entry, pieces = lax.optimization_barrier((own, entry, pieces))
         found += pieces
-    found += [local(*job, own) for job in jobs]
-    shift, late = factors[6 * (levels - 1) * poles :].reshape(2, poles, channels)
+    for job in jobs:
+        piece, *more = local(*job, own)
+        found.append(piece)
+        factors = more[0] if more else factors
+    shift, late = factors[-2 * poles :].reshape(2, poles, channels)
 
     def choose(when_later, otherwise):
         return late * when_later + (1.0 - late) * otherwise

time: 21.2 us -> 20.4 us (0.962)
  Pallas kernels: 10 us -> 9.24 us
    pallas_call x1, Pallas kernels: 4.36 us -> 3.73 us  [shards(): pl.pallas_call(functools.partial(state_kernel, seg_len, blocks), out_shap...]
  transfers between devices with their start and end apart: 4 -> 4, of which waited for: 3 -> 3; matrix products, arithmetic and copies ran while one was open for 0% -> 0% of each run, Pallas kernels for 15% -> 16%
where the time goes in v7:
time: 20.4 us; the launch traced here: 20.3 us
  Pallas kernels  9.24 us (45%)
  starting transfers between devices  7.91 us (39%)
  waiting for transfers between devices  2.36 us (12%)
  between operations  0.7 us (3%)
    ppermute x3, starting transfers between devices, shards(): other = lax.ppermute(own, 'ctx', partners(bit))  5.08 us
    pallas_call x2, Pallas kernels, finish(): pl.pallas_call(functools.partial(finish_kernel, seg_len, blocks, settled)...  3.82 us
    pallas_call x1, Pallas kernels, shards(): pl.pallas_call(functools.partial(state_kernel, seg_len, blocks), out_shap...  3.73 us
    ppermute x1, starting transfers between devices, shards(): other = lax.ppermute(sent, 'ctx', partners(levels - 1))  2.82 us
    ppermute x3, waiting for transfers between devices, shards(): other = lax.ppermute(own, 'ctx', partners(bit))  2.36 us
    pallas_call x2, Pallas kernels, local(): pl.pallas_call(functools.partial(local_kernel, seg_len, blocks, backward)...  1.69 us
  transfers between devices with their start and end apart: 4, of which 3 were waited for; matrix products, arithmetic and copies ran while one was open for 0% of the time, Pallas kernels for 16%

profile of v7, /device:TPU:0, one launch (start us, length us, event | category | flops | bytes accessed | tf_op | source)
XLA Modules:
  0.0 20.3 jit_solution(2220202539188010648)
XLA Ops:
  0.6 0.0 copy-start
  0.6 3.7 %states.1 = (f32[2,1088,128]{2,1,0:T(8,128)S(1)}, f32[2,1088,128]{2,1,0:T(8,128)S(1)}, f32[2,1024,128]{2,1,0:T(8,128)S(1)}, f32[2,1024,128]{2,1,0:T(8,128)S(1)},...) custom-call(bf16[1024,256]{1,0:T(8,128)(2,1)} %outer_hbm.1, ...), custom_call_target="tpu_custom_call" | custom-call | tf_op jit(solution)/shard_map/states/pallas_call | solution.py:371
  4.4 0.5 %collective-permute-start = (f32[32,256]{1,0:T(8,128)S(1)}, f32[32,256]{1,0:T(8,128)S(1)}, u32[]{:S(2)}, u32[]{:S(2)}) collective-permute-start(f32[32,256]{1,0:T(8,128)S(1)} %get-tuple-element.43), channel_id=1, source_target_pairs={{0,1},{1,0},{2,3},{3,2},{4,5},{5,4},{6,7},{7,6},{8,9},{9,8},{10,11... | collective-permute-start | bytes 98312 | tf_op jit(solution)/shard_map/ppermute | solution.py:412
  4.9 0.9 %collective-permute-done = f32[32,256]{1,0:T(8,128)S(1)} collective-permute-done((f32[32,256]{1,0:T(8,128)S(1)}, f32[32,256]{1,0:T(8,128)S(1)}, u32[]{:S(2)}, u32[]{:S(2)}) %collective-permute-start) | collective-permute-done | bytes 32800 | tf_op jit(solution)/shard_map/ppermute | solution.py:412
  5.8 2.7 %collective-permute-start.1 = (f32[32,256]{1,0:T(8,128)S(1)}, f32[32,256]{1,0:T(8,128)S(1)}, u32[]{:S(2)}, u32[]{:S(2)}) collective-permute-start(f32[32,256]{1,0:T(8,128)S(1)} %get-tuple-element.44), channel_id=1, source_target_pairs={{0,3},{1,2},{2,1},{3,0},{4,7},{5,6},{6,5},{7,4},{8,11},{9,10},{10,... | collective-permute-start | bytes 98312 | tf_op jit(solution)/shard_map/ppermute | solution.py:412
  8.4 0.0 copy-done
  8.4 0.9 %local.2 = (f32[2,1088,128]{2,1,0:T(8,128)S(1)}, f32[224,256]{1,0:T(8,128)S(1)}) custom-call(f32[2,1088,128]{2,1,0:T(8,128)S(1)} %get-tuple-element.45.signal_ref, f32[32,256]{1,0:T(8,128)S(1)} %get-tuple-element.46.table_ref, f32[1,256]{1,0:T(1,128)S(1)} %bitcast.3), custom_call_target="tpu_custom_call", output_to_operand_aliasing={{0}: (0, {})} | custom-call | flops 4456448 | bytes 2228224 | tf_op jit(solution)/shard_map/local/pallas_call | solution.py:392
  9.3 0.7 %collective-permute-done.1 = f32[32,256]{1,0:T(8,128)S(1)} collective-permute-done((f32[32,256]{1,0:T(8,128)S(1)}, f32[32,256]{1,0:T(8,128)S(1)}, u32[]{:S(2)}, u32[]{:S(2)}) %collective-permute-start.1) | collective-permute-done | bytes 32800 | tf_op jit(solution)/shard_map/ppermute | solution.py:412
  10.1 1.9 %collective-permute-start.2 = (f32[32,256]{1,0:T(8,128)S(1)}, f32[32,256]{1,0:T(8,128)S(1)}, u32[]{:S(2)}, u32[]{:S(2)}) collective-permute-start(f32[32,256]{1,0:T(8,128)S(1)} %get-tuple-element.51), channel_id=1, source_target_pairs={{0,5},{1,4},{2,7},{3,6},{4,1},{5,0},{6,3},{7,2},{8,13},{9,12},{10,... | collective-permute-start | bytes 98312 | tf_op jit(solution)/shard_map/ppermute | solution.py:412
  12.0 0.8 %local.3.back_ref = f32[2,1088,128]{2,1,0:T(8,128)S(1)} custom-call(f32[2,1088,128]{2,1,0:T(8,128)S(1)} %get-tuple-element.54.signal_ref, f32[32,256]{1,0:T(8,128)S(1)} %get-tuple-element.46.table_ref, f32[1,256]{1,0:T(1,128)S(1)} %bitcast.4), custom_call_target="tpu_custom_call", output_to_operand_aliasing={{}: (0, {})} | custom-call | flops 4456448 | bytes 2228224 | tf_op jit(solution)/shard_map/local/pallas_call | solution.py:392
  12.8 0.8 %collective-permute-done.2 = f32[32,256]{1,0:T(8,128)S(1)} collective-permute-done((f32[32,256]{1,0:T(8,128)S(1)}, f32[32,256]{1,0:T(8,128)S(1)}, u32[]{:S(2)}, u32[]{:S(2)}) %collective-permute-start.2) | collective-permute-done | bytes 32800 | tf_op jit(solution)/shard_map/ppermute | solution.py:412
  13.6 2.8 %collective-permute-start.3 = (f32[16,256]{1,0:T(8,128)S(1)}, f32[16,256]{1,0:T(8,128)S(1)}, u32[]{:S(2)}, u32[]{:S(2)}) collective-permute-start(f32[16,256]{1,0:T(8,128)S(1)} %get-tuple-element.63), channel_id=1, source_target_pairs={{0,9},{1,8},{2,11},{3,10},{4,13},{5,12},{6,15},{7,14},{8,1},{9,0},... | collective-permute-start | bytes 49160 | tf_op jit(solution)/shard_map/ppermute | solution.py:442
  16.4 1.5 %settled.1 = (bf16[1024,256]{1,0:T(8,128)(2,1)S(1)}, bf16[1024,256]{1,0:T(8,128)(2,1)S(1)}) custom-call(bf16[1024,256]{1,0:T(8,128)(2,1)S(1)} %get-tuple-element.37.outer_ref, bf16[1024,256]{1,0:T(8,128)(2,1)S(1)} %get-tuple-element.38.inner_ref, bf16[1024,256]{1,0:T(8,128)(2,1)S(1)} %get-tuple-element.39.values_ref, ...), custom_call_target="tpu_custom_call" | custom-call | flops 8388608 | bytes 3145728 | tf_op jit(solution)/shard_map/settled/pallas_call | solution.py:449
  17.9 0.0 collective-permute-done.3
  17.9 2.3 %last.1 = (bf16[1024,256]{1,0:T(8,128)(2,1)}, bf16[1024,256]{1,0:T(8,128)(2,1)}, bf16[1024,256]{1,0:T(8,128)(2,1)}, bf16[1024,256]{1,0:T(8,128)(2,1)}) custom-call(bf16[1024,256]{1,0:T(8,128)(2,1)S(1)} %get-tuple-element.37.outer_ref, bf16[1024,256]{1,0:T(8,128)(2,1)S(1)} %get-tuple-element.38.inner_ref, bf16[1024,256]{1,0:T(8,128)(2,1)S(1)} %get-tuple-element.39.values_ref, ...), custom_call_target="tpu_custom_call" | custom-call | flops 8388608 | bytes 3145728 | tf_op jit(solution)/shard_map/last/pallas_call | solution.py:449
  (5 shorter events, 0.1 us)
Async XLA Ops:
  0.6 7.8 %copy-start = (f32[256]{0:T(256)S(1)}, f32[256]{0:T(256)}, u32[]{:S(2)}) copy-start(f32[256]{0:T(256)} %param.13) | copy-start | bytes 3076
  4.4 1.4 %collective-permute-start = (f32[32,256]{1,0:T(8,128)S(1)}, f32[32,256]{1,0:T(8,128)S(1)}, u32[]{:S(2)}, u32[]{:S(2)}) collective-permute-start(f32[32,256]{1,0:T(8,128)S(1)} %get-tuple-element.43), channel_id=1, source_target_pairs={{0,1},{1,0},{2,3},{3,2},{4,5},{5,4},{6,7},{7,6},{8,9},{9,8},{10,11... | collective-permute-start | bytes 98312 | tf_op jit(solution)/shard_map/ppermute | solution.py:412
  5.8 4.3 %collective-permute-start.1 = (f32[32,256]{1,0:T(8,128)S(1)}, f32[32,256]{1,0:T(8,128)S(1)}, u32[]{:S(2)}, u32[]{:S(2)}) collective-permute-start(f32[32,256]{1,0:T(8,128)S(1)} %get-tuple-element.44), channel_id=1, source_target_pairs={{0,3},{1,2},{2,1},{3,0},{4,7},{5,6},{6,5},{7,4},{8,11},{9,10},{10,... | collective-permute-start | bytes 98312 | tf_op jit(solution)/shard_map/ppermute | solution.py:412
  10.1 3.5 %collective-permute-start.2 = (f32[32,256]{1,0:T(8,128)S(1)}, f32[32,256]{1,0:T(8,128)S(1)}, u32[]{:S(2)}, u32[]{:S(2)}) collective-permute-start(f32[32,256]{1,0:T(8,128)S(1)} %get-tuple-element.51), channel_id=1, source_target_pairs={{0,5},{1,4},{2,7},{3,6},{4,1},{5,0},{6,3},{7,2},{8,13},{9,12},{10,... | collective-permute-start | bytes 98312 | tf_op jit(solution)/shard_map/ppermute | solution.py:412
  13.6 4.3 %collective-permute-start.3 = (f32[16,256]{1,0:T(8,128)S(1)}, f32[16,256]{1,0:T(8,128)S(1)}, u32[]{:S(2)}, u32[]{:S(2)}) collective-permute-start(f32[16,256]{1,0:T(8,128)S(1)} %get-tuple-element.63), channel_id=1, source_target_pairs={{0,9},{1,8},{2,11},{3,10},{4,13},{5,12},{6,15},{7,14},{8,1},{9,0},... | collective-permute-start | bytes 49160 | tf_op jit(solution)/shard_map/ppermute | solution.py:442

commit v8 on v7

--- a/solution.py
+++ b/solution.py
@@ -227,7 +227,7 @@
     chunk_ref,
     edge_ref,
     table_ref,
-    entry_ref,
+    entry,
     targets,
     state_ref,
     total_ref,
@@ -241,7 +241,7 @@
     seg_decay = jnp.exp(-float(seg_len) * rates)
     for h in range(local_ref.shape[0]):
         lanes = lane_slice(h)
-        state = entry_ref[:, lanes]
+        state = entry(lanes)
         for n in range(SEGS):
             q = SEGS - 1 - n if backward else n
             state_ref[pl.ds(q, poles, stride=SEGS), :] = state
@@ -267,7 +267,7 @@
                 for k in range(poles)
             )
 
-        lax.fori_loop(0, chunks, body, carried)
+        lax.fori_loop(0, chunks, body, carried, unroll=2)
 
         def gate(q, _):
             whole = total_ref[pl.ds(pl.multiple_of(q * pitch, 8), seg_len), :]
@@ -303,7 +303,7 @@
     if settled:
         out_a, out_b, state_ref, total_ref = rest
     else:
-        done_a, done_b, *outs, out_a, out_b, state_ref, total_ref, done_sems, out_sems = rest
+        shift_ref, other_ref, done_a, done_b, *outs, out_a, out_b, state_ref, total_ref, done_sems, out_sems = rest
     later = lax.axis_index("ctx") >= blocks // 2
 
     def run(backward):
@@ -325,6 +325,11 @@
                 )
                 copy.start()
                 copies.append(copy)
+
+        def entry(lanes):
+            if settled:
+                return entry_ref[:, lanes]
+            return entry_ref[:, lanes] + shift_ref[:, lanes] * other_ref[:, lanes]
 
         if backward:
             gates = (values_ref, inner_ref)
@@ -338,7 +343,7 @@
             gates,
             *parts,
             table_ref,
-            entry_ref,
+            entry,
             (out_a, out_b),
             state_ref,
             total_ref,
@@ -432,9 +437,10 @@
 
     ahead, back = own[:poles], own[poles:]
     ahead_entry, back_entry = entry[:poles], entry[poles:]
-    sent, settled_entry, open_entry = lax.optimization_barrier(
+    sent, shift, settled_entry, open_entry = lax.optimization_barrier(
         (
             choose(back, ahead),
+            shift,
             choose(back_entry, ahead_entry),
             choose(ahead_entry, back_entry),
         )
@@ -461,7 +467,7 @@
 
     ready = finish(True, settled_entry, ())
     other, ready = lax.optimization_barrier((other, ready))
-    return finish(False, open_entry + shift * other, ready)
+    return finish(False, open_entry, (shift, other, *ready))
 
 
 def solution(mesh):

time: 20.4 us -> 20.4 us (level)
  no operation moved by 1% of the time
where the time goes in v8:
time: 20.4 us; the launch traced here: 20.2 us
  Pallas kernels  9.21 us (45%)
  starting transfers between devices  7.91 us (39%)
  waiting for transfers between devices  2.36 us (12%)
  between operations  0.69 us (3%)
    ppermute x3, starting transfers between devices, shards(): other = lax.ppermute(own, 'ctx', partners(bit))  5.08 us
    pallas_call x2, Pallas kernels, finish(): pl.pallas_call(functools.partial(finish_kernel, seg_len, blocks, settled)...  3.79 us
    pallas_call x1, Pallas kernels, shards(): pl.pallas_call(functools.partial(state_kernel, seg_len, blocks), out_shap...  3.73 us
    ppermute x1, starting transfers between devices, shards(): other = lax.ppermute(sent, 'ctx', partners(levels - 1))  2.82 us
    ppermute x3, waiting for transfers between devices, shards(): other = lax.ppermute(own, 'ctx', partners(bit))  2.36 us
    pallas_call x2, Pallas kernels, local(): pl.pallas_call(functools.partial(local_kernel, seg_len, blocks, backward)...  1.69 us
  transfers between devices with their start and end apart: 4, of which 3 were waited for; matrix products, arithmetic and copies ran while one was open for 0% of the time, Pallas kernels for 16%

profile of v8, /device:TPU:0, one launch (start us, length us, event | category | flops | bytes accessed | tf_op | source)
XLA Modules:
  0.0 20.2 jit_solution(2721896294788219607)
XLA Ops:
  0.6 0.0 copy-start
  0.6 3.7 %states.1 = (f32[2,1088,128]{2,1,0:T(8,128)S(1)}, f32[2,1088,128]{2,1,0:T(8,128)S(1)}, f32[2,1024,128]{2,1,0:T(8,128)S(1)}, f32[2,1024,128]{2,1,0:T(8,128)S(1)},...) custom-call(bf16[1024,256]{1,0:T(8,128)(2,1)} %outer_hbm.1, ...), custom_call_target="tpu_custom_call" | custom-call | tf_op jit(solution)/shard_map/states/pallas_call | solution.py:376
  4.4 0.5 %collective-permute-start = (f32[32,256]{1,0:T(8,128)S(1)}, f32[32,256]{1,0:T(8,128)S(1)}, u32[]{:S(2)}, u32[]{:S(2)}) collective-permute-start(f32[32,256]{1,0:T(8,128)S(1)} %get-tuple-element.44), channel_id=1, source_target_pairs={{0,1},{1,0},{2,3},{3,2},{4,5},{5,4},{6,7},{7,6},{8,9},{9,8},{10,11... | collective-permute-start | bytes 98312 | tf_op jit(solution)/shard_map/ppermute | solution.py:417
  4.9 0.9 %collective-permute-done = f32[32,256]{1,0:T(8,128)S(1)} collective-permute-done((f32[32,256]{1,0:T(8,128)S(1)}, f32[32,256]{1,0:T(8,128)S(1)}, u32[]{:S(2)}, u32[]{:S(2)}) %collective-permute-start) | collective-permute-done | bytes 32800 | tf_op jit(solution)/shard_map/ppermute | solution.py:417
  5.8 2.7 %collective-permute-start.1 = (f32[32,256]{1,0:T(8,128)S(1)}, f32[32,256]{1,0:T(8,128)S(1)}, u32[]{:S(2)}, u32[]{:S(2)}) collective-permute-start(f32[32,256]{1,0:T(8,128)S(1)} %get-tuple-element.45), channel_id=1, source_target_pairs={{0,3},{1,2},{2,1},{3,0},{4,7},{5,6},{6,5},{7,4},{8,11},{9,10},{10,... | collective-permute-start | bytes 98312 | tf_op jit(solution)/shard_map/ppermute | solution.py:417
  8.4 0.0 copy-done
  8.4 0.9 %local.2 = (f32[2,1088,128]{2,1,0:T(8,128)S(1)}, f32[224,256]{1,0:T(8,128)S(1)}) custom-call(f32[2,1088,128]{2,1,0:T(8,128)S(1)} %get-tuple-element.46.signal_ref, f32[32,256]{1,0:T(8,128)S(1)} %get-tuple-element.47.table_ref, f32[1,256]{1,0:T(1,128)S(1)} %bitcast.3), custom_call_target="tpu_custom_call", output_to_operand_aliasing={{0}: (0, {})} | custom-call | flops 4456448 | bytes 2228224 | tf_op jit(solution)/shard_map/local/pallas_call | solution.py:397
  9.3 0.7 %collective-permute-done.1 = f32[32,256]{1,0:T(8,128)S(1)} collective-permute-done((f32[32,256]{1,0:T(8,128)S(1)}, f32[32,256]{1,0:T(8,128)S(1)}, u32[]{:S(2)}, u32[]{:S(2)}) %collective-permute-start.1) | collective-permute-done | bytes 32800 | tf_op jit(solution)/shard_map/ppermute | solution.py:417
  10.1 1.9 %collective-permute-start.2 = (f32[32,256]{1,0:T(8,128)S(1)}, f32[32,256]{1,0:T(8,128)S(1)}, u32[]{:S(2)}, u32[]{:S(2)}) collective-permute-start(f32[32,256]{1,0:T(8,128)S(1)} %get-tuple-element.52), channel_id=1, source_target_pairs={{0,5},{1,4},{2,7},{3,6},{4,1},{5,0},{6,3},{7,2},{8,13},{9,12},{10,... | collective-permute-start | bytes 98312 | tf_op jit(solution)/shard_map/ppermute | solution.py:417
  12.0 0.8 %local.3.back_ref = f32[2,1088,128]{2,1,0:T(8,128)S(1)} custom-call(f32[2,1088,128]{2,1,0:T(8,128)S(1)} %get-tuple-element.55.signal_ref, f32[32,256]{1,0:T(8,128)S(1)} %get-tuple-element.47.table_ref, f32[1,256]{1,0:T(1,128)S(1)} %bitcast.4), custom_call_target="tpu_custom_call", output_to_operand_aliasing={{}: (0, {})} | custom-call | flops 4456448 | bytes 2228224 | tf_op jit(solution)/shard_map/local/pallas_call | solution.py:397
  12.8 0.8 %collective-permute-done.2 = f32[32,256]{1,0:T(8,128)S(1)} collective-permute-done((f32[32,256]{1,0:T(8,128)S(1)}, f32[32,256]{1,0:T(8,128)S(1)}, u32[]{:S(2)}, u32[]{:S(2)}) %collective-permute-start.2) | collective-permute-done | bytes 32800 | tf_op jit(solution)/shard_map/ppermute | solution.py:417
  13.6 2.8 %collective-permute-start.3 = (f32[16,256]{1,0:T(8,128)S(1)}, f32[16,256]{1,0:T(8,128)S(1)}, u32[]{:S(2)}, u32[]{:S(2)}) collective-permute-start(f32[16,256]{1,0:T(8,128)S(1)} %get-tuple-element.65), channel_id=1, source_target_pairs={{0,9},{1,8},{2,11},{3,10},{4,13},{5,12},{6,15},{7,14},{8,1},{9,0},... | collective-permute-start | bytes 49160 | tf_op jit(solution)/shard_map/ppermute | solution.py:448
  16.4 1.5 %settled.1 = (bf16[1024,256]{1,0:T(8,128)(2,1)S(1)}, bf16[1024,256]{1,0:T(8,128)(2,1)S(1)}) custom-call(bf16[1024,256]{1,0:T(8,128)(2,1)S(1)} %get-tuple-element.38.outer_ref, bf16[1024,256]{1,0:T(8,128)(2,1)S(1)} %get-tuple-element.39.inner_ref, bf16[1024,256]{1,0:T(8,128)(2,1)S(1)} %get-tuple-element.40.values_ref, ...), custom_call_target="tpu_custom_call" | custom-call | flops 8388608 | bytes 3145728 | tf_op jit(solution)/shard_map/settled/pallas_call | solution.py:455
  17.9 0.0 collective-permute-done.3.rest_1_
  17.9 2.3 %last.1 = (bf16[1024,256]{1,0:T(8,128)(2,1)}, bf16[1024,256]{1,0:T(8,128)(2,1)}, bf16[1024,256]{1,0:T(8,128)(2,1)}, bf16[1024,256]{1,0:T(8,128)(2,1)}) custom-call(bf16[1024,256]{1,0:T(8,128)(2,1)S(1)} %get-tuple-element.38.outer_ref, bf16[1024,256]{1,0:T(8,128)(2,1)S(1)} %get-tuple-element.39.inner_ref, bf16[1024,256]{1,0:T(8,128)(2,1)S(1)} %get-tuple-element.40.values_ref, ...), custom_call_target="tpu_custom_call" | custom-call | flops 8388608 | bytes 3145728 | tf_op jit(solution)/shard_map/last/pallas_call | solution.py:455
  (4 shorter events, 0.1 us)
Async XLA Ops:
  0.6 7.8 %copy-start = (f32[256]{0:T(256)S(1)}, f32[256]{0:T(256)}, u32[]{:S(2)}) copy-start(f32[256]{0:T(256)} %param.13) | copy-start | bytes 3076
  4.4 1.4 %collective-permute-start = (f32[32,256]{1,0:T(8,128)S(1)}, f32[32,256]{1,0:T(8,128)S(1)}, u32[]{:S(2)}, u32[]{:S(2)}) collective-permute-start(f32[32,256]{1,0:T(8,128)S(1)} %get-tuple-element.44), channel_id=1, source_target_pairs={{0,1},{1,0},{2,3},{3,2},{4,5},{5,4},{6,7},{7,6},{8,9},{9,8},{10,11... | collective-permute-start | bytes 98312 | tf_op jit(solution)/shard_map/ppermute | solution.py:417
  5.8 4.3 %collective-permute-start.1 = (f32[32,256]{1,0:T(8,128)S(1)}, f32[32,256]{1,0:T(8,128)S(1)}, u32[]{:S(2)}, u32[]{:S(2)}) collective-permute-start(f32[32,256]{1,0:T(8,128)S(1)} %get-tuple-element.45), channel_id=1, source_target_pairs={{0,3},{1,2},{2,1},{3,0},{4,7},{5,6},{6,5},{7,4},{8,11},{9,10},{10,... | collective-permute-start | bytes 98312 | tf_op jit(solution)/shard_map/ppermute | solution.py:417
  10.1 3.5 %collective-permute-start.2 = (f32[32,256]{1,0:T(8,128)S(1)}, f32[32,256]{1,0:T(8,128)S(1)}, u32[]{:S(2)}, u32[]{:S(2)}) collective-permute-start(f32[32,256]{1,0:T(8,128)S(1)} %get-tuple-element.52), channel_id=1, source_target_pairs={{0,5},{1,4},{2,7},{3,6},{4,1},{5,0},{6,3},{7,2},{8,13},{9,12},{10,... | collective-permute-start | bytes 98312 | tf_op jit(solution)/shard_map/ppermute | solution.py:417
  13.6 4.3 %collective-permute-start.3 = (f32[16,256]{1,0:T(8,128)S(1)}, f32[16,256]{1,0:T(8,128)S(1)}, u32[]{:S(2)}, u32[]{:S(2)}) collective-permute-start(f32[16,256]{1,0:T(8,128)S(1)} %get-tuple-element.65), channel_id=1, source_target_pairs={{0,9},{1,8},{2,11},{3,10},{4,13},{5,12},{6,15},{7,14},{8,1},{9,0},... | collective-permute-start | bytes 49160 | tf_op jit(solution)/shard_map/ppermute | solution.py:448

commit v9 on v8

--- a/solution.py
+++ b/solution.py
@@ -125,7 +125,7 @@
                 target_ref[h, target, :] = product
                 return _
 
-            lax.fori_loop(0, SEGS, segment, 0, unroll=4)
+            lax.fori_loop(0, SEGS, segment, 0, unroll=8)
 
         def sums(signal_ref, chunk_ref, backward):
             steps = spread_rows(decay, lanes, poles)
@@ -216,7 +216,7 @@
                 out_ref[h, pl.ds(m * CHUNK + j, SEGS, stride=pitch), :] = add_up(terms)
             return following
 
-        lax.fori_loop(0, chunks, body, fetch(0))
+        lax.fori_loop(0, chunks, body, fetch(0), unroll=2)
 
 
 def finish_way(

time: 20.4 us -> 20.4 us (level)
  transfers between devices with their start and end apart: 4 -> 4, of which waited for: 3 -> 3; matrix products, arithmetic and copies ran while one was open for 0% -> 0% of each run, Pallas kernels for 16% -> 15%
where the time goes in v9:
time: 20.4 us; the launch traced here: 20.2 us
  Pallas kernels  9.09 us (45%)
  starting transfers between devices  7.91 us (39%)
  waiting for transfers between devices  2.46 us (12%)
  between operations  0.69 us (3%)
    ppermute x3, starting transfers between devices, shards(): other = lax.ppermute(own, 'ctx', partners(bit))  5.08 us
    pallas_call x2, Pallas kernels, finish(): pl.pallas_call(functools.partial(finish_kernel, seg_len, blocks, settled)...  3.79 us
    pallas_call x1, Pallas kernels, shards(): pl.pallas_call(functools.partial(state_kernel, seg_len, blocks), out_shap...  3.72 us
    ppermute x1, starting transfers between devices, shards(): other = lax.ppermute(sent, 'ctx', partners(levels - 1))  2.82 us
    ppermute x3, waiting for transfers between devices, shards(): other = lax.ppermute(own, 'ctx', partners(bit))  2.46 us
    pallas_call x2, Pallas kernels, local(): pl.pallas_call(functools.partial(local_kernel, seg_len, blocks, backward)...  1.58 us
  transfers between devices with their start and end apart: 4, of which 3 were waited for; matrix products, arithmetic and copies ran while one was open for 0% of the time, Pallas kernels for 15%

profile of v9, /device:TPU:0, one launch (start us, length us, event | category | flops | bytes accessed | tf_op | source)
XLA Modules:
  0.0 20.2 jit_solution(3925802491069540499)
XLA Ops:
  0.6 0.0 copy-start
  0.6 3.7 %states.1 = (f32[2,1088,128]{2,1,0:T(8,128)S(1)}, f32[2,1088,128]{2,1,0:T(8,128)S(1)}, f32[2,1024,128]{2,1,0:T(8,128)S(1)}, f32[2,1024,128]{2,1,0:T(8,128)S(1)},...) custom-call(bf16[1024,256]{1,0:T(8,128)(2,1)} %outer_hbm.1, ...), custom_call_target="tpu_custom_call" | custom-call | tf_op jit(solution)/shard_map/states/pallas_call | solution.py:376
  4.4 0.5 %collective-permute-start = (f32[32,256]{1,0:T(8,128)S(1)}, f32[32,256]{1,0:T(8,128)S(1)}, u32[]{:S(2)}, u32[]{:S(2)}) collective-permute-start(f32[32,256]{1,0:T(8,128)S(1)} %get-tuple-element.44), channel_id=1, source_target_pairs={{0,1},{1,0},{2,3},{3,2},{4,5},{5,4},{6,7},{7,6},{8,9},{9,8},{10,11... | collective-permute-start | bytes 98312 | tf_op jit(solution)/shard_map/ppermute | solution.py:417
  4.9 0.9 %collective-permute-done = f32[32,256]{1,0:T(8,128)S(1)} collective-permute-done((f32[32,256]{1,0:T(8,128)S(1)}, f32[32,256]{1,0:T(8,128)S(1)}, u32[]{:S(2)}, u32[]{:S(2)}) %collective-permute-start) | collective-permute-done | bytes 32800 | tf_op jit(solution)/shard_map/ppermute | solution.py:417
  5.8 2.7 %collective-permute-start.1 = (f32[32,256]{1,0:T(8,128)S(1)}, f32[32,256]{1,0:T(8,128)S(1)}, u32[]{:S(2)}, u32[]{:S(2)}) collective-permute-start(f32[32,256]{1,0:T(8,128)S(1)} %get-tuple-element.45), channel_id=1, source_target_pairs={{0,3},{1,2},{2,1},{3,0},{4,7},{5,6},{6,5},{7,4},{8,11},{9,10},{10,... | collective-permute-start | bytes 98312 | tf_op jit(solution)/shard_map/ppermute | solution.py:417
  8.4 0.0 copy-done
  8.4 0.8 %local.2 = (f32[2,1088,128]{2,1,0:T(8,128)S(1)}, f32[224,256]{1,0:T(8,128)S(1)}) custom-call(f32[2,1088,128]{2,1,0:T(8,128)S(1)} %get-tuple-element.46.signal_ref, f32[32,256]{1,0:T(8,128)S(1)} %get-tuple-element.47.table_ref, f32[1,256]{1,0:T(1,128)S(1)} %bitcast.3), custom_call_target="tpu_custom_call", output_to_operand_aliasing={{0}: (0, {})} | custom-call | flops 4456448 | bytes 2228224 | tf_op jit(solution)/shard_map/local/pallas_call | solution.py:397
  9.3 0.8 %collective-permute-done.1 = f32[32,256]{1,0:T(8,128)S(1)} collective-permute-done((f32[32,256]{1,0:T(8,128)S(1)}, f32[32,256]{1,0:T(8,128)S(1)}, u32[]{:S(2)}, u32[]{:S(2)}) %collective-permute-start.1) | collective-permute-done | bytes 32800 | tf_op jit(solution)/shard_map/ppermute | solution.py:417
  10.0 1.9 %collective-permute-start.2 = (f32[32,256]{1,0:T(8,128)S(1)}, f32[32,256]{1,0:T(8,128)S(1)}, u32[]{:S(2)}, u32[]{:S(2)}) collective-permute-start(f32[32,256]{1,0:T(8,128)S(1)} %get-tuple-element.52), channel_id=1, source_target_pairs={{0,5},{1,4},{2,7},{3,6},{4,1},{5,0},{6,3},{7,2},{8,13},{9,12},{10,... | collective-permute-start | bytes 98312 | tf_op jit(solution)/shard_map/ppermute | solution.py:417
  11.9 0.8 %local.3.back_ref = f32[2,1088,128]{2,1,0:T(8,128)S(1)} custom-call(f32[2,1088,128]{2,1,0:T(8,128)S(1)} %get-tuple-element.55.signal_ref, f32[32,256]{1,0:T(8,128)S(1)} %get-tuple-element.47.table_ref, f32[1,256]{1,0:T(1,128)S(1)} %bitcast.4), custom_call_target="tpu_custom_call", output_to_operand_aliasing={{}: (0, {})} | custom-call | flops 4456448 | bytes 2228224 | tf_op jit(solution)/shard_map/local/pallas_call | solution.py:397
  12.7 0.8 %collective-permute-done.2 = f32[32,256]{1,0:T(8,128)S(1)} collective-permute-done((f32[32,256]{1,0:T(8,128)S(1)}, f32[32,256]{1,0:T(8,128)S(1)}, u32[]{:S(2)}, u32[]{:S(2)}) %collective-permute-start.2) | collective-permute-done | bytes 32800 | tf_op jit(solution)/shard_map/ppermute | solution.py:417
  13.6 2.8 %collective-permute-start.3 = (f32[16,256]{1,0:T(8,128)S(1)}, f32[16,256]{1,0:T(8,128)S(1)}, u32[]{:S(2)}, u32[]{:S(2)}) collective-permute-start(f32[16,256]{1,0:T(8,128)S(1)} %get-tuple-element.65), channel_id=1, source_target_pairs={{0,9},{1,8},{2,11},{3,10},{4,13},{5,12},{6,15},{7,14},{8,1},{9,0},... | collective-permute-start | bytes 49160 | tf_op jit(solution)/shard_map/ppermute | solution.py:448
  16.4 1.5 %settled.1 = (bf16[1024,256]{1,0:T(8,128)(2,1)S(1)}, bf16[1024,256]{1,0:T(8,128)(2,1)S(1)}) custom-call(bf16[1024,256]{1,0:T(8,128)(2,1)S(1)} %get-tuple-element.38.outer_ref, bf16[1024,256]{1,0:T(8,128)(2,1)S(1)} %get-tuple-element.39.inner_ref, bf16[1024,256]{1,0:T(8,128)(2,1)S(1)} %get-tuple-element.40.values_ref, ...), custom_call_target="tpu_custom_call" | custom-call | flops 8388608 | bytes 3145728 | tf_op jit(solution)/shard_map/settled/pallas_call | solution.py:455
  17.9 0.0 collective-permute-done.3.rest_1_
  17.9 2.3 %last.1 = (bf16[1024,256]{1,0:T(8,128)(2,1)}, bf16[1024,256]{1,0:T(8,128)(2,1)}, bf16[1024,256]{1,0:T(8,128)(2,1)}, bf16[1024,256]{1,0:T(8,128)(2,1)}) custom-call(bf16[1024,256]{1,0:T(8,128)(2,1)S(1)} %get-tuple-element.38.outer_ref, bf16[1024,256]{1,0:T(8,128)(2,1)S(1)} %get-tuple-element.39.inner_ref, bf16[1024,256]{1,0:T(8,128)(2,1)S(1)} %get-tuple-element.40.values_ref, ...), custom_call_target="tpu_custom_call" | custom-call | flops 8388608 | bytes 3145728 | tf_op jit(solution)/shard_map/last/pallas_call | solution.py:455
  (4 shorter events, 0.1 us)
Async XLA Ops:
  0.6 7.8 %copy-start = (f32[256]{0:T(256)S(1)}, f32[256]{0:T(256)}, u32[]{:S(2)}) copy-start(f32[256]{0:T(256)} %param.13) | copy-start | bytes 3076
  4.4 1.4 %collective-permute-start = (f32[32,256]{1,0:T(8,128)S(1)}, f32[32,256]{1,0:T(8,128)S(1)}, u32[]{:S(2)}, u32[]{:S(2)}) collective-permute-start(f32[32,256]{1,0:T(8,128)S(1)} %get-tuple-element.44), channel_id=1, source_target_pairs={{0,1},{1,0},{2,3},{3,2},{4,5},{5,4},{6,7},{7,6},{8,9},{9,8},{10,11... | collective-permute-start | bytes 98312 | tf_op jit(solution)/shard_map/ppermute | solution.py:417
  5.8 4.3 %collective-permute-start.1 = (f32[32,256]{1,0:T(8,128)S(1)}, f32[32,256]{1,0:T(8,128)S(1)}, u32[]{:S(2)}, u32[]{:S(2)}) collective-permute-start(f32[32,256]{1,0:T(8,128)S(1)} %get-tuple-element.45), channel_id=1, source_target_pairs={{0,3},{1,2},{2,1},{3,0},{4,7},{5,6},{6,5},{7,4},{8,11},{9,10},{10,... | collective-permute-start | bytes 98312 | tf_op jit(solution)/shard_map/ppermute | solution.py:417
  10.0 3.5 %collective-permute-start.2 = (f32[32,256]{1,0:T(8,128)S(1)}, f32[32,256]{1,0:T(8,128)S(1)}, u32[]{:S(2)}, u32[]{:S(2)}) collective-permute-start(f32[32,256]{1,0:T(8,128)S(1)} %get-tuple-element.52), channel_id=1, source_target_pairs={{0,5},{1,4},{2,7},{3,6},{4,1},{5,0},{6,3},{7,2},{8,13},{9,12},{10,... | collective-permute-start | bytes 98312 | tf_op jit(solution)/shard_map/ppermute | solution.py:417
  13.6 4.3 %collective-permute-start.3 = (f32[16,256]{1,0:T(8,128)S(1)}, f32[16,256]{1,0:T(8,128)S(1)}, u32[]{:S(2)}, u32[]{:S(2)}) collective-permute-start(f32[16,256]{1,0:T(8,128)S(1)} %get-tuple-element.65), channel_id=1, source_target_pairs={{0,9},{1,8},{2,11},{3,10},{4,13},{5,12},{6,15},{7,14},{8,1},{9,0},... | collective-permute-start | bytes 49160 | tf_op jit(solution)/shard_map/ppermute | solution.py:448
